TPU v7x, 256 devices: a whole 4x4x8 slice. The times are simulated.
256 devices in a mesh: seq: 64 (over y, z, core), mp: 4 (over x).
Axes of the slice: x: 4, y: 4, z: 8, core: 2. Of those that a mesh axis runs over, the one named last changes fastest.
Arguments:
- byte_acts: bfloat16 [32768, 2048], P('seq', 'mp'), may hold values from -20 to 20
- byte_grads: bfloat16 [32768, 2048], P('seq', 'mp'), may hold values from -6 to 6
- row_of_byte: int32 [32768], P('seq'), may hold values from 0 to 14239, as said below
- w_in: bfloat16 [2048, 4096], P('seq', 'mp'), may hold values from -0.125 to 0.125
- w_out: bfloat16 [2048, 4096], P('seq', 'mp'), may hold values from -0.09375 to 0.09375
Outputs:
- byte_act_grad: bfloat16 [32768, 2048], P('seq', 'mp')
- grad_in: float32 [2048, 4096], P('seq', 'mp')
- grad_out: float32 [2048, 4096], P('seq', 'mp')
Inputs may be any that keep to these rules, and one draw needn't show every extreme that they name: `row_of_byte`: equal values form runs of bytes, the segments, and values never fall along the sequence; the first byte begins a segment. With shards of 512 bytes, the j-th segment that begins in shard k has the value k * 224 + j, and between 32 and 224 segments begin in each shard, 224 in some shard and 128 in the last one. The segments that begin in shards 0 to k - 1 number k * 128 plus 0 to 3 * 128 // 4 (both ends are reached), and 8192 in all.
All inputs are finite; a program needn't handle non-finite values.
Results may differ from a plain program's by a relative error of at most 0.0075.
Values may be sent and summed in bfloat16 or wider, within the bound.
No kernel may reach another device: no remote copies, remote signals or barrier semaphores. Data moves between devices by JAX's collectives and lax.ppermute only.
A program may use at most 64 MiB of HBM per device.

v0:
```python
import math

import jax
import jax.numpy as jnp
from jax import lax
from jax.experimental import pallas as pl
from jax.experimental.pallas import tpu as pltpu
from jax.sharding import PartitionSpec as P

BAL = 128
CAP = 224
NY, NZ, NC, NX = 4, 8, 2, 4
SEQ = NY * NZ * NC
epsilon = 1e-05
bf16 = jnp.bfloat16
f32 = jnp.float32


def seq_of(y, z, c):
    return ((y % NY) * NZ + (z % NZ)) * NC + c


def coords_of(s):
    return s // (NZ * NC), (s // NC) % NZ, s % NC


CORE_SWAP = [(s, s ^ 1) for s in range(SEQ)]
ZC_GROUPS = [[seq_of(y, z, c) for z in range(NZ) for c in range(NC)] for y in range(NY)]


def y_pairs(step):
    pairs = []
    for s in range(SEQ):
        y, z, c = coords_of(s)
        pairs.append((s, seq_of(y + step, z, c)))
    return pairs


def swap_cores(value):
    return lax.ppermute(value, "seq", CORE_SWAP)


def send_y(value, step):
    return lax.ppermute(value, "seq", y_pairs(step))


def send_x(value, step):
    return lax.ppermute(value, "mp", [(i, (i + step) % NX) for i in range(NX)])


def exchange(value, groups):
    return lax.all_to_all(value, "seq", 0, 0, axis_index_groups=groups, tiled=True)


def pick(value, index):
    return lax.dynamic_index_in_dim(value, index, 0, keepdims=False)


def gelu_tanh(values):
    return jax.nn.gelu(values, approximate=True)


def gather_by_y(column):
    return [column] + [send_y(column, step) for step in (1, 3, 2)]


def start_and_wait(pairs, sems):
    copies = [
        pltpu.make_async_copy(source, target, sems.at[n])
        for n, (source, target) in enumerate(pairs)
    ]
    for item in copies:
        item.start()
    for item in copies:
        item.wait()


STEPS = (0, 1, 3, 2)


def weight_kernel(at_ref, *refs):
    parts, (full_ref, sems) = refs[:4], refs[4:]
    pairs = [
        (part, full_ref.at[lax.rem(at_ref[1] + NY - step, NY)])
        for part, step in zip(parts, STEPS)
    ]
    start_and_wait(pairs, sems)


def rows_kernel(at_ref, own_ref, other_ref, pooled_ref, up_ref, sems):
    rows, quarter = own_ref.shape[2:]
    pairs = []
    for half, part in enumerate((own_ref, other_ref)):
        for n, step in enumerate(STEPS):
            x = lax.rem(at_ref[0] + NX - step, NX)
            where = (
                pl.ds(half * rows, rows),
                pl.ds(pl.multiple_of(x * quarter, quarter), quarter),
            )
            pairs.append((part.at[n, 0], pooled_ref.at[where]))
            pairs.append((part.at[n, 1], up_ref.at[where]))
    start_and_wait(pairs, sems)


def place(kernel, at, parts, shapes, n_copies):
    moved = sum(2 * math.prod(shape) for shape in shapes)
    return pl.pallas_call(
        kernel,
        out_shape=tuple(jax.ShapeDtypeStruct(shape, bf16) for shape in shapes),
        in_specs=[pl.BlockSpec(memory_space=pltpu.SMEM)]
        + [pl.BlockSpec(memory_space=pl.ANY)] * len(parts),
        out_specs=(pl.BlockSpec(memory_space=pltpu.VMEM),) * len(shapes),
        scratch_shapes=[pltpu.SemaphoreType.DMA((n_copies,))],
        cost_estimate=pl.CostEstimate(flops=0, bytes_accessed=2 * moved, transcendentals=0),
    )(at, *parts)


def place_weight(at, parts):
    depth, hidden = parts[0].shape
    (full,) = place(weight_kernel, at, parts, [(NY, depth, hidden)], 4)
    return full.reshape(NY * depth, hidden)


def place_rows(at, own_parts, other_parts):
    rows, quarter = own_parts.shape[2:]
    wide = (2 * rows, NX * quarter)
    return place(rows_kernel, at, [own_parts, other_parts], [wide, wide], 16)


def reduce_by_y(pieces, y_idx):
    total = pick(pieces, y_idx).astype(f32)
    for step in (1, 3, 2):
        got = send_y(pick(pieces, (y_idx + step) % NY).astype(bf16), step)
        total = total + got.astype(f32)
    return total


def local(byte_acts, byte_grads, row_of_byte, w_in, w_out):
    quarter = byte_acts.shape[1]
    width = quarter * NX
    hidden = w_in.shape[1] // NC
    shard_idx = lax.axis_index("seq")
    x_idx = lax.axis_index("mp")
    y_idx = shard_idx // (NZ * NC)

    def spread(weight):
        halves = weight.reshape(1, 32, NC, hidden).swapaxes(1, 2)
        copies = jnp.broadcast_to(halves, (NZ, NC, 32, hidden)).reshape(NZ * NC, 32, hidden)
        return exchange(copies, ZC_GROUPS).reshape(NZ * NC * 32, hidden)

    in_column = spread(w_in)
    in_parts = gather_by_y(in_column)
    out_column = spread(w_out)
    out_parts = gather_by_y(out_column)

    local_row = row_of_byte - shard_idx * CAP
    leading = local_row < 0
    slot_idx = jnp.where(leading, CAP, local_row)
    one_hot = (jnp.arange(CAP + 1, dtype=jnp.int32)[:, None] == slot_idx[None, :]).astype(bf16)
    act_sums = jnp.dot(one_hot, byte_acts, preferred_element_type=f32)
    grad_sums = jnp.dot(one_hot, byte_grads, preferred_element_type=f32)
    byte_counts = jnp.sum(one_hot.astype(f32), axis=1)
    own_count = jnp.max(jnp.where(leading, -1, local_row)) + 1
    frag = jnp.stack(
        [act_sums[CAP], grad_sums[CAP], jnp.broadcast_to(byte_counts[CAP], (quarter,))]
    )
    frag = lax.ppermute(frag, "seq", [(s, s - 1) for s in range(1, SEQ)])
    last_mark = (jnp.arange(CAP, dtype=jnp.int32) == own_count - 1).astype(f32)
    act_total = act_sums[:CAP] + last_mark[:, None] * frag[0][None, :]
    grad_total = grad_sums[:CAP] + last_mark[:, None] * frag[1][None, :]
    row_lengths = byte_counts[:CAP] + last_mark * frag[2, 0]
    inv_length = 1.0 / jnp.maximum(row_lengths, 1.0)
    pooled = (act_total * inv_length[:, None]).astype(bf16)
    up_grad = grad_total.astype(bf16)

    rows = jnp.stack([pooled, up_grad])
    own_parts = [rows] + [send_x(rows, step) for step in (1, 3, 2)]
    own_parts = jnp.stack(own_parts)
    other_parts = swap_cores(own_parts)
    at = jnp.stack([x_idx, y_idx]).astype(jnp.int32)
    wide_pooled, wide_up = place_rows(at, own_parts, other_parts)
    full_w_in = place_weight(at, in_parts)
    full_w_out = place_weight(at, out_parts)

    wide_f32 = wide_pooled.astype(f32)
    inv_rms = lax.rsqrt(jnp.mean(wide_f32 * wide_f32, axis=1) + epsilon)
    normed = (wide_f32 * inv_rms[:, None]).astype(bf16)
    pre_act = jnp.dot(normed, full_w_in, preferred_element_type=f32)
    activation = gelu_tanh(pre_act).astype(bf16)
    out_part = lax.dot_general(
        wide_up, activation, (((0,), (0,)), ((), ())), preferred_element_type=f32
    )
    out_pieces = out_part.astype(bf16).reshape(NY, NZ * NC, 32, hidden).swapaxes(0, 1)
    out_rows = exchange(out_pieces.reshape(NZ * NC, NY * 32, hidden), ZC_GROUPS)
    out_rows = jnp.sum(out_rows.astype(f32).reshape(NZ, NC, NY, 32, hidden), axis=0)
    grad_out = reduce_by_y(out_rows.swapaxes(0, 1), y_idx)
    up_proj = jnp.dot(wide_up, full_w_out, preferred_element_type=f32)
    act_grad = jax.vjp(gelu_tanh, pre_act)[1](up_proj)[0].astype(bf16)
    stat_part = jnp.sum(act_grad.astype(f32) * pre_act, axis=1) / inv_rms
    in_part = lax.dot_general(
        normed, act_grad, (((0,), (0,)), ((), ())), preferred_element_type=f32
    ).astype(bf16)
    in_rows = reduce_by_y(in_part.reshape(NY, NZ * NC * 32, hidden), y_idx)
    in_rows = exchange(in_rows.astype(bf16).reshape(NZ * NC, 32, hidden), ZC_GROUPS)
    grad_in = jnp.sum(in_rows.astype(f32).reshape(NZ, NC, 32, hidden), axis=0)

    normed_part = lax.dot_general(
        act_grad, full_w_in, (((1,), (1,)), ((), ())), preferred_element_type=f32
    )
    stat_high = stat_part.astype(bf16)
    stat_low = (stat_part - stat_high.astype(f32)).astype(bf16)
    lane = jnp.arange(128)[None, :]
    stat_cols = jnp.where(lane == 0, stat_high[:, None], stat_low[:, None])
    stat_cols = jnp.where(lane < 2, stat_cols, jnp.zeros((), bf16))
    sent = jnp.concatenate([normed_part[CAP:].astype(bf16), stat_cols[CAP:]], axis=1)
    got = swap_cores(sent)
    got = got.astype(f32)
    chip_part = normed_part[:CAP] + got[:, :width]
    chip_stat = stat_part[:CAP] + got[:, width] + got[:, width + 1]
    stat_high = chip_stat.astype(bf16)
    stat_low = (chip_stat - stat_high.astype(f32)).astype(bf16)
    stat_cols = jnp.where(lane == 0, stat_high[:, None], stat_low[:, None])
    stat_cols = jnp.where(lane < 2, stat_cols, jnp.zeros((), bf16))
    normed_grad = lax.dynamic_slice_in_dim(chip_part, x_idx * quarter, quarter, 1)
    row_stat = chip_stat
    for step in (1, 3, 2):
        piece = lax.dynamic_slice_in_dim(
            chip_part, ((x_idx + step) % NX) * quarter, quarter, 1
        ).astype(bf16)
        piece = jnp.concatenate([piece, stat_cols], axis=1)
        got = send_x(piece, step)
        got = got.astype(f32)
        normed_grad = normed_grad + got[:, :quarter]
        row_stat = row_stat + got[:, quarter] + got[:, quarter + 1]
    row_stat = row_stat / width
    own_rms = inv_rms[:CAP]
    pooled_grad = (
        up_grad.astype(f32)
        + own_rms[:, None] * normed_grad
        - pooled.astype(f32) * (own_rms**3 * row_stat)[:, None]
    ).astype(bf16)

    grad_spread = pooled_grad.astype(f32) * inv_length[:, None]
    last_spread = lax.dynamic_slice_in_dim(grad_spread, own_count - 1, 1, 0)
    tail_spread = lax.ppermute(last_spread, "seq", [(s, s + 1) for s in range(SEQ - 1)])
    grad_table = jnp.concatenate([grad_spread, tail_spread], axis=0)
    byte_act_grad = (byte_grads.astype(f32) + jnp.take(grad_table, slot_idx, axis=0)).astype(bf16)

    grad_scale = 1.0 / math.sqrt(SEQ * BAL)
    grad_in = grad_in.swapaxes(0, 1).reshape(32, NC * hidden) * grad_scale
    grad_out = grad_out.swapaxes(0, 1).reshape(32, NC * hidden) * grad_scale
    return (byte_act_grad, grad_in, grad_out)


def solution(mesh):
    in_specs = (P("seq", "mp"), P("seq", "mp"), P("seq"), P("seq", "mp"), P("seq", "mp"))
    out_specs = (P("seq", "mp"), P("seq", "mp"), P("seq", "mp"))

    return jax.shard_map(local, mesh=mesh, in_specs=in_specs, out_specs=out_specs, check_vma=False)
```

profile of v0, /device:TPU:2, one launch (start us, length us, event | category | flops | bytes accessed | tf_op | source)
XLA Modules:
  0.0 244.4 jit_solution(11053244022995088001)
XLA Ops:
  7.4 9.3 %all-to-all-start.1 = ((bf16[16,32,512]{2,1,0:T(8,128)(2,1)}), bf16[16,32,512]{2,1,0:T(8,128)(2,1)S(1)}, u32[]{:S(2)}, u32[]{:S(2)}) async-start(bf16[16,32,512]{2,1,0:T(8,128)(2,1)} %bitcast.19), calls=%async_computation.1 | async-start | bytes 1048576 | tf_op jit(solution)/shard_map/all_to_all | solution.py:52
  25.4 8.1 %collective-permute-done.2 = bf16[2,224,512]{2,1,0:T(8,128)(2,1)S(1)} collective-permute-done((bf16[2,224,512]{2,1,0:T(8,128)(2,1)S(1)}, bf16[2,224,512]{2,1,0:T(8,128)(2,1)S(1)}, u32[]{:S(2)}, u32[]{:S(2)}) %collective-permute-start.2) | collective-permute-done | bytes 458784 | tf_op jit(solution)/shard_map/ppermute | solution.py:48
  33.5 10.8 %collective-permute-done.3 = bf16[2,224,512]{2,1,0:T(8,128)(2,1)S(1)} collective-permute-done((bf16[2,224,512]{2,1,0:T(8,128)(2,1)S(1)}, bf16[2,224,512]{2,1,0:T(8,128)(2,1)S(1)}, u32[]{:S(2)}, u32[]{:S(2)}) %collective-permute-start.3) | collective-permute-done | bytes 458784 | tf_op jit(solution)/shard_map/ppermute | solution.py:48
  47.6 7.0 %all-to-all-start = ((bf16[16,32,512]{2,1,0:T(8,128)(2,1)}), bf16[16,32,512]{2,1,0:T(8,128)(2,1)S(1)}, u32[]{:S(2)}, u32[]{:S(2)}) async-start(bf16[16,32,512]{2,1,0:T(8,128)(2,1)} %bitcast.14), calls=%async_computation | async-start | bytes 1048576 | tf_op jit(solution)/shard_map/all_to_all | solution.py:52
  54.7 3.3 %collective-permute-start.10 = (bf16[512,512]{1,0:T(8,128)(2,1)S(1)}, bf16[512,512]{1,0:T(8,128)(2,1)S(1)}, u32[]{:S(2)}, u32[]{:S(2)}) collective-permute-start(bf16[512,512]{1,0:T(8,128)(2,1)S(1)} %bitcast.95), channel_id=1, source_target_pairs={{0,128},{4,132},{8,136},{12,140},{16,144},{20,148},{24,152},{28,15... | collective-permute-start | bytes 1572872 | tf_op jit(solution)/shard_map/ppermute | solution.py:44
  61.2 9.4 %all-to-all-done = bf16[16,32,512]{2,1,0:T(8,128)(2,1)S(1)} async-done(((bf16[16,32,512]{2,1,0:T(8,128)(2,1)}), bf16[16,32,512]{2,1,0:T(8,128)(2,1)S(1)}, u32[]{:S(2)}, u32[]{:S(2)}) %all-to-all-start) | async-done | bytes 524320 | tf_op jit(solution)/shard_map/all_to_all | solution.py:52
  74.4 7.4 %collective-permute-done.8.refs_1_ = bf16[512,512]{1,0:T(8,128)(2,1)} collective-permute-done((bf16[512,512]{1,0:T(8,128)(2,1)S(1)}, bf16[512,512]{1,0:T(8,128)(2,1)}, u32[]{:S(2)}, u32[]{:S(2)}) %collective-permute-start.8) | collective-permute-done | bytes 524320 | tf_op jit(solution)/shard_map/ppermute | solution.py:44
  81.8 3.2 %collective-permute-start.7 = (bf16[512,512]{1,0:T(8,128)(2,1)S(1)}, bf16[512,512]{1,0:T(8,128)(2,1)}, u32[]{:S(2)}, u32[]{:S(2)}) collective-permute-start(bf16[512,512]{1,0:T(8,128)(2,1)S(1)} %bitcast.101), channel_id=1, source_target_pairs={{0,128},{4,132},{8,136},{12,140},{16,144},{20,148},{24,152},{28,15... | collective-permute-start | bytes 1572872 | tf_op jit(solution)/shard_map/ppermute | solution.py:44
  85.6 3.6 %shard_map.78 = bf16[4,512,512]{2,1,0:T(8,128)(2,1)} custom-call(s32[2]{0:T(128)} %pad_add_fusion.at_ref, bf16[512,512]{1,0:T(8,128)(2,1)} %bitcast.98, bf16[512,512]{1,0:T(8,128)(2,1)} %collective-permute-done.8.refs_1_, bf16[512,512]{1,0:T(8,128)(2,1)} %collective-permute-done.9.refs_2_, bf16[512,512]{1,0:T(8,128)(2,1)} %copy-done.12), custom_call_target="tpu_custom_call" | custom-call | bytes 4194304 | tf_op jit(solution)/shard_map/pallas_call | solution.py:107
  89.3 4.3 %collective-permute-done.5.refs_1_ = bf16[512,512]{1,0:T(8,128)(2,1)} collective-permute-done((bf16[512,512]{1,0:T(8,128)(2,1)S(1)}, bf16[512,512]{1,0:T(8,128)(2,1)}, u32[]{:S(2)}, u32[]{:S(2)}) %collective-permute-start.5) | collective-permute-done | bytes 524320 | tf_op jit(solution)/shard_map/ppermute | solution.py:44
  94.3 9.9 %collective-permute-done.7.refs_3_ = bf16[512,512]{1,0:T(8,128)(2,1)} collective-permute-done((bf16[512,512]{1,0:T(8,128)(2,1)S(1)}, bf16[512,512]{1,0:T(8,128)(2,1)}, u32[]{:S(2)}, u32[]{:S(2)}) %collective-permute-start.7) | collective-permute-done | bytes 524320 | tf_op jit(solution)/shard_map/ppermute | solution.py:44
  104.3 3.6 %shard_map.77 = bf16[4,512,512]{2,1,0:T(8,128)(2,1)} custom-call(s32[2]{0:T(128)} %pad_add_fusion.at_ref, bf16[512,512]{1,0:T(8,128)(2,1)} %bitcast.102, bf16[512,512]{1,0:T(8,128)(2,1)} %collective-permute-done.5.refs_1_, bf16[512,512]{1,0:T(8,128)(2,1)} %collective-permute-done.6.refs_2_, bf16[512,512]{1,0:T(8,128)(2,1)} %collective-permute-done.7.refs_3_), custom_call_target="tpu_custom_call" | custom-call | bytes 4194304 | tf_op jit(solution)/shard_map/pallas_call | solution.py:107
  107.9 4.9 %shard_map.76 = (bf16[448,2048]{1,0:T(8,128)(2,1)}, bf16[448,2048]{1,0:T(8,128)(2,1)}) custom-call(s32[2]{0:T(128)} %pad_add_fusion.at_ref, bf16[4,2,224,512]{3,2,1,0:T(8,128)(2,1)} %pad_maximum_fusion.own_ref, bf16[4,2,224,512]{3,2,1,0:T(8,128)(2,1)} %collective-permute-done.4.other_ref), custom_call_target="tpu_custom_call" | custom-call | bytes 7340032 | tf_op jit(solution)/shard_map/pallas_call | solution.py:107
  130.2 3.0 %fusion.54 = f32[448,2048]{1,0:T(8,128)} fusion(bf16[448,512]{1,0:T(8,128)(2,1)S(1)} %get-tuple-element.21, bf16[2048,512]{1,0:T(8,128)(2,1)S(1)} %bitcast.94), kind=kOutput, calls=%fused_computation.120 | convolution fusion | flops 939524096 | bytes 6225920 | tf_op jit(solution)/shard_map/dot_general | solution.py:207
  133.2 6.8 %collective-permute-done.16 = bf16[512,512]{1,0:T(8,128)(2,1)} collective-permute-done((bf16[512,512]{1,0:T(8,128)(2,1)}, bf16[512,512]{1,0:T(8,128)(2,1)}, u32[]{:S(2)}, u32[]{:S(2)}) %collective-permute-start.16) | collective-permute-done | bytes 524320 | tf_op jit(solution)/shard_map/ppermute | solution.py:44
  140.0 10.2 %collective-permute-done.17 = bf16[512,512]{1,0:T(8,128)(2,1)} collective-permute-done((bf16[512,512]{1,0:T(8,128)(2,1)}, bf16[512,512]{1,0:T(8,128)(2,1)}, u32[]{:S(2)}, u32[]{:S(2)}) %collective-permute-start.17) | collective-permute-done | bytes 524320 | tf_op jit(solution)/shard_map/ppermute | solution.py:44
  154.7 6.8 %all-to-all-start.2 = ((bf16[16,32,512]{2,1,0:T(8,128)(2,1)}), bf16[16,32,512]{2,1,0:T(8,128)(2,1)S(1)}, u32[]{:S(2)}, u32[]{:S(2)}) async-start(bf16[16,32,512]{2,1,0:T(8,128)(2,1)} %bitcast.27), calls=%async_computation.2 | async-start | bytes 1048576 | tf_op jit(solution)/shard_map/all_to_all | solution.py:52
  168.2 9.3 %all-to-all-done.2 = bf16[16,32,512]{2,1,0:T(8,128)(2,1)S(1)} async-done(((bf16[16,32,512]{2,1,0:T(8,128)(2,1)}), bf16[16,32,512]{2,1,0:T(8,128)(2,1)S(1)}, u32[]{:S(2)}, u32[]{:S(2)}) %all-to-all-start.2) | async-done | bytes 524320 | tf_op jit(solution)/shard_map/all_to_all | solution.py:52
  178.3 4.2 %all-to-all-start.3 = ((bf16[16,128,512]{2,1,0:T(8,128)(2,1)}), bf16[16,128,512]{2,1,0:T(8,128)(2,1)S(1)}, u32[]{:S(2)}, u32[]{:S(2)}) async-start(bf16[16,128,512]{2,1,0:T(8,128)(2,1)} %bitcast.92), calls=%async_computation.3 | async-start | bytes 4194304 | tf_op jit(solution)/shard_map/all_to_all | solution.py:52
  195.1 3.6 %collective-permute-done.12 = bf16[224,640]{1,0:T(8,128)(2,1)} collective-permute-done((bf16[224,640]{1,0:T(8,128)(2,1)}, bf16[224,640]{1,0:T(8,128)(2,1)}, u32[]{:S(2)}, u32[]{:S(2)}) %collective-permute-start.12) | collective-permute-done | bytes 286752 | tf_op jit(solution)/shard_map/ppermute | solution.py:48
  200.8 6.4 %collective-permute-done.14 = bf16[224,640]{1,0:T(8,128)(2,1)S(1)} collective-permute-done((bf16[224,640]{1,0:T(8,128)(2,1)}, bf16[224,640]{1,0:T(8,128)(2,1)S(1)}, u32[]{:S(2)}, u32[]{:S(2)}) %collective-permute-start.14) | collective-permute-done | bytes 286752 | tf_op jit(solution)/shard_map/ppermute | solution.py:48
  217.0 14.7 %all-to-all-done.3 = bf16[16,128,512]{2,1,0:T(8,128)(2,1)S(1)} async-done(((bf16[16,128,512]{2,1,0:T(8,128)(2,1)}), bf16[16,128,512]{2,1,0:T(8,128)(2,1)S(1)}, u32[]{:S(2)}, u32[]{:S(2)}) %all-to-all-start.3) | async-done | bytes 2097184 | tf_op jit(solution)/shard_map/all_to_all | solution.py:52
  232.1 5.8 %collective-permute-start.19 = (bf16[2,32,512]{2,1,0:T(8,128)(2,1)S(1)}, bf16[2,32,512]{2,1,0:T(8,128)(2,1)S(1)}, u32[]{:S(2)}, u32[]{:S(2)}) collective-permute-start(bf16[2,32,512]{2,1,0:T(8,128)(2,1)S(1)} %get-tuple-element.28), channel_id=1, source_target_pairs={{0,64},{4,68},{8,72},{12,76},{16,80},{20,84},{24,88},{28,92},{32,9... | collective-permute-start | bytes 196616 | tf_op jit(solution)/shard_map/ppermute | solution.py:44
  237.9 3.2 %collective-permute-start.21 = (bf16[2,32,512]{2,1,0:T(8,128)(2,1)S(1)}, bf16[2,32,512]{2,1,0:T(8,128)(2,1)S(1)}, u32[]{:S(2)}, u32[]{:S(2)}) collective-permute-start(bf16[2,32,512]{2,1,0:T(8,128)(2,1)S(1)} %get-tuple-element.30), channel_id=1, source_target_pairs={{0,128},{4,132},{8,136},{12,140},{16,144},{20,148},{24,152},{28,15... | collective-permute-start | bytes 196616 | tf_op jit(solution)/shard_map/ppermute | solution.py:44
  (176 shorter events, 82.2 us)
Async XLA Ops:
  5.2 12.8 %collective-permute-start = (f32[3,512]{1,0:T(4,128)S(1)}, f32[3,512]{1,0:T(4,128)S(1)}, u32[]{:S(2)}, u32[]{:S(2)}) collective-permute-start(f32[3,512]{1,0:T(4,128)S(1)} %maximum_maximum_fusion), channel_id=1, source_target_pairs={{4,0},{8,4},{12,8},{16,12},{20,16},{24,20},{28,24},{32,28},{36,32}... | collective-permute-start | bytes 18440 | tf_op jit(solution)/shard_map/ppermute | solution.py:167
  7.4 39.3 %all-to-all-start.1 = ((bf16[16,32,512]{2,1,0:T(8,128)(2,1)}), bf16[16,32,512]{2,1,0:T(8,128)(2,1)S(1)}, u32[]{:S(2)}, u32[]{:S(2)}) async-start(bf16[16,32,512]{2,1,0:T(8,128)(2,1)} %bitcast.19), calls=%async_computation.1 | async-start | bytes 1048576 | tf_op jit(solution)/shard_map/all_to_all | solution.py:52
  20.6 12.9 %collective-permute-start.2 = (bf16[2,224,512]{2,1,0:T(8,128)(2,1)S(1)}, bf16[2,224,512]{2,1,0:T(8,128)(2,1)S(1)}, u32[]{:S(2)}, u32[]{:S(2)}) collective-permute-start(bf16[2,224,512]{2,1,0:T(8,128)(2,1)S(1)} %get-tuple-element.32), channel_id=1, source_target_pairs={{0,3},{1,0},{2,1},{3,2},{4,7},{5,4},{6,5},{7,6},{8,11},{9,8},{10,9... | collective-permute-start | bytes 1376264 | tf_op jit(solution)/shard_map/ppermute | solution.py:48
  21.2 23.1 %collective-permute-start.3 = (bf16[2,224,512]{2,1,0:T(8,128)(2,1)S(1)}, bf16[2,224,512]{2,1,0:T(8,128)(2,1)S(1)}, u32[]{:S(2)}, u32[]{:S(2)}) collective-permute-start(bf16[2,224,512]{2,1,0:T(8,128)(2,1)S(1)} %get-tuple-element.32), channel_id=1, source_target_pairs={{0,2},{1,3},{2,0},{3,1},{4,6},{5,7},{6,4},{7,5},{8,10},{9,11},{10,... | collective-permute-start | bytes 1376264 | tf_op jit(solution)/shard_map/ppermute | solution.py:48
  23.6 21.5 %collective-permute-start.1 = (bf16[2,224,512]{2,1,0:T(8,128)(2,1)S(1)}, bf16[2,224,512]{2,1,0:T(8,128)(2,1)S(1)}, u32[]{:S(2)}, u32[]{:S(2)}) collective-permute-start(bf16[2,224,512]{2,1,0:T(8,128)(2,1)S(1)} %get-tuple-element.32), channel_id=1, source_target_pairs={{0,1},{1,2},{2,3},{3,0},{4,5},{5,6},{6,7},{7,4},{8,9},{9,10},{10,1... | collective-permute-start | bytes 1376264 | tf_op jit(solution)/shard_map/ppermute | solution.py:48
  46.6 61.3 %collective-permute-start.4 = (bf16[4,2,224,512]{3,2,1,0:T(8,128)(2,1)}, bf16[4,2,224,512]{3,2,1,0:T(8,128)(2,1)}, u32[]{:S(2)}, u32[]{:S(2)}) collective-permute-start(bf16[4,2,224,512]{3,2,1,0:T(8,128)(2,1)} %pad_maximum_fusion.own_ref), channel_id=1, source_target_pairs={{0,4},{4,0},{8,12},{12,8},{16,20},{20,16},{24,28},{28,24},{32,36},... | collective-permute-start | bytes 5505032 | tf_op jit(solution)/shard_map/ppermute | solution.py:40
  47.6 23.0 %all-to-all-start = ((bf16[16,32,512]{2,1,0:T(8,128)(2,1)}), bf16[16,32,512]{2,1,0:T(8,128)(2,1)S(1)}, u32[]{:S(2)}, u32[]{:S(2)}) async-start(bf16[16,32,512]{2,1,0:T(8,128)(2,1)} %bitcast.14), calls=%async_computation | async-start | bytes 1048576 | tf_op jit(solution)/shard_map/all_to_all | solution.py:52
  54.7 17.5 %collective-permute-start.10 = (bf16[512,512]{1,0:T(8,128)(2,1)S(1)}, bf16[512,512]{1,0:T(8,128)(2,1)S(1)}, u32[]{:S(2)}, u32[]{:S(2)}) collective-permute-start(bf16[512,512]{1,0:T(8,128)(2,1)S(1)} %bitcast.95), channel_id=1, source_target_pairs={{0,128},{4,132},{8,136},{12,140},{16,144},{20,148},{24,152},{28,15... | collective-permute-start | bytes 1572872 | tf_op jit(solution)/shard_map/ppermute | solution.py:44
  58.0 23.9 %collective-permute-start.8 = (bf16[512,512]{1,0:T(8,128)(2,1)S(1)}, bf16[512,512]{1,0:T(8,128)(2,1)}, u32[]{:S(2)}, u32[]{:S(2)}) collective-permute-start(bf16[512,512]{1,0:T(8,128)(2,1)S(1)} %bitcast.96), channel_id=1, source_target_pairs={{0,64},{4,68},{8,72},{12,76},{16,80},{20,84},{24,88},{28,92},{32,9... | collective-permute-start | bytes 1572872 | tf_op jit(solution)/shard_map/ppermute | solution.py:44
  58.9 26.7 %collective-permute-start.9 = (bf16[512,512]{1,0:T(8,128)(2,1)S(1)}, bf16[512,512]{1,0:T(8,128)(2,1)}, u32[]{:S(2)}, u32[]{:S(2)}) collective-permute-start(bf16[512,512]{1,0:T(8,128)(2,1)S(1)} %bitcast.97), channel_id=1, source_target_pairs={{0,192},{4,196},{8,200},{12,204},{16,208},{20,212},{24,216},{28,22... | collective-permute-start | bytes 1572872 | tf_op jit(solution)/shard_map/ppermute | solution.py:44
  70.6 23.0 %collective-permute-start.5 = (bf16[512,512]{1,0:T(8,128)(2,1)S(1)}, bf16[512,512]{1,0:T(8,128)(2,1)}, u32[]{:S(2)}, u32[]{:S(2)}) collective-permute-start(bf16[512,512]{1,0:T(8,128)(2,1)S(1)} %bitcast.99), channel_id=1, source_target_pairs={{0,64},{4,68},{8,72},{12,76},{16,80},{20,84},{24,88},{28,92},{32,9... | collective-permute-start | bytes 1572872 | tf_op jit(solution)/shard_map/ppermute | solution.py:44
  72.2 22.1 %collective-permute-start.6 = (bf16[512,512]{1,0:T(8,128)(2,1)S(1)}, bf16[512,512]{1,0:T(8,128)(2,1)}, u32[]{:S(2)}, u32[]{:S(2)}) collective-permute-start(bf16[512,512]{1,0:T(8,128)(2,1)S(1)} %bitcast.100), channel_id=1, source_target_pairs={{0,192},{4,196},{8,200},{12,204},{16,208},{20,212},{24,216},{28,22... | collective-permute-start | bytes 1572872 | tf_op jit(solution)/shard_map/ppermute | solution.py:44
  81.8 22.4 %collective-permute-start.7 = (bf16[512,512]{1,0:T(8,128)(2,1)S(1)}, bf16[512,512]{1,0:T(8,128)(2,1)}, u32[]{:S(2)}, u32[]{:S(2)}) collective-permute-start(bf16[512,512]{1,0:T(8,128)(2,1)S(1)} %bitcast.101), channel_id=1, source_target_pairs={{0,128},{4,132},{8,136},{12,140},{16,144},{20,148},{24,152},{28,15... | collective-permute-start | bytes 1572872 | tf_op jit(solution)/shard_map/ppermute | solution.py:44
  124.5 15.5 %collective-permute-start.16 = (bf16[512,512]{1,0:T(8,128)(2,1)}, bf16[512,512]{1,0:T(8,128)(2,1)}, u32[]{:S(2)}, u32[]{:S(2)}) collective-permute-start(bf16[512,512]{1,0:T(8,128)(2,1)} %get-tuple-element.22), channel_id=1, source_target_pairs={{0,64},{4,68},{8,72},{12,76},{16,80},{20,84},{24,88},{28,92},{32,9... | collective-permute-start | bytes 1572872 | tf_op jit(solution)/shard_map/ppermute | solution.py:44
  126.1 24.1 %collective-permute-start.17 = (bf16[512,512]{1,0:T(8,128)(2,1)}, bf16[512,512]{1,0:T(8,128)(2,1)}, u32[]{:S(2)}, u32[]{:S(2)}) collective-permute-start(bf16[512,512]{1,0:T(8,128)(2,1)} %get-tuple-element.24), channel_id=1, source_target_pairs={{0,192},{4,196},{8,200},{12,204},{16,208},{20,212},{24,216},{28,22... | collective-permute-start | bytes 1572872 | tf_op jit(solution)/shard_map/ppermute | solution.py:44
  127.8 24.3 %collective-permute-start.18 = (bf16[512,512]{1,0:T(8,128)(2,1)}, bf16[512,512]{1,0:T(8,128)(2,1)}, u32[]{:S(2)}, u32[]{:S(2)}) collective-permute-start(bf16[512,512]{1,0:T(8,128)(2,1)} %get-tuple-element.23), channel_id=1, source_target_pairs={{0,128},{4,132},{8,136},{12,140},{16,144},{20,148},{24,152},{28,15... | collective-permute-start | bytes 1572872 | tf_op jit(solution)/shard_map/ppermute | solution.py:44
  154.7 22.8 %all-to-all-start.2 = ((bf16[16,32,512]{2,1,0:T(8,128)(2,1)}), bf16[16,32,512]{2,1,0:T(8,128)(2,1)S(1)}, u32[]{:S(2)}, u32[]{:S(2)}) async-start(bf16[16,32,512]{2,1,0:T(8,128)(2,1)} %bitcast.27), calls=%async_computation.2 | async-start | bytes 1048576 | tf_op jit(solution)/shard_map/all_to_all | solution.py:52
  164.7 17.8 %collective-permute-start.11 = (bf16[224,2176]{1,0:T(8,128)(2,1)}, bf16[224,2176]{1,0:T(8,128)(2,1)}, u32[]{:S(2)}, u32[]{:S(2)}) collective-permute-start(bf16[224,2176]{1,0:T(8,128)(2,1)} %pad_maximum_fusion.1), channel_id=1, source_target_pairs={{0,4},{4,0},{8,12},{12,8},{16,20},{20,16},{24,28},{28,24},{32,36},... | collective-permute-start | bytes 2924552 | tf_op jit(solution)/shard_map/ppermute | solution.py:40
  178.3 53.4 %all-to-all-start.3 = ((bf16[16,128,512]{2,1,0:T(8,128)(2,1)}), bf16[16,128,512]{2,1,0:T(8,128)(2,1)S(1)}, u32[]{:S(2)}, u32[]{:S(2)}) async-start(bf16[16,128,512]{2,1,0:T(8,128)(2,1)} %bitcast.92), calls=%async_computation.3 | async-start | bytes 4194304 | tf_op jit(solution)/shard_map/all_to_all | solution.py:52
  188.4 10.4 %collective-permute-start.12 = (bf16[224,640]{1,0:T(8,128)(2,1)}, bf16[224,640]{1,0:T(8,128)(2,1)}, u32[]{:S(2)}, u32[]{:S(2)}) collective-permute-start(bf16[224,640]{1,0:T(8,128)(2,1)} %get-tuple-element.33), channel_id=1, source_target_pairs={{0,1},{1,2},{2,3},{3,0},{4,5},{5,6},{6,7},{7,4},{8,9},{9,10},{10,1... | collective-permute-start | bytes 860168 | tf_op jit(solution)/shard_map/ppermute | solution.py:48
  189.9 9.9 %collective-permute-start.13 = (bf16[224,640]{1,0:T(8,128)(2,1)}, bf16[224,640]{1,0:T(8,128)(2,1)}, u32[]{:S(2)}, u32[]{:S(2)}) collective-permute-start(bf16[224,640]{1,0:T(8,128)(2,1)} %get-tuple-element.34), channel_id=1, source_target_pairs={{0,3},{1,0},{2,1},{3,2},{4,7},{5,4},{6,5},{7,6},{8,11},{9,8},{10,9... | collective-permute-start | bytes 860168 | tf_op jit(solution)/shard_map/ppermute | solution.py:48
  191.4 15.7 %collective-permute-start.14 = (bf16[224,640]{1,0:T(8,128)(2,1)}, bf16[224,640]{1,0:T(8,128)(2,1)S(1)}, u32[]{:S(2)}, u32[]{:S(2)}) collective-permute-start(bf16[224,640]{1,0:T(8,128)(2,1)} %get-tuple-element.35), channel_id=1, source_target_pairs={{0,2},{1,3},{2,0},{3,1},{4,6},{5,7},{6,4},{7,5},{8,10},{9,11},{10,... | collective-permute-start | bytes 860168 | tf_op jit(solution)/shard_map/ppermute | solution.py:48
  232.1 9.7 %collective-permute-start.19 = (bf16[2,32,512]{2,1,0:T(8,128)(2,1)S(1)}, bf16[2,32,512]{2,1,0:T(8,128)(2,1)S(1)}, u32[]{:S(2)}, u32[]{:S(2)}) collective-permute-start(bf16[2,32,512]{2,1,0:T(8,128)(2,1)S(1)} %get-tuple-element.28), channel_id=1, source_target_pairs={{0,64},{4,68},{8,72},{12,76},{16,80},{20,84},{24,88},{28,92},{32,9... | collective-permute-start | bytes 196616 | tf_op jit(solution)/shard_map/ppermute | solution.py:44
  237.9 5.8 %collective-permute-start.21 = (bf16[2,32,512]{2,1,0:T(8,128)(2,1)S(1)}, bf16[2,32,512]{2,1,0:T(8,128)(2,1)S(1)}, u32[]{:S(2)}, u32[]{:S(2)}) collective-permute-start(bf16[2,32,512]{2,1,0:T(8,128)(2,1)S(1)} %get-tuple-element.30), channel_id=1, source_target_pairs={{0,128},{4,132},{8,136},{12,140},{16,144},{20,148},{24,152},{28,15... | collective-permute-start | bytes 196616 | tf_op jit(solution)/shard_map/ppermute | solution.py:44
  (40 other events, 382.1 us)
where the time goes:
time: 248 us; the launch traced here: 244 us
  waiting for transfers between devices  107 us (43%)
  starting transfers between devices  68.7 us (28%)
  other arithmetic  23.1 us (9%)
  local copies, waits for them, and re-layouts  17.6 us (7%)
  matrix products  12.6 us (5%)
  Pallas kernels  12.1 us (5%)
  between operations  3.27 us (1%)
    ppermute x12, waiting for transfers between devices, send_y(): return lax.ppermute(value, 'seq', y_pairs(step))  43.2 us
    all_to_all x4, waiting for transfers between devices, exchange(): lax.all_to_all(value, 'seq', 0, 0, axis_index_groups=groups, tiled=True)  33.4 us
    ppermute x6, waiting for transfers between devices, send_x(): return lax.ppermute(value, 'mp', [(i, (i + step) % NX) for i in range(NX)])  29.7 us
    ppermute x12, starting transfers between devices, send_y(): return lax.ppermute(value, 'seq', y_pairs(step))  27.8 us
    all_to_all x4, starting transfers between devices, exchange(): lax.all_to_all(value, 'seq', 0, 0, axis_index_groups=groups, tiled=True)  27.4 us
    pallas_call x3, Pallas kernels, place(): pl.pallas_call(kernel, out_shape=tuple((jax.ShapeDtypeStruct(shape, bf16)...  12.1 us
    ppermute x6, starting transfers between devices, send_x(): return lax.ppermute(value, 'mp', [(i, (i + step) % NX) for i in range(NX)])  9.68 us
  transfers between devices with their start and end apart: 26, of which 18 were waited for; matrix products, arithmetic and copies ran while one was open for 13% of the time, Pallas kernels for 3%

commit v1 on v0

--- a/solution.py
+++ b/solution.py
@@ -190,10 +190,15 @@
     out_part = lax.dot_general(
         wide_up, activation, (((0,), (0,)), ((), ())), preferred_element_type=f32
     )
-    out_pieces = out_part.astype(bf16).reshape(NY, NZ * NC, 32, hidden).swapaxes(0, 1)
-    out_rows = exchange(out_pieces.reshape(NZ * NC, NY * 32, hidden), ZC_GROUPS)
-    out_rows = jnp.sum(out_rows.astype(f32).reshape(NZ, NC, NY, 32, hidden), axis=0)
-    grad_out = reduce_by_y(out_rows.swapaxes(0, 1), y_idx)
+    out_part = out_part.astype(bf16)
+    z_first = hidden - hidden // 4
+    out_pieces = out_part[:, :z_first].reshape(NY, NZ * NC, 32, z_first).swapaxes(0, 1)
+    out_rows = exchange(out_pieces.reshape(NZ * NC, NY * 32, z_first), ZC_GROUPS)
+    out_rows = jnp.sum(out_rows.astype(f32).reshape(NZ, NC, NY, 32, z_first), axis=0)
+    out_first = reduce_by_y(out_rows.swapaxes(0, 1), y_idx)
+    out_second = reduce_by_y(
+        out_part[:, z_first:].reshape(NY, NZ * NC * 32, hidden - z_first), y_idx
+    )
     up_proj = jnp.dot(wide_up, full_w_out, preferred_element_type=f32)
     act_grad = jax.vjp(gelu_tanh, pre_act)[1](up_proj)[0].astype(bf16)
     stat_part = jnp.sum(act_grad.astype(f32) * pre_act, axis=1) / inv_rms
@@ -201,8 +206,11 @@
         normed, act_grad, (((0,), (0,)), ((), ())), preferred_element_type=f32
     ).astype(bf16)
     in_rows = reduce_by_y(in_part.reshape(NY, NZ * NC * 32, hidden), y_idx)
-    in_rows = exchange(in_rows.astype(bf16).reshape(NZ * NC, 32, hidden), ZC_GROUPS)
-    grad_in = jnp.sum(in_rows.astype(f32).reshape(NZ, NC, 32, hidden), axis=0)
+    in_rows = jnp.concatenate([in_rows, out_second], axis=1).astype(bf16)
+    in_rows = exchange(in_rows.reshape(NZ * NC, 32, in_rows.shape[1]), ZC_GROUPS)
+    in_rows = jnp.sum(in_rows.astype(f32).reshape(NZ, NC, 32, in_rows.shape[2]), axis=0)
+    grad_in = in_rows[:, :, :hidden]
+    grad_out = jnp.concatenate([out_first, in_rows[:, :, hidden:]], axis=2)
 
     normed_part = lax.dot_general(
         act_grad, full_w_in, (((1,), (1,)), ((), ())), preferred_element_type=f32

time: 248 us -> 247 us (level)
  starting transfers between devices: 68.7 us -> 87.6 us
  other arithmetic: 23.1 us -> 17.4 us
  matrix products: 12.6 us -> 7.46 us
  local copies, waits for them, and re-layouts: 17.6 us -> 13 us
  waiting for transfers between devices: 107 us -> 103 us
    ppermute x2, starting transfers between devices: 0.41 us -> 8.64 us  [swap_cores(): return lax.ppermute(value, 'seq', CORE_SWAP)]
    ppermute x6, waiting for transfers between devices: 29.7 us -> 21.9 us  [send_x(): return lax.ppermute(value, 'mp', [(i, (i + step) % NX) for i in range(NX)])]
    all_to_all x4, starting transfers between devices: 27.4 us -> 34.9 us  [exchange(): lax.all_to_all(value, 'seq', 0, 0, axis_index_groups=groups, tiled=True)]
    ppermute x12 -> x15, waiting for transfers between devices: 43.2 us -> 50.6 us  [send_y(): return lax.ppermute(value, 'seq', y_pairs(step))]
    all_to_all x4, waiting for transfers between devices: 33.4 us -> 29.2 us  [exchange(): lax.all_to_all(value, 'seq', 0, 0, axis_index_groups=groups, tiled=True)]
    unnamed x76 -> x30, local copies, waits for them, and re-layouts: 4.58 us -> 1.58 us
    convert_element_type x1 -> x0, other arithmetic: 2.58 us -> none  [local(): in_rows.astype(bf16).reshape(NZ * NC, 32, hidden)]
    ppermute x12 -> x15, starting transfers between devices: 27.8 us -> 29 us  [send_y(): return lax.ppermute(value, 'seq', y_pairs(step))]
  transfers between devices with their start and end apart: 26 -> 29, of which waited for: 18 -> 18; matrix products, arithmetic and copies ran while one was open for 13% -> 9% of each run, Pallas kernels for 3% -> 3%
where the time goes in v1:
time: 247 us; the launch traced here: 244 us
  waiting for transfers between devices  103 us (42%)
  starting transfers between devices  87.6 us (35%)
  other arithmetic  17.4 us (7%)
  local copies, waits for them, and re-layouts  13 us (5%)
  Pallas kernels  12 us (5%)
  matrix products  7.46 us (3%)
  between operations  2.89 us (1%)
    ppermute x15, waiting for transfers between devices, send_y(): return lax.ppermute(value, 'seq', y_pairs(step))  50.6 us
    all_to_all x4, starting transfers between devices, exchange(): lax.all_to_all(value, 'seq', 0, 0, axis_index_groups=groups, tiled=True)  34.9 us
    all_to_all x4, waiting for transfers between devices, exchange(): lax.all_to_all(value, 'seq', 0, 0, axis_index_groups=groups, tiled=True)  29.2 us
    ppermute x15, starting transfers between devices, send_y(): return lax.ppermute(value, 'seq', y_pairs(step))  29 us
    ppermute x6, waiting for transfers between devices, send_x(): return lax.ppermute(value, 'mp', [(i, (i + step) % NX) for i in range(NX)])  21.9 us
    pallas_call x3, Pallas kernels, place(): pl.pallas_call(kernel, out_shape=tuple((jax.ShapeDtypeStruct(shape, bf16)...  12 us
    ppermute x6, starting transfers between devices, send_x(): return lax.ppermute(value, 'mp', [(i, (i + step) % NX) for i in range(NX)])  11.1 us
    ppermute x2, starting transfers between devices, swap_cores(): return lax.ppermute(value, 'seq', CORE_SWAP)  8.64 us
  transfers between devices with their start and end apart: 29, of which 18 were waited for; matrix products, arithmetic and copies ran while one was open for 9% of the time, Pallas kernels for 3%

profile of v1, /device:TPU:2, one launch (start us, length us, event | category | flops | bytes accessed | tf_op | source)
XLA Modules:
  0.0 243.5 jit_solution(3377203339081029548)
XLA Ops:
  2.5 8.6 %all-to-all-start.1 = ((bf16[16,32,512]{2,1,0:T(8,128)(2,1)}), bf16[16,32,512]{2,1,0:T(8,128)(2,1)}, u32[]{:S(2)}, u32[]{:S(2)}) async-start(bf16[16,32,512]{2,1,0:T(8,128)(2,1)} %bitcast.19), calls=%async_computation.1 | async-start | bytes 1048576 | tf_op jit(solution)/shard_map/all_to_all | solution.py:52
  20.5 3.3 %collective-permute-start.3 = (bf16[2,224,512]{2,1,0:T(8,128)(2,1)S(1)}, bf16[2,224,512]{2,1,0:T(8,128)(2,1)S(1)}, u32[]{:S(2)}, u32[]{:S(2)}) collective-permute-start(bf16[2,224,512]{2,1,0:T(8,128)(2,1)S(1)} %get-tuple-element.32), channel_id=1, source_target_pairs={{0,2},{1,3},{2,0},{3,1},{4,6},{5,7},{6,4},{7,5},{8,10},{9,11},{10,... | collective-permute-start | bytes 1376264 | tf_op jit(solution)/shard_map/ppermute | solution.py:48
  23.8 3.1 %collective-permute-done.2 = bf16[2,224,512]{2,1,0:T(8,128)(2,1)S(1)} collective-permute-done((bf16[2,224,512]{2,1,0:T(8,128)(2,1)S(1)}, bf16[2,224,512]{2,1,0:T(8,128)(2,1)S(1)}, u32[]{:S(2)}, u32[]{:S(2)}) %collective-permute-start.2) | collective-permute-done | bytes 458784 | tf_op jit(solution)/shard_map/ppermute | solution.py:48
  28.2 6.0 %collective-permute-done.3 = bf16[2,224,512]{2,1,0:T(8,128)(2,1)S(1)} collective-permute-done((bf16[2,224,512]{2,1,0:T(8,128)(2,1)S(1)}, bf16[2,224,512]{2,1,0:T(8,128)(2,1)S(1)}, u32[]{:S(2)}, u32[]{:S(2)}) %collective-permute-start.3) | collective-permute-done | bytes 458784 | tf_op jit(solution)/shard_map/ppermute | solution.py:48
  34.5 8.3 %collective-permute-start.4 = (bf16[4,2,224,512]{3,2,1,0:T(8,128)(2,1)S(1)}, bf16[4,2,224,512]{3,2,1,0:T(8,128)(2,1)}, u32[]{:S(2)}, u32[]{:S(2)}) collective-permute-start(bf16[4,2,224,512]{3,2,1,0:T(8,128)(2,1)S(1)} %pad_maximum_fusion.own_ref), channel_id=1, source_target_pairs={{0,4},{4,0},{8,12},{12,8},{16,20},{20,16},{24,28},{28,24},{32,36},... | collective-permute-start | bytes 5505032 | tf_op jit(solution)/shard_map/ppermute | solution.py:40
  43.7 14.6 %all-to-all-start = ((bf16[16,32,512]{2,1,0:T(8,128)(2,1)}), bf16[16,32,512]{2,1,0:T(8,128)(2,1)}, u32[]{:S(2)}, u32[]{:S(2)}) async-start(bf16[16,32,512]{2,1,0:T(8,128)(2,1)} %bitcast.107), calls=%async_computation | async-start | bytes 1048576 | tf_op jit(solution)/shard_map/all_to_all | solution.py:52
  58.2 3.3 %collective-permute-start.10 = (bf16[512,512]{1,0:T(8,128)(2,1)}, bf16[512,512]{1,0:T(8,128)(2,1)}, u32[]{:S(2)}, u32[]{:S(2)}) collective-permute-start(bf16[512,512]{1,0:T(8,128)(2,1)} %bitcast.20.refs_0_), channel_id=1, source_target_pairs={{0,128},{4,132},{8,136},{12,140},{16,144},{20,148},{24,152},{28,15... | collective-permute-start | bytes 1572872 | tf_op jit(solution)/shard_map/ppermute | solution.py:44
  63.6 10.7 %all-to-all-done = bf16[16,32,512]{2,1,0:T(8,128)(2,1)} async-done(((bf16[16,32,512]{2,1,0:T(8,128)(2,1)}), bf16[16,32,512]{2,1,0:T(8,128)(2,1)}, u32[]{:S(2)}, u32[]{:S(2)}) %all-to-all-start) | async-done | bytes 524320 | tf_op jit(solution)/shard_map/all_to_all | solution.py:52
  74.2 3.2 %collective-permute-start.7 = (bf16[512,512]{1,0:T(8,128)(2,1)}, bf16[512,512]{1,0:T(8,128)(2,1)}, u32[]{:S(2)}, u32[]{:S(2)}) collective-permute-start(bf16[512,512]{1,0:T(8,128)(2,1)} %bitcast.15.refs_0_), channel_id=1, source_target_pairs={{0,128},{4,132},{8,136},{12,140},{16,144},{20,148},{24,152},{28,15... | collective-permute-start | bytes 1572872 | tf_op jit(solution)/shard_map/ppermute | solution.py:44
  78.5 8.1 %collective-permute-done.9.refs_2_ = bf16[512,512]{1,0:T(8,128)(2,1)} collective-permute-done((bf16[512,512]{1,0:T(8,128)(2,1)}, bf16[512,512]{1,0:T(8,128)(2,1)}, u32[]{:S(2)}, u32[]{:S(2)}) %collective-permute-start.9) | collective-permute-done | bytes 524320 | tf_op jit(solution)/shard_map/ppermute | solution.py:44
  88.5 3.5 %shard_map.78 = bf16[4,512,512]{2,1,0:T(8,128)(2,1)} custom-call(s32[2]{0:T(128)} %pad_add_fusion.at_ref, bf16[512,512]{1,0:T(8,128)(2,1)} %bitcast.20.refs_0_, bf16[512,512]{1,0:T(8,128)(2,1)} %collective-permute-done.8.refs_1_, bf16[512,512]{1,0:T(8,128)(2,1)} %collective-permute-done.9.refs_2_, bf16[512,512]{1,0:T(8,128)(2,1)} %collective-permute-done.10.refs_3_), custom_call_target="tpu_custom_call" | custom-call | bytes 4194304 | tf_op jit(solution)/shard_map/pallas_call | solution.py:107
  92.0 5.5 %collective-permute-done.7.refs_3_ = bf16[512,512]{1,0:T(8,128)(2,1)} collective-permute-done((bf16[512,512]{1,0:T(8,128)(2,1)}, bf16[512,512]{1,0:T(8,128)(2,1)}, u32[]{:S(2)}, u32[]{:S(2)}) %collective-permute-start.7) | collective-permute-done | bytes 524320 | tf_op jit(solution)/shard_map/ppermute | solution.py:44
  97.5 10.9 %collective-permute-done.6.refs_2_ = bf16[512,512]{1,0:T(8,128)(2,1)} collective-permute-done((bf16[512,512]{1,0:T(8,128)(2,1)}, bf16[512,512]{1,0:T(8,128)(2,1)}, u32[]{:S(2)}, u32[]{:S(2)}) %collective-permute-start.6) | collective-permute-done | bytes 524320 | tf_op jit(solution)/shard_map/ppermute | solution.py:44
  108.4 3.5 %shard_map.77 = bf16[4,512,512]{2,1,0:T(8,128)(2,1)} custom-call(s32[2]{0:T(128)} %pad_add_fusion.at_ref, bf16[512,512]{1,0:T(8,128)(2,1)} %bitcast.15.refs_0_, bf16[512,512]{1,0:T(8,128)(2,1)} %collective-permute-done.5.refs_1_, bf16[512,512]{1,0:T(8,128)(2,1)} %collective-permute-done.6.refs_2_, bf16[512,512]{1,0:T(8,128)(2,1)} %collective-permute-done.7.refs_3_), custom_call_target="tpu_custom_call" | custom-call | bytes 4194304 | tf_op jit(solution)/shard_map/pallas_call | solution.py:107
  111.9 4.9 %shard_map.76 = (bf16[448,2048]{1,0:T(8,128)(2,1)}, bf16[448,2048]{1,0:T(8,128)(2,1)}) custom-call(s32[2]{0:T(128)} %pad_add_fusion.at_ref, bf16[4,2,224,512]{3,2,1,0:T(8,128)(2,1)} %copy-done.3, bf16[4,2,224,512]{3,2,1,0:T(8,128)(2,1)} %collective-permute-done.4.other_ref), custom_call_target="tpu_custom_call" | custom-call | bytes 7340032 | tf_op jit(solution)/shard_map/pallas_call | solution.py:107
  136.7 22.6 %collective-permute-done.21 = bf16[512,128]{1,0:T(8,128)(2,1)S(1)} collective-permute-done((bf16[512,128]{1,0:T(8,128)(2,1)S(1)}, bf16[512,128]{1,0:T(8,128)(2,1)S(1)}, u32[]{:S(2)}, u32[]{:S(2)}) %collective-permute-start.21) | collective-permute-done | bytes 131104 | tf_op jit(solution)/shard_map/ppermute | solution.py:44
  161.5 7.0 %all-to-all-start.2 = ((bf16[16,32,640]{2,1,0:T(8,128)(2,1)}), bf16[16,32,640]{2,1,0:T(8,128)(2,1)}, u32[]{:S(2)}, u32[]{:S(2)}) async-start(bf16[16,32,640]{2,1,0:T(8,128)(2,1)} %pad_maximum_fusion.2), calls=%async_computation.2 | async-start | bytes 1310720 | tf_op jit(solution)/shard_map/all_to_all | solution.py:52
  173.7 13.1 %all-to-all-done.2 = bf16[16,32,640]{2,1,0:T(8,128)(2,1)} async-done(((bf16[16,32,640]{2,1,0:T(8,128)(2,1)}), bf16[16,32,640]{2,1,0:T(8,128)(2,1)}, u32[]{:S(2)}, u32[]{:S(2)}) %all-to-all-start.2) | async-done | bytes 655392 | tf_op jit(solution)/shard_map/all_to_all | solution.py:52
  186.8 4.8 %all-to-all-start.3 = ((bf16[16,128,384]{2,1,0:T(8,128)(2,1)}), bf16[16,128,384]{2,1,0:T(8,128)(2,1)}, u32[]{:S(2)}, u32[]{:S(2)}) async-start(bf16[16,128,384]{2,1,0:T(8,128)(2,1)} %bitcast.100), calls=%async_computation.3 | async-start | bytes 3145728 | tf_op jit(solution)/shard_map/all_to_all | solution.py:52
  202.8 3.0 %collective-permute-done.12 = bf16[224,640]{1,0:T(8,128)(2,1)S(1)} collective-permute-done((bf16[224,640]{1,0:T(8,128)(2,1)S(1)}, bf16[224,640]{1,0:T(8,128)(2,1)S(1)}, u32[]{:S(2)}, u32[]{:S(2)}) %collective-permute-start.12) | collective-permute-done | bytes 286752 | tf_op jit(solution)/shard_map/ppermute | solution.py:48
  206.7 7.6 %collective-permute-done.14 = bf16[224,640]{1,0:T(8,128)(2,1)S(1)} collective-permute-done((bf16[224,640]{1,0:T(8,128)(2,1)}, bf16[224,640]{1,0:T(8,128)(2,1)S(1)}, u32[]{:S(2)}, u32[]{:S(2)}) %collective-permute-start.14) | collective-permute-done | bytes 286752 | tf_op jit(solution)/shard_map/ppermute | solution.py:48
  216.3 2.8 %collective-permute-start.15 = (f32[1,512]{1,0:T(1,128)S(1)}, f32[1,512]{1,0:T(1,128)S(1)}, u32[]{:S(2)}, u32[]{:S(2)}) collective-permute-start(f32[1,512]{1,0:T(1,128)S(1)} %constant_dynamic-slice_fusion), channel_id=1, source_target_pairs={{0,4},{4,8},{8,12},{12,16},{16,20},{20,24},{24,28},{28,32},{32,36}... | collective-permute-start | bytes 6152 | tf_op jit(solution)/shard_map/ppermute | solution.py:253
  223.8 5.5 %all-to-all-done.3 = bf16[16,128,384]{2,1,0:T(8,128)(2,1)} async-done(((bf16[16,128,384]{2,1,0:T(8,128)(2,1)}), bf16[16,128,384]{2,1,0:T(8,128)(2,1)}, u32[]{:S(2)}, u32[]{:S(2)}) %all-to-all-start.3) | async-done | bytes 1572896 | tf_op jit(solution)/shard_map/all_to_all | solution.py:52
  231.0 4.7 %collective-permute-start.22 = (bf16[2,32,384]{2,1,0:T(8,128)(2,1)S(1)}, bf16[2,32,384]{2,1,0:T(8,128)(2,1)S(1)}, u32[]{:S(2)}, u32[]{:S(2)}) collective-permute-start(bf16[2,32,384]{2,1,0:T(8,128)(2,1)S(1)} %get-tuple-element.33), channel_id=1, source_target_pairs={{0,64},{4,68},{8,72},{12,76},{16,80},{20,84},{24,88},{28,92},{32,9... | collective-permute-start | bytes 147464 | tf_op jit(solution)/shard_map/ppermute | solution.py:44
  (144 shorter events, 72.1 us)
Async XLA Ops:
  2.5 40.3 %all-to-all-start.1 = ((bf16[16,32,512]{2,1,0:T(8,128)(2,1)}), bf16[16,32,512]{2,1,0:T(8,128)(2,1)}, u32[]{:S(2)}, u32[]{:S(2)}) async-start(bf16[16,32,512]{2,1,0:T(8,128)(2,1)} %bitcast.19), calls=%async_computation.1 | async-start | bytes 1048576 | tf_op jit(solution)/shard_map/all_to_all | solution.py:52
  18.4 8.6 %collective-permute-start.2 = (bf16[2,224,512]{2,1,0:T(8,128)(2,1)S(1)}, bf16[2,224,512]{2,1,0:T(8,128)(2,1)S(1)}, u32[]{:S(2)}, u32[]{:S(2)}) collective-permute-start(bf16[2,224,512]{2,1,0:T(8,128)(2,1)S(1)} %get-tuple-element.32), channel_id=1, source_target_pairs={{0,3},{1,0},{2,1},{3,2},{4,7},{5,4},{6,5},{7,6},{8,11},{9,8},{10,9... | collective-permute-start | bytes 1376264 | tf_op jit(solution)/shard_map/ppermute | solution.py:48
  19.0 9.2 %collective-permute-start.1 = (bf16[2,224,512]{2,1,0:T(8,128)(2,1)S(1)}, bf16[2,224,512]{2,1,0:T(8,128)(2,1)S(1)}, u32[]{:S(2)}, u32[]{:S(2)}) collective-permute-start(bf16[2,224,512]{2,1,0:T(8,128)(2,1)S(1)} %get-tuple-element.32), channel_id=1, source_target_pairs={{0,1},{1,2},{2,3},{3,0},{4,5},{5,6},{6,7},{7,4},{8,9},{9,10},{10,1... | collective-permute-start | bytes 1376264 | tf_op jit(solution)/shard_map/ppermute | solution.py:48
  20.5 13.8 %collective-permute-start.3 = (bf16[2,224,512]{2,1,0:T(8,128)(2,1)S(1)}, bf16[2,224,512]{2,1,0:T(8,128)(2,1)S(1)}, u32[]{:S(2)}, u32[]{:S(2)}) collective-permute-start(bf16[2,224,512]{2,1,0:T(8,128)(2,1)S(1)} %get-tuple-element.32), channel_id=1, source_target_pairs={{0,2},{1,3},{2,0},{3,1},{4,6},{5,7},{6,4},{7,5},{8,10},{9,11},{10,... | collective-permute-start | bytes 1376264 | tf_op jit(solution)/shard_map/ppermute | solution.py:48
  34.5 77.4 %collective-permute-start.4 = (bf16[4,2,224,512]{3,2,1,0:T(8,128)(2,1)S(1)}, bf16[4,2,224,512]{3,2,1,0:T(8,128)(2,1)}, u32[]{:S(2)}, u32[]{:S(2)}) collective-permute-start(bf16[4,2,224,512]{3,2,1,0:T(8,128)(2,1)S(1)} %pad_maximum_fusion.own_ref), channel_id=1, source_target_pairs={{0,4},{4,0},{8,12},{12,8},{16,20},{20,16},{24,28},{28,24},{32,36},... | collective-permute-start | bytes 5505032 | tf_op jit(solution)/shard_map/ppermute | solution.py:40
  43.7 30.6 %all-to-all-start = ((bf16[16,32,512]{2,1,0:T(8,128)(2,1)}), bf16[16,32,512]{2,1,0:T(8,128)(2,1)}, u32[]{:S(2)}, u32[]{:S(2)}) async-start(bf16[16,32,512]{2,1,0:T(8,128)(2,1)} %bitcast.107), calls=%async_computation | async-start | bytes 1048576 | tf_op jit(solution)/shard_map/all_to_all | solution.py:52
  58.2 19.2 %collective-permute-start.10 = (bf16[512,512]{1,0:T(8,128)(2,1)}, bf16[512,512]{1,0:T(8,128)(2,1)}, u32[]{:S(2)}, u32[]{:S(2)}) collective-permute-start(bf16[512,512]{1,0:T(8,128)(2,1)} %bitcast.20.refs_0_), channel_id=1, source_target_pairs={{0,128},{4,132},{8,136},{12,140},{16,144},{20,148},{24,152},{28,15... | collective-permute-start | bytes 1572872 | tf_op jit(solution)/shard_map/ppermute | solution.py:44
  61.5 25.0 %collective-permute-start.9 = (bf16[512,512]{1,0:T(8,128)(2,1)}, bf16[512,512]{1,0:T(8,128)(2,1)}, u32[]{:S(2)}, u32[]{:S(2)}) collective-permute-start(bf16[512,512]{1,0:T(8,128)(2,1)} %bitcast.20.refs_0_), channel_id=1, source_target_pairs={{0,192},{4,196},{8,200},{12,204},{16,208},{20,212},{24,216},{28,22... | collective-permute-start | bytes 1572872 | tf_op jit(solution)/shard_map/ppermute | solution.py:44
  62.6 25.9 %collective-permute-start.8 = (bf16[512,512]{1,0:T(8,128)(2,1)}, bf16[512,512]{1,0:T(8,128)(2,1)}, u32[]{:S(2)}, u32[]{:S(2)}) collective-permute-start(bf16[512,512]{1,0:T(8,128)(2,1)} %bitcast.20.refs_0_), channel_id=1, source_target_pairs={{0,64},{4,68},{8,72},{12,76},{16,80},{20,84},{24,88},{28,92},{32,9... | collective-permute-start | bytes 1572872 | tf_op jit(solution)/shard_map/ppermute | solution.py:44
  74.2 23.3 %collective-permute-start.7 = (bf16[512,512]{1,0:T(8,128)(2,1)}, bf16[512,512]{1,0:T(8,128)(2,1)}, u32[]{:S(2)}, u32[]{:S(2)}) collective-permute-start(bf16[512,512]{1,0:T(8,128)(2,1)} %bitcast.15.refs_0_), channel_id=1, source_target_pairs={{0,128},{4,132},{8,136},{12,140},{16,144},{20,148},{24,152},{28,15... | collective-permute-start | bytes 1572872 | tf_op jit(solution)/shard_map/ppermute | solution.py:44
  77.4 31.0 %collective-permute-start.6 = (bf16[512,512]{1,0:T(8,128)(2,1)}, bf16[512,512]{1,0:T(8,128)(2,1)}, u32[]{:S(2)}, u32[]{:S(2)}) collective-permute-start(bf16[512,512]{1,0:T(8,128)(2,1)} %bitcast.15.refs_0_), channel_id=1, source_target_pairs={{0,192},{4,196},{8,200},{12,204},{16,208},{20,212},{24,216},{28,22... | collective-permute-start | bytes 1572872 | tf_op jit(solution)/shard_map/ppermute | solution.py:44
  86.6 21.8 %collective-permute-start.5 = (bf16[512,512]{1,0:T(8,128)(2,1)}, bf16[512,512]{1,0:T(8,128)(2,1)}, u32[]{:S(2)}, u32[]{:S(2)}) collective-permute-start(bf16[512,512]{1,0:T(8,128)(2,1)} %bitcast.15.refs_0_), channel_id=1, source_target_pairs={{0,64},{4,68},{8,72},{12,76},{16,80},{20,84},{24,88},{28,92},{32,9... | collective-permute-start | bytes 1572872 | tf_op jit(solution)/shard_map/ppermute | solution.py:44
  126.5 8.1 %collective-permute-start.19 = (bf16[512,128]{1,0:T(8,128)(2,1)S(1)}, bf16[512,128]{1,0:T(8,128)(2,1)S(1)}, u32[]{:S(2)}, u32[]{:S(2)}) collective-permute-start(bf16[512,128]{1,0:T(8,128)(2,1)S(1)} %get-tuple-element.28), channel_id=1, source_target_pairs={{0,64},{4,68},{8,72},{12,76},{16,80},{20,84},{24,88},{28,92},{32,9... | collective-permute-start | bytes 393224 | tf_op jit(solution)/shard_map/ppermute | solution.py:44
  128.1 32.2 %collective-permute-start.16 = (bf16[512,512]{1,0:T(8,128)(2,1)S(1)}, bf16[512,512]{1,0:T(8,128)(2,1)S(1)}, u32[]{:S(2)}, u32[]{:S(2)}) collective-permute-start(bf16[512,512]{1,0:T(8,128)(2,1)S(1)} %get-tuple-element.22), channel_id=1, source_target_pairs={{0,64},{4,68},{8,72},{12,76},{16,80},{20,84},{24,88},{28,92},{32,9... | collective-permute-start | bytes 1572872 | tf_op jit(solution)/shard_map/ppermute | solution.py:44
  129.6 30.7 %collective-permute-start.18 = (bf16[512,512]{1,0:T(8,128)(2,1)S(1)}, bf16[512,512]{1,0:T(8,128)(2,1)S(1)}, u32[]{:S(2)}, u32[]{:S(2)}) collective-permute-start(bf16[512,512]{1,0:T(8,128)(2,1)S(1)} %get-tuple-element.23), channel_id=1, source_target_pairs={{0,128},{4,132},{8,136},{12,140},{16,144},{20,148},{24,152},{28,15... | collective-permute-start | bytes 1572872 | tf_op jit(solution)/shard_map/ppermute | solution.py:44
  131.5 28.8 %collective-permute-start.17 = (bf16[512,512]{1,0:T(8,128)(2,1)S(1)}, bf16[512,512]{1,0:T(8,128)(2,1)S(1)}, u32[]{:S(2)}, u32[]{:S(2)}) collective-permute-start(bf16[512,512]{1,0:T(8,128)(2,1)S(1)} %get-tuple-element.24), channel_id=1, source_target_pairs={{0,192},{4,196},{8,200},{12,204},{16,208},{20,212},{24,216},{28,22... | collective-permute-start | bytes 1572872 | tf_op jit(solution)/shard_map/ppermute | solution.py:44
  133.6 25.7 %collective-permute-start.21 = (bf16[512,128]{1,0:T(8,128)(2,1)S(1)}, bf16[512,128]{1,0:T(8,128)(2,1)S(1)}, u32[]{:S(2)}, u32[]{:S(2)}) collective-permute-start(bf16[512,128]{1,0:T(8,128)(2,1)S(1)} %get-tuple-element.29), channel_id=1, source_target_pairs={{0,128},{4,132},{8,136},{12,140},{16,144},{20,148},{24,152},{28,15... | collective-permute-start | bytes 393224 | tf_op jit(solution)/shard_map/ppermute | solution.py:44
  134.6 25.6 %collective-permute-start.20 = (bf16[512,128]{1,0:T(8,128)(2,1)S(1)}, bf16[512,128]{1,0:T(8,128)(2,1)S(1)}, u32[]{:S(2)}, u32[]{:S(2)}) collective-permute-start(bf16[512,128]{1,0:T(8,128)(2,1)S(1)} %get-tuple-element.30), channel_id=1, source_target_pairs={{0,192},{4,196},{8,200},{12,204},{16,208},{20,212},{24,216},{28,22... | collective-permute-start | bytes 393224 | tf_op jit(solution)/shard_map/ppermute | solution.py:44
  161.5 25.3 %all-to-all-start.2 = ((bf16[16,32,640]{2,1,0:T(8,128)(2,1)}), bf16[16,32,640]{2,1,0:T(8,128)(2,1)}, u32[]{:S(2)}, u32[]{:S(2)}) async-start(bf16[16,32,640]{2,1,0:T(8,128)(2,1)} %pad_maximum_fusion.2), calls=%async_computation.2 | async-start | bytes 1310720 | tf_op jit(solution)/shard_map/all_to_all | solution.py:52
  186.8 42.5 %all-to-all-start.3 = ((bf16[16,128,384]{2,1,0:T(8,128)(2,1)}), bf16[16,128,384]{2,1,0:T(8,128)(2,1)}, u32[]{:S(2)}, u32[]{:S(2)}) async-start(bf16[16,128,384]{2,1,0:T(8,128)(2,1)} %bitcast.100), calls=%async_computation.3 | async-start | bytes 3145728 | tf_op jit(solution)/shard_map/all_to_all | solution.py:52
  195.5 10.3 %collective-permute-start.12 = (bf16[224,640]{1,0:T(8,128)(2,1)S(1)}, bf16[224,640]{1,0:T(8,128)(2,1)S(1)}, u32[]{:S(2)}, u32[]{:S(2)}) collective-permute-start(bf16[224,640]{1,0:T(8,128)(2,1)S(1)} %get-tuple-element.36), channel_id=1, source_target_pairs={{0,1},{1,2},{2,3},{3,0},{4,5},{5,6},{6,7},{7,4},{8,9},{9,10},{10,1... | collective-permute-start | bytes 860168 | tf_op jit(solution)/shard_map/ppermute | solution.py:48
  197.3 9.3 %collective-permute-start.13 = (bf16[224,640]{1,0:T(8,128)(2,1)S(1)}, bf16[224,640]{1,0:T(8,128)(2,1)S(1)}, u32[]{:S(2)}, u32[]{:S(2)}) collective-permute-start(bf16[224,640]{1,0:T(8,128)(2,1)S(1)} %get-tuple-element.37), channel_id=1, source_target_pairs={{0,3},{1,0},{2,1},{3,2},{4,7},{5,4},{6,5},{7,6},{8,11},{9,8},{10,9... | collective-permute-start | bytes 860168 | tf_op jit(solution)/shard_map/ppermute | solution.py:48
  199.1 15.2 %collective-permute-start.14 = (bf16[224,640]{1,0:T(8,128)(2,1)}, bf16[224,640]{1,0:T(8,128)(2,1)S(1)}, u32[]{:S(2)}, u32[]{:S(2)}) collective-permute-start(bf16[224,640]{1,0:T(8,128)(2,1)} %get-tuple-element.38), channel_id=1, source_target_pairs={{0,2},{1,3},{2,0},{3,1},{4,6},{5,7},{6,4},{7,5},{8,10},{9,11},{10,... | collective-permute-start | bytes 860168 | tf_op jit(solution)/shard_map/ppermute | solution.py:48
  231.0 9.2 %collective-permute-start.22 = (bf16[2,32,384]{2,1,0:T(8,128)(2,1)S(1)}, bf16[2,32,384]{2,1,0:T(8,128)(2,1)S(1)}, u32[]{:S(2)}, u32[]{:S(2)}) collective-permute-start(bf16[2,32,384]{2,1,0:T(8,128)(2,1)S(1)} %get-tuple-element.33), channel_id=1, source_target_pairs={{0,64},{4,68},{8,72},{12,76},{16,80},{20,84},{24,88},{28,92},{32,9... | collective-permute-start | bytes 147464 | tf_op jit(solution)/shard_map/ppermute | solution.py:44
  (21 other events, 189.2 us)

commit v2 on v0

--- a/solution.py
+++ b/solution.py
@@ -64,30 +64,29 @@
     return [column] + [send_y(column, step) for step in (1, 3, 2)]
 
 
-def start_and_wait(pairs, sems):
-    copies = [
+STEPS = (0, 1, 3, 2)
+CHUNK = 64
+MIB = 1 << 20
+
+
+def copies_of(pairs, sems):
+    return [
         pltpu.make_async_copy(source, target, sems.at[n])
         for n, (source, target) in enumerate(pairs)
     ]
-    for item in copies:
-        item.start()
-    for item in copies:
-        item.wait()
-
-
-STEPS = (0, 1, 3, 2)
-
-
-def weight_kernel(at_ref, *refs):
-    parts, (full_ref, sems) = refs[:4], refs[4:]
-    pairs = [
-        (part, full_ref.at[lax.rem(at_ref[1] + NY - step, NY)])
-        for part, step in zip(parts, STEPS)
-    ]
-    start_and_wait(pairs, sems)
-
-
-def rows_kernel(at_ref, own_ref, other_ref, pooled_ref, up_ref, sems):
+
+
+def weight_copies(at_ref, parts, full_ref, sems):
+    return copies_of(
+        [
+            (part, full_ref.at[lax.rem(at_ref[1] + NY - step, NY)])
+            for part, step in zip(parts, STEPS)
+        ],
+        sems,
+    )
+
+
+def norm_kernel(at_ref, own_ref, other_ref, normed_ref, up_ref, rms_ref, pooled_ref, sems):
     rows, quarter = own_ref.shape[2:]
     pairs = []
     for half, part in enumerate((own_ref, other_ref)):
@@ -99,32 +98,131 @@
             )
             pairs.append((part.at[n, 0], pooled_ref.at[where]))
             pairs.append((part.at[n, 1], up_ref.at[where]))
-    start_and_wait(pairs, sems)
-
-
-def place(kernel, at, parts, shapes, n_copies):
-    moved = sum(2 * math.prod(shape) for shape in shapes)
+    copies = copies_of(pairs, sems)
+    for item in copies:
+        item.start()
+    for item in copies:
+        item.wait()
+
+    def norm_rows(i, carry):
+        at = pl.ds(pl.multiple_of(i * CHUNK, CHUNK), CHUNK)
+        values = pooled_ref[at, :].astype(f32)
+        rms = lax.rsqrt(jnp.mean(values * values, axis=1, keepdims=True) + epsilon)
+        normed_ref[at, :] = (values * rms).astype(bf16)
+        rms_ref[at, :] = jnp.broadcast_to(rms, (CHUNK, rms_ref.shape[1]))
+        return carry
+
+    lax.fori_loop(0, pooled_ref.shape[0] // CHUNK, norm_rows, 0)
+
+
+def act_kernel(at_ref, *refs):
+    parts, (normed_ref, up_ref, w_in_ref, pre_ref, out_ref, act_ref, sems) = refs[:4], refs[4:]
+    copies = weight_copies(at_ref, parts, w_in_ref, sems)
+    for item in copies:
+        item.start()
+    for item in copies:
+        item.wait()
+    rows, width = normed_ref.shape
+    depth, hidden = w_in_ref.shape[1:]
+    for n in range(0, hidden, 256):
+        weight = w_in_ref[:, :, n : n + 256].reshape(width, 256)
+        pre_ref[:, n : n + 256] = jnp.dot(normed_ref[...], weight, preferred_element_type=f32)
+
+    def act_rows(i, carry):
+        at = pl.ds(pl.multiple_of(i * CHUNK, CHUNK), CHUNK)
+        act_ref[at, :] = gelu_tanh(pre_ref[at, :]).astype(bf16)
+        return carry
+
+    lax.fori_loop(0, rows // CHUNK, act_rows, 0)
+    for y in range(NY):
+        part = lax.dot_general(
+            up_ref[:, y * depth : (y + 1) * depth],
+            act_ref[...],
+            (((0,), (0,)), ((), ())),
+            preferred_element_type=f32,
+        ).astype(bf16)
+        out_ref[:, y * 32 : (y + 1) * 32, :] = part.reshape(NZ * NC, 32, hidden)
+
+
+GELU_K = math.sqrt(2.0 / math.pi)
+
+
+def gelu_slope(v):
+    square = v * v
+    t = jnp.tanh(GELU_K * (v + 0.044715 * (square * v)))
+    inner = GELU_K * (1.0 + 3 * 0.044715 * square)
+    return 0.5 * (1.0 + t) + 0.5 * v * ((1.0 - t * t) * inner)
+
+
+def grad_kernel(at_ref, *refs):
+    parts, refs = refs[:4], refs[4:]
+    normed_ref, up_ref, w_in_ref, pre_ref, rms_ref = refs[:5]
+    in_refs, (own_ref, sent_ref, stat_ref) = refs[5:9], refs[9:12]
+    w_out_ref, proj_ref, grad_ref, row_ref, sems = refs[12:]
+    copies = weight_copies(at_ref, parts, w_out_ref, sems)
+    for item in copies:
+        item.start()
+    for item in copies:
+        item.wait()
+    rows, width = normed_ref.shape
+    depth, hidden = w_in_ref.shape[1:]
+    half = rows // 2
+    for n in range(0, hidden, 256):
+        weight = w_out_ref[:, :, n : n + 256].reshape(width, 256)
+        proj_ref[:, n : n + 256] = jnp.dot(up_ref[...], weight, preferred_element_type=f32)
+
+    def grad_rows(i, carry):
+        at = pl.ds(pl.multiple_of(i * CHUNK, CHUNK), CHUNK)
+        pre = pre_ref[at, :]
+        grad = (proj_ref[at, :] * gelu_slope(pre)).astype(bf16)
+        grad_ref[at, :] = grad
+        stat = jnp.sum(grad.astype(f32) * pre, axis=1, keepdims=True)
+        row_ref[at, :] = jnp.broadcast_to(stat, (CHUNK, 128)) / rms_ref[at, :]
+        return carry
+
+    lax.fori_loop(0, rows // CHUNK, grad_rows, 0)
+    for step, in_ref in zip(STEPS, in_refs):
+        y = lax.rem(at_ref[1] + step, NY)
+        block = normed_ref[:, pl.ds(pl.multiple_of(y * depth, depth), depth)]
+        in_ref[...] = lax.dot_general(
+            block, grad_ref[...], (((0,), (0,)), ((), ())), preferred_element_type=f32
+        ).astype(bf16)
+    for n in range(NY):
+        part = lax.dot_general(
+            grad_ref[...], w_in_ref[n], (((1,), (1,)), ((), ())), preferred_element_type=f32
+        )
+        own_ref[:, n * depth : (n + 1) * depth] = part[:half]
+        sent_ref[:, n * depth : (n + 1) * depth] = part[half:].astype(bf16)
+    stat = row_ref[half:, :]
+    high = stat.astype(bf16).astype(f32)
+    lane = lax.broadcasted_iota(jnp.int32, (half, 128), 1)
+    low = jnp.where(lane == 1, stat - high, 0.0)
+    sent_ref[:, width:] = jnp.where(lane == 0, high, low).astype(bf16)
+    stat_ref[...] = row_ref[:half, :]
+
+
+def call(kernel, at, far, near, outs, scratch, n_copies, limit, flops):
+    outs = [jax.ShapeDtypeStruct(shape, dtype) for shape, dtype in outs]
+    moved = sum(v.size * v.dtype.itemsize for v in [*far, *near, *outs])
     return pl.pallas_call(
         kernel,
-        out_shape=tuple(jax.ShapeDtypeStruct(shape, bf16) for shape in shapes),
+        out_shape=tuple(outs),
         in_specs=[pl.BlockSpec(memory_space=pltpu.SMEM)]
-        + [pl.BlockSpec(memory_space=pl.ANY)] * len(parts),
-        out_specs=(pl.BlockSpec(memory_space=pltpu.VMEM),) * len(shapes),
-        scratch_shapes=[pltpu.SemaphoreType.DMA((n_copies,))],
-        cost_estimate=pl.CostEstimate(flops=0, bytes_accessed=2 * moved, transcendentals=0),
-    )(at, *parts)
-
-
-def place_weight(at, parts):
-    depth, hidden = parts[0].shape
-    (full,) = place(weight_kernel, at, parts, [(NY, depth, hidden)], 4)
-    return full.reshape(NY * depth, hidden)
-
-
-def place_rows(at, own_parts, other_parts):
-    rows, quarter = own_parts.shape[2:]
-    wide = (2 * rows, NX * quarter)
-    return place(rows_kernel, at, [own_parts, other_parts], [wide, wide], 16)
+        + [pl.BlockSpec(memory_space=pl.ANY)] * len(far)
+        + [pl.BlockSpec(memory_space=pltpu.VMEM)] * len(near),
+        out_specs=(pl.BlockSpec(memory_space=pltpu.VMEM),) * len(outs),
+        scratch_shapes=[pltpu.VMEM(shape, dtype) for shape, dtype in scratch]
+        + [pltpu.SemaphoreType.DMA((n_copies,))],
+        cost_estimate=pl.CostEstimate(flops=flops, bytes_accessed=moved, transcendentals=0),
+        compiler_params=pltpu.CompilerParams(vmem_limit_bytes=limit * MIB),
+    )(at, *far, *near)
+
+
+def reduce_sent(own, pieces):
+    total = own.astype(f32)
+    for piece, step in zip(pieces, STEPS[1:]):
+        total = total + send_y(piece, step).astype(f32)
+    return total
 
 
 def reduce_by_y(pieces, y_idx):
@@ -178,45 +276,63 @@
     own_parts = jnp.stack(own_parts)
     other_parts = swap_cores(own_parts)
     at = jnp.stack([x_idx, y_idx]).astype(jnp.int32)
-    wide_pooled, wide_up = place_rows(at, own_parts, other_parts)
-    full_w_in = place_weight(at, in_parts)
-    full_w_out = place_weight(at, out_parts)
-
-    wide_f32 = wide_pooled.astype(f32)
-    inv_rms = lax.rsqrt(jnp.mean(wide_f32 * wide_f32, axis=1) + epsilon)
-    normed = (wide_f32 * inv_rms[:, None]).astype(bf16)
-    pre_act = jnp.dot(normed, full_w_in, preferred_element_type=f32)
-    activation = gelu_tanh(pre_act).astype(bf16)
-    out_part = lax.dot_general(
-        wide_up, activation, (((0,), (0,)), ((), ())), preferred_element_type=f32
-    )
-    out_pieces = out_part.astype(bf16).reshape(NY, NZ * NC, 32, hidden).swapaxes(0, 1)
-    out_rows = exchange(out_pieces.reshape(NZ * NC, NY * 32, hidden), ZC_GROUPS)
+    rows_all, depth = 2 * CAP, width // NY
+    normed, wide_up, wide_rms = call(
+        norm_kernel,
+        at,
+        [own_parts, other_parts],
+        [],
+        [((rows_all, width), bf16), ((rows_all, width), bf16), ((rows_all, 128), f32)],
+        [((rows_all, width), bf16)],
+        16,
+        16,
+        0,
+    )
+    product = 2 * rows_all * width * hidden
+    full_w_in, pre_act, out_pieces = call(
+        act_kernel,
+        at,
+        in_parts,
+        [normed, wide_up],
+        [
+            ((NY, depth, hidden), bf16),
+            ((rows_all, hidden), f32),
+            ((NZ * NC, NY * 32, hidden), bf16),
+        ],
+        [((rows_all, hidden), bf16)],
+        4,
+        24,
+        2 * product,
+    )
+    out_rows = exchange(out_pieces, ZC_GROUPS)
     out_rows = jnp.sum(out_rows.astype(f32).reshape(NZ, NC, NY, 32, hidden), axis=0)
     grad_out = reduce_by_y(out_rows.swapaxes(0, 1), y_idx)
-    up_proj = jnp.dot(wide_up, full_w_out, preferred_element_type=f32)
-    act_grad = jax.vjp(gelu_tanh, pre_act)[1](up_proj)[0].astype(bf16)
-    stat_part = jnp.sum(act_grad.astype(f32) * pre_act, axis=1) / inv_rms
-    in_part = lax.dot_general(
-        normed, act_grad, (((0,), (0,)), ((), ())), preferred_element_type=f32
-    ).astype(bf16)
-    in_rows = reduce_by_y(in_part.reshape(NY, NZ * NC * 32, hidden), y_idx)
+    *in_pieces, own_part, sent, own_stat = call(
+        grad_kernel,
+        at,
+        out_parts,
+        [normed, wide_up, full_w_in, pre_act, wide_rms],
+        [((depth, hidden), bf16)] * NY
+        + [((CAP, width), f32), ((CAP, width + 128), bf16), ((CAP, 128), f32)],
+        [
+            ((NY, depth, hidden), bf16),
+            ((rows_all, hidden), f32),
+            ((rows_all, hidden), bf16),
+            ((rows_all, 128), f32),
+        ],
+        4,
+        32,
+        3 * product,
+    )
+    in_rows = reduce_sent(in_pieces[0], in_pieces[1:])
     in_rows = exchange(in_rows.astype(bf16).reshape(NZ * NC, 32, hidden), ZC_GROUPS)
     grad_in = jnp.sum(in_rows.astype(f32).reshape(NZ, NC, 32, hidden), axis=0)
 
-    normed_part = lax.dot_general(
-        act_grad, full_w_in, (((1,), (1,)), ((), ())), preferred_element_type=f32
-    )
-    stat_high = stat_part.astype(bf16)
-    stat_low = (stat_part - stat_high.astype(f32)).astype(bf16)
-    lane = jnp.arange(128)[None, :]
-    stat_cols = jnp.where(lane == 0, stat_high[:, None], stat_low[:, None])
-    stat_cols = jnp.where(lane < 2, stat_cols, jnp.zeros((), bf16))
-    sent = jnp.concatenate([normed_part[CAP:].astype(bf16), stat_cols[CAP:]], axis=1)
     got = swap_cores(sent)
     got = got.astype(f32)
-    chip_part = normed_part[:CAP] + got[:, :width]
-    chip_stat = stat_part[:CAP] + got[:, width] + got[:, width + 1]
+    chip_part = own_part + got[:, :width]
+    chip_stat = own_stat[:, 0] + got[:, width] + got[:, width + 1]
+    lane = jnp.arange(128)[None, :]
     stat_high = chip_stat.astype(bf16)
     stat_low = (chip_stat - stat_high.astype(f32)).astype(bf16)
     stat_cols = jnp.where(lane == 0, stat_high[:, None], stat_low[:, None])
@@ -233,7 +349,7 @@
         normed_grad = normed_grad + got[:, :quarter]
         row_stat = row_stat + got[:, quarter] + got[:, quarter + 1]
     row_stat = row_stat / width
-    own_rms = inv_rms[:CAP]
+    own_rms = wide_rms[:CAP, 0]
     pooled_grad = (
         up_grad.astype(f32)
         + own_rms[:, None] * normed_grad

time: 248 us -> 223 us (0.90)
  blocking collectives: 0 us -> 22.6 us
  other arithmetic: 23.1 us -> 11.5 us
  matrix products: 12.6 us -> 1.82 us
  local copies, waits for them, and re-layouts: 17.6 us -> 7.01 us
  starting transfers between devices: 68.7 us -> 58.2 us
  waiting for transfers between devices: 107 us -> 98.9 us
  Pallas kernels: 12.1 us -> 16.2 us
    all_to_all x0 -> x1, blocking collectives: none -> 22.6 us  [exchange(): lax.all_to_all(value, 'seq', 0, 0, axis_index_groups=groups, tiled=True)]
    dot_general x5 -> x0, matrix products: 10.9 us -> none  [the longest x1 2.97 us: local(): lax.dot_general(act_grad, full_w_in, (((1,), (1,)), ((), ())), preferred_...]
    all_to_all x4 -> x3, starting transfers between devices: 27.4 us -> 18.9 us  [exchange(): lax.all_to_all(value, 'seq', 0, 0, axis_index_groups=groups, tiled=True)]
    ppermute x6, waiting for transfers between devices: 29.7 us -> 21.9 us  [send_x(): return lax.ppermute(value, 'mp', [(i, (i + step) % NX) for i in range(NX)])]
    unnamed x76 -> x28, local copies, waits for them, and re-layouts: 4.58 us -> 0.25 us
    pallas_call x3, Pallas kernels: 12.1 us -> 16.2 us  [call(): pl.pallas_call(kernel, out_shape=tuple(outs), in_specs=[pl.BlockSpec(memo...]
    ppermute x12, starting transfers between devices: 27.8 us -> 23.9 us  [send_y(): return lax.ppermute(value, 'seq', y_pairs(step))]
    slice x7 -> x0, local copies, waits for them, and re-layouts: 2.71 us -> none  [the longest x1 1.77 us: local(): normed_part[CAP:].astype(bf16)]
  transfers between devices with their start and end apart: 26 -> 25, of which waited for: 18 -> 20; matrix products, arithmetic and copies ran while one was open for 13% -> 5% of each run, Pallas kernels for 3% -> 4%
where the time goes in v2:
time: 223 us; the launch traced here: 219 us
  waiting for transfers between devices  98.9 us (44%)
  starting transfers between devices  58.2 us (26%)
  blocking collectives  22.6 us (10%)
  Pallas kernels  16.2 us (7%)
  other arithmetic  11.5 us (5%)
  local copies, waits for them, and re-layouts  7.01 us (3%)
  between operations  3.02 us (1%)
    ppermute x12, waiting for transfers between devices, send_y(): return lax.ppermute(value, 'seq', y_pairs(step))  42.2 us
    all_to_all x3, waiting for transfers between devices, exchange(): lax.all_to_all(value, 'seq', 0, 0, axis_index_groups=groups, tiled=True)  33.1 us
    ppermute x12, starting transfers between devices, send_y(): return lax.ppermute(value, 'seq', y_pairs(step))  23.9 us
    all_to_all x1, blocking collectives, exchange(): lax.all_to_all(value, 'seq', 0, 0, axis_index_groups=groups, tiled=True)  22.6 us
    ppermute x6, waiting for transfers between devices, send_x(): return lax.ppermute(value, 'mp', [(i, (i + step) % NX) for i in range(NX)])  21.9 us
    all_to_all x3, starting transfers between devices, exchange(): lax.all_to_all(value, 'seq', 0, 0, axis_index_groups=groups, tiled=True)  18.9 us
    pallas_call x3, Pallas kernels, call(): pl.pallas_call(kernel, out_shape=tuple(outs), in_specs=[pl.BlockSpec(memo...  16.2 us
    ppermute x6, starting transfers between devices, send_x(): return lax.ppermute(value, 'mp', [(i, (i + step) % NX) for i in range(NX)])  9.77 us
  transfers between devices with their start and end apart: 25, of which 20 were waited for; matrix products, arithmetic and copies ran while one was open for 5% of the time, Pallas kernels for 4%

profile of v2, /device:TPU:2, one launch (start us, length us, event | category | flops | bytes accessed | tf_op | source)
XLA Modules:
  0.0 219.2 jit_solution(13984422887166769032)
XLA Ops:
  10.1 2.3 %collective-permute-start.2 = (bf16[2,224,512]{2,1,0:T(8,128)(2,1)S(1)}, bf16[2,224,512]{2,1,0:T(8,128)(2,1)}, u32[]{:S(2)}, u32[]{:S(2)}) collective-permute-start(bf16[2,224,512]{2,1,0:T(8,128)(2,1)S(1)} %get-tuple-element.43), channel_id=1, source_target_pairs={{0,3},{1,0},{2,1},{3,2},{4,7},{5,4},{6,5},{7,6},{8,11},{9,8},{10,9... | collective-permute-start | bytes 1376264 | tf_op jit(solution)/shard_map/ppermute | solution.py:48
  15.9 9.8 %all-to-all-start.1 = ((bf16[16,32,512]{2,1,0:T(8,128)(2,1)}), bf16[16,32,512]{2,1,0:T(8,128)(2,1)S(1)}, u32[]{:S(2)}, u32[]{:S(2)}) async-start(bf16[16,32,512]{2,1,0:T(8,128)(2,1)} %bitcast.18), calls=%async_computation.1 | async-start | bytes 1048576 | tf_op jit(solution)/shard_map/all_to_all | solution.py:52
  25.7 7.5 %collective-permute-done.3 = bf16[2,224,512]{2,1,0:T(8,128)(2,1)} collective-permute-done((bf16[2,224,512]{2,1,0:T(8,128)(2,1)S(1)}, bf16[2,224,512]{2,1,0:T(8,128)(2,1)}, u32[]{:S(2)}, u32[]{:S(2)}) %collective-permute-start.3) | collective-permute-done | bytes 458784 | tf_op jit(solution)/shard_map/ppermute | solution.py:48
  37.4 4.3 %all-to-all-done.1 = bf16[16,32,512]{2,1,0:T(8,128)(2,1)S(1)} async-done(((bf16[16,32,512]{2,1,0:T(8,128)(2,1)}), bf16[16,32,512]{2,1,0:T(8,128)(2,1)S(1)}, u32[]{:S(2)}, u32[]{:S(2)}) %all-to-all-start.1) | async-done | bytes 524320 | tf_op jit(solution)/shard_map/all_to_all | solution.py:52
  42.5 4.5 %all-to-all-start = ((bf16[16,32,512]{2,1,0:T(8,128)(2,1)}), bf16[16,32,512]{2,1,0:T(8,128)(2,1)S(1)}, u32[]{:S(2)}, u32[]{:S(2)}) async-start(bf16[16,32,512]{2,1,0:T(8,128)(2,1)} %bitcast.78), calls=%async_computation | async-start | bytes 1048576 | tf_op jit(solution)/shard_map/all_to_all | solution.py:52
  47.0 3.3 %collective-permute-start.10 = (bf16[512,512]{1,0:T(8,128)(2,1)S(1)}, bf16[512,512]{1,0:T(8,128)(2,1)}, u32[]{:S(2)}, u32[]{:S(2)}) collective-permute-start(bf16[512,512]{1,0:T(8,128)(2,1)S(1)} %bitcast.68), channel_id=1, source_target_pairs={{0,128},{4,132},{8,136},{12,140},{16,144},{20,148},{24,152},{28,15... | collective-permute-start | bytes 1572872 | tf_op jit(solution)/shard_map/ppermute | solution.py:44
  51.0 2.6 %collective-permute-start.9 = (bf16[512,512]{1,0:T(8,128)(2,1)S(1)}, bf16[512,512]{1,0:T(8,128)(2,1)}, u32[]{:S(2)}, u32[]{:S(2)}) collective-permute-start(bf16[512,512]{1,0:T(8,128)(2,1)S(1)} %bitcast.70), channel_id=1, source_target_pairs={{0,192},{4,196},{8,200},{12,204},{16,208},{20,212},{24,216},{28,22... | collective-permute-start | bytes 1572872 | tf_op jit(solution)/shard_map/ppermute | solution.py:44
  53.5 9.6 %all-to-all-done = bf16[16,32,512]{2,1,0:T(8,128)(2,1)S(1)} async-done(((bf16[16,32,512]{2,1,0:T(8,128)(2,1)}), bf16[16,32,512]{2,1,0:T(8,128)(2,1)S(1)}, u32[]{:S(2)}, u32[]{:S(2)}) %all-to-all-start) | async-done | bytes 524320 | tf_op jit(solution)/shard_map/all_to_all | solution.py:52
  68.4 3.5 %shard_map.76 = (bf16[448,2048]{1,0:T(8,128)(2,1)S(1)}, bf16[448,2048]{1,0:T(8,128)(2,1)S(1)}, f32[448,128]{1,0:T(8,128)S(1)}) custom-call(s32[2]{0:T(128)S(1)} %pad_add_fusion.at_ref, bf16[4,2,224,512]{3,2,1,0:T(8,128)(2,1)S(1)} %pad_maximum_fusion.own_ref, bf16[4,2,224,512]{3,2,1,0:T(8,128)(2,1)} %collective-permute-done.4.other_ref), custom_call_target="tpu_custom_call" | custom-call | bytes 7569408 | tf_op jit(solution)/shard_map/pallas_call | solution.py:207
  71.9 2.5 %collective-permute-done.8.refs_1_ = bf16[512,512]{1,0:T(8,128)(2,1)} collective-permute-done((bf16[512,512]{1,0:T(8,128)(2,1)S(1)}, bf16[512,512]{1,0:T(8,128)(2,1)}, u32[]{:S(2)}, u32[]{:S(2)}) %collective-permute-start.8) | collective-permute-done | bytes 524320 | tf_op jit(solution)/shard_map/ppermute | solution.py:44
  75.1 6.1 %shard_map.77 = (bf16[4,512,512]{2,1,0:T(8,128)(2,1)S(1)}, f32[448,512]{1,0:T(8,128)S(1)}, bf16[16,128,512]{2,1,0:T(8,128)(2,1)}) custom-call(s32[2]{0:T(128)S(1)} %pad_add_fusion.at_ref, bf16[512,512]{1,0:T(8,128)(2,1)S(1)} %bitcast.71, bf16[512,512]{1,0:T(8,128)(2,1)} %collective-permute-done.8.refs_1_, bf16[512,512]{1,0:T(8,128)(2,1)} %collective-permute-done.9.refs_2_, ...), custom_call_target="tpu_custom_call" | custom-call | flops 1879048192 | bytes 10878976 | tf_op jit(solution)/shard_map/pallas_call | solution.py:207
  81.2 4.7 %collective-permute-done.5.refs_1_ = bf16[512,512]{1,0:T(8,128)(2,1)} collective-permute-done((bf16[512,512]{1,0:T(8,128)(2,1)S(1)}, bf16[512,512]{1,0:T(8,128)(2,1)}, u32[]{:S(2)}, u32[]{:S(2)}) %collective-permute-start.5) | collective-permute-done | bytes 524320 | tf_op jit(solution)/shard_map/ppermute | solution.py:44
  86.3 10.6 %collective-permute-done.7.refs_3_ = bf16[512,512]{1,0:T(8,128)(2,1)} collective-permute-done((bf16[512,512]{1,0:T(8,128)(2,1)S(1)}, bf16[512,512]{1,0:T(8,128)(2,1)}, u32[]{:S(2)}, u32[]{:S(2)}) %collective-permute-start.7) | collective-permute-done | bytes 524320 | tf_op jit(solution)/shard_map/ppermute | solution.py:44
  96.9 6.6 %shard_map.78 = (bf16[512,512]{1,0:T(8,128)(2,1)S(1)}, bf16[512,512]{1,0:T(8,128)(2,1)S(1)}, bf16[512,512]{1,0:T(8,128)(2,1)S(1)}, bf16[512,512]{1,0:T(8,128)(2,...) custom-call(s32[2]{0:T(128)S(1)} %pad_add_fusion.at_ref, ...), custom_call_target="tpu_custom_call" | custom-call | flops 2818572288 | bytes 14032896 | tf_op jit(solution)/shard_map/pallas_call | solution.py:207
  108.9 10.5 %collective-permute-done.16 = bf16[512,512]{1,0:T(8,128)(2,1)S(1)} collective-permute-done((bf16[512,512]{1,0:T(8,128)(2,1)S(1)}, bf16[512,512]{1,0:T(8,128)(2,1)S(1)}, u32[]{:S(2)}, u32[]{:S(2)}) %collective-permute-start.16) | collective-permute-done | bytes 524320 | tf_op jit(solution)/shard_map/ppermute | solution.py:44
  120.0 10.3 %collective-permute-done.18 = bf16[512,512]{1,0:T(8,128)(2,1)S(1)} collective-permute-done((bf16[512,512]{1,0:T(8,128)(2,1)S(1)}, bf16[512,512]{1,0:T(8,128)(2,1)S(1)}, u32[]{:S(2)}, u32[]{:S(2)}) %collective-permute-start.18) | collective-permute-done | bytes 524320 | tf_op jit(solution)/shard_map/ppermute | solution.py:44
  130.6 22.6 %all_to_all.20 = bf16[16,32,512]{2,1,0:T(8,128)(2,1)} all-to-all(bf16[16,32,512]{2,1,0:T(8,128)(2,1)S(1)} %bitcast.76), channel_id=1, replica_groups={{0,4,8,12,16,20,24,28,32,36,40,44,48,52,56,60},{64,68,72,76,80,84,88,92..., dimensions={0} | all-to-all | bytes 1048576 | tf_op jit(solution)/shard_map/all_to_all | solution.py:52
  153.1 4.6 %all-to-all-start.3 = ((bf16[16,128,512]{2,1,0:T(8,128)(2,1)}), bf16[16,128,512]{2,1,0:T(8,128)(2,1)}, u32[]{:S(2)}, u32[]{:S(2)}) async-start(bf16[16,128,512]{2,1,0:T(8,128)(2,1)} %get-tuple-element.28), calls=%async_computation.3 | async-start | bytes 4194304 | tf_op jit(solution)/shard_map/all_to_all | solution.py:52
  169.0 5.6 %collective-permute-done.12 = bf16[224,640]{1,0:T(8,128)(2,1)S(1)} collective-permute-done((bf16[224,640]{1,0:T(8,128)(2,1)S(1)}, bf16[224,640]{1,0:T(8,128)(2,1)S(1)}, u32[]{:S(2)}, u32[]{:S(2)}) %collective-permute-start.12) | collective-permute-done | bytes 286752 | tf_op jit(solution)/shard_map/ppermute | solution.py:48
  174.7 7.4 %collective-permute-done.14 = bf16[224,640]{1,0:T(8,128)(2,1)S(1)} collective-permute-done((bf16[224,640]{1,0:T(8,128)(2,1)S(1)}, bf16[224,640]{1,0:T(8,128)(2,1)S(1)}, u32[]{:S(2)}, u32[]{:S(2)}) %collective-permute-start.14) | collective-permute-done | bytes 286752 | tf_op jit(solution)/shard_map/ppermute | solution.py:48
  187.7 19.3 %all-to-all-done.3 = bf16[16,128,512]{2,1,0:T(8,128)(2,1)} async-done(((bf16[16,128,512]{2,1,0:T(8,128)(2,1)}), bf16[16,128,512]{2,1,0:T(8,128)(2,1)}, u32[]{:S(2)}, u32[]{:S(2)}) %all-to-all-start.3) | async-done | bytes 2097184 | tf_op jit(solution)/shard_map/all_to_all | solution.py:52
  207.0 2.0 convert_reduce_fusion
  209.1 3.6 %collective-permute-start.19 = (bf16[2,32,512]{2,1,0:T(8,128)(2,1)S(1)}, bf16[2,32,512]{2,1,0:T(8,128)(2,1)S(1)}, u32[]{:S(2)}, u32[]{:S(2)}) collective-permute-start(bf16[2,32,512]{2,1,0:T(8,128)(2,1)S(1)} %get-tuple-element.39), channel_id=1, source_target_pairs={{0,64},{4,68},{8,72},{12,76},{16,80},{20,84},{24,88},{28,92},{32,9... | collective-permute-start | bytes 196616 | tf_op jit(solution)/shard_map/ppermute | solution.py:44
  212.7 3.2 %collective-permute-start.21 = (bf16[2,32,512]{2,1,0:T(8,128)(2,1)S(1)}, bf16[2,32,512]{2,1,0:T(8,128)(2,1)S(1)}, u32[]{:S(2)}, u32[]{:S(2)}) collective-permute-start(bf16[2,32,512]{2,1,0:T(8,128)(2,1)S(1)} %get-tuple-element.41), channel_id=1, source_target_pairs={{0,128},{4,132},{8,136},{12,140},{16,144},{20,148},{24,152},{28,15... | collective-permute-start | bytes 196616 | tf_op jit(solution)/shard_map/ppermute | solution.py:44
  (108 shorter events, 49.2 us)
Async XLA Ops:
  5.0 3.1 %collective-permute-start = (f32[3,512]{1,0:T(4,128)S(1)}, f32[3,512]{1,0:T(4,128)S(1)}, u32[]{:S(2)}, u32[]{:S(2)}) collective-permute-start(f32[3,512]{1,0:T(4,128)S(1)} %maximum_maximum_fusion), channel_id=1, source_target_pairs={{4,0},{8,4},{12,8},{16,12},{20,16},{24,20},{28,24},{32,28},{36,32}... | collective-permute-start | bytes 18440 | tf_op jit(solution)/shard_map/ppermute | solution.py:265
  10.1 15.6 %collective-permute-start.2 = (bf16[2,224,512]{2,1,0:T(8,128)(2,1)S(1)}, bf16[2,224,512]{2,1,0:T(8,128)(2,1)}, u32[]{:S(2)}, u32[]{:S(2)}) collective-permute-start(bf16[2,224,512]{2,1,0:T(8,128)(2,1)S(1)} %get-tuple-element.43), channel_id=1, source_target_pairs={{0,3},{1,0},{2,1},{3,2},{4,7},{5,4},{6,5},{7,6},{8,11},{9,8},{10,9... | collective-permute-start | bytes 1376264 | tf_op jit(solution)/shard_map/ppermute | solution.py:48
  12.4 20.8 %collective-permute-start.3 = (bf16[2,224,512]{2,1,0:T(8,128)(2,1)S(1)}, bf16[2,224,512]{2,1,0:T(8,128)(2,1)}, u32[]{:S(2)}, u32[]{:S(2)}) collective-permute-start(bf16[2,224,512]{2,1,0:T(8,128)(2,1)S(1)} %get-tuple-element.43), channel_id=1, source_target_pairs={{0,2},{1,3},{2,0},{3,1},{4,6},{5,7},{6,4},{7,5},{8,10},{9,11},{10,... | collective-permute-start | bytes 1376264 | tf_op jit(solution)/shard_map/ppermute | solution.py:48
  13.2 21.5 %collective-permute-start.1 = (bf16[2,224,512]{2,1,0:T(8,128)(2,1)S(1)}, bf16[2,224,512]{2,1,0:T(8,128)(2,1)}, u32[]{:S(2)}, u32[]{:S(2)}) collective-permute-start(bf16[2,224,512]{2,1,0:T(8,128)(2,1)S(1)} %get-tuple-element.43), channel_id=1, source_target_pairs={{0,1},{1,2},{2,3},{3,0},{4,5},{5,6},{6,7},{7,4},{8,9},{9,10},{10,1... | collective-permute-start | bytes 1376264 | tf_op jit(solution)/shard_map/ppermute | solution.py:48
  15.9 25.8 %all-to-all-start.1 = ((bf16[16,32,512]{2,1,0:T(8,128)(2,1)}), bf16[16,32,512]{2,1,0:T(8,128)(2,1)S(1)}, u32[]{:S(2)}, u32[]{:S(2)}) async-start(bf16[16,32,512]{2,1,0:T(8,128)(2,1)} %bitcast.18), calls=%async_computation.1 | async-start | bytes 1048576 | tf_op jit(solution)/shard_map/all_to_all | solution.py:52
  36.2 30.3 %collective-permute-start.4 = (bf16[4,2,224,512]{3,2,1,0:T(8,128)(2,1)S(1)}, bf16[4,2,224,512]{3,2,1,0:T(8,128)(2,1)}, u32[]{:S(2)}, u32[]{:S(2)}) collective-permute-start(bf16[4,2,224,512]{3,2,1,0:T(8,128)(2,1)S(1)} %pad_maximum_fusion.own_ref), channel_id=1, source_target_pairs={{0,4},{4,0},{8,12},{12,8},{16,20},{20,16},{24,28},{28,24},{32,36},... | collective-permute-start | bytes 5505032 | tf_op jit(solution)/shard_map/ppermute | solution.py:40
  42.5 20.6 %all-to-all-start = ((bf16[16,32,512]{2,1,0:T(8,128)(2,1)}), bf16[16,32,512]{2,1,0:T(8,128)(2,1)S(1)}, u32[]{:S(2)}, u32[]{:S(2)}) async-start(bf16[16,32,512]{2,1,0:T(8,128)(2,1)} %bitcast.78), calls=%async_computation | async-start | bytes 1048576 | tf_op jit(solution)/shard_map/all_to_all | solution.py:52
  47.0 17.7 %collective-permute-start.10 = (bf16[512,512]{1,0:T(8,128)(2,1)S(1)}, bf16[512,512]{1,0:T(8,128)(2,1)}, u32[]{:S(2)}, u32[]{:S(2)}) collective-permute-start(bf16[512,512]{1,0:T(8,128)(2,1)S(1)} %bitcast.68), channel_id=1, source_target_pairs={{0,128},{4,132},{8,136},{12,140},{16,144},{20,148},{24,152},{28,15... | collective-permute-start | bytes 1572872 | tf_op jit(solution)/shard_map/ppermute | solution.py:44
  50.3 24.2 %collective-permute-start.8 = (bf16[512,512]{1,0:T(8,128)(2,1)S(1)}, bf16[512,512]{1,0:T(8,128)(2,1)}, u32[]{:S(2)}, u32[]{:S(2)}) collective-permute-start(bf16[512,512]{1,0:T(8,128)(2,1)S(1)} %bitcast.69), channel_id=1, source_target_pairs={{0,64},{4,68},{8,72},{12,76},{16,80},{20,84},{24,88},{28,92},{32,9... | collective-permute-start | bytes 1572872 | tf_op jit(solution)/shard_map/ppermute | solution.py:44
  51.0 24.2 %collective-permute-start.9 = (bf16[512,512]{1,0:T(8,128)(2,1)S(1)}, bf16[512,512]{1,0:T(8,128)(2,1)}, u32[]{:S(2)}, u32[]{:S(2)}) collective-permute-start(bf16[512,512]{1,0:T(8,128)(2,1)S(1)} %bitcast.70), channel_id=1, source_target_pairs={{0,192},{4,196},{8,200},{12,204},{16,208},{20,212},{24,216},{28,22... | collective-permute-start | bytes 1572872 | tf_op jit(solution)/shard_map/ppermute | solution.py:44
  63.1 22.8 %collective-permute-start.5 = (bf16[512,512]{1,0:T(8,128)(2,1)S(1)}, bf16[512,512]{1,0:T(8,128)(2,1)}, u32[]{:S(2)}, u32[]{:S(2)}) collective-permute-start(bf16[512,512]{1,0:T(8,128)(2,1)S(1)} %bitcast.72), channel_id=1, source_target_pairs={{0,64},{4,68},{8,72},{12,76},{16,80},{20,84},{24,88},{28,92},{32,9... | collective-permute-start | bytes 1572872 | tf_op jit(solution)/shard_map/ppermute | solution.py:44
  64.7 21.7 %collective-permute-start.6 = (bf16[512,512]{1,0:T(8,128)(2,1)S(1)}, bf16[512,512]{1,0:T(8,128)(2,1)}, u32[]{:S(2)}, u32[]{:S(2)}) collective-permute-start(bf16[512,512]{1,0:T(8,128)(2,1)S(1)} %bitcast.73), channel_id=1, source_target_pairs={{0,192},{4,196},{8,200},{12,204},{16,208},{20,212},{24,216},{28,22... | collective-permute-start | bytes 1572872 | tf_op jit(solution)/shard_map/ppermute | solution.py:44
  66.6 30.4 %collective-permute-start.7 = (bf16[512,512]{1,0:T(8,128)(2,1)S(1)}, bf16[512,512]{1,0:T(8,128)(2,1)}, u32[]{:S(2)}, u32[]{:S(2)}) collective-permute-start(bf16[512,512]{1,0:T(8,128)(2,1)S(1)} %bitcast.74), channel_id=1, source_target_pairs={{0,128},{4,132},{8,136},{12,140},{16,144},{20,148},{24,152},{28,15... | collective-permute-start | bytes 1572872 | tf_op jit(solution)/shard_map/ppermute | solution.py:44
  103.6 15.8 %collective-permute-start.16 = (bf16[512,512]{1,0:T(8,128)(2,1)S(1)}, bf16[512,512]{1,0:T(8,128)(2,1)S(1)}, u32[]{:S(2)}, u32[]{:S(2)}) collective-permute-start(bf16[512,512]{1,0:T(8,128)(2,1)S(1)} %get-tuple-element.25), channel_id=1, source_target_pairs={{0,64},{4,68},{8,72},{12,76},{16,80},{20,84},{24,88},{28,92},{32,9... | collective-permute-start | bytes 1572872 | tf_op jit(solution)/shard_map/ppermute | solution.py:44
  105.2 14.8 %collective-permute-start.17 = (bf16[512,512]{1,0:T(8,128)(2,1)S(1)}, bf16[512,512]{1,0:T(8,128)(2,1)S(1)}, u32[]{:S(2)}, u32[]{:S(2)}) collective-permute-start(bf16[512,512]{1,0:T(8,128)(2,1)S(1)} %get-tuple-element.26), channel_id=1, source_target_pairs={{0,192},{4,196},{8,200},{12,204},{16,208},{20,212},{24,216},{28,22... | collective-permute-start | bytes 1572872 | tf_op jit(solution)/shard_map/ppermute | solution.py:44
  106.9 23.4 %collective-permute-start.18 = (bf16[512,512]{1,0:T(8,128)(2,1)S(1)}, bf16[512,512]{1,0:T(8,128)(2,1)S(1)}, u32[]{:S(2)}, u32[]{:S(2)}) collective-permute-start(bf16[512,512]{1,0:T(8,128)(2,1)S(1)} %get-tuple-element.27), channel_id=1, source_target_pairs={{0,128},{4,132},{8,136},{12,140},{16,144},{20,148},{24,152},{28,15... | collective-permute-start | bytes 1572872 | tf_op jit(solution)/shard_map/ppermute | solution.py:44
  153.1 53.8 %all-to-all-start.3 = ((bf16[16,128,512]{2,1,0:T(8,128)(2,1)}), bf16[16,128,512]{2,1,0:T(8,128)(2,1)}, u32[]{:S(2)}, u32[]{:S(2)}) async-start(bf16[16,128,512]{2,1,0:T(8,128)(2,1)} %get-tuple-element.28), calls=%async_computation.3 | async-start | bytes 4194304 | tf_op jit(solution)/shard_map/all_to_all | solution.py:52
  157.7 4.1 %collective-permute-start.11 = (bf16[224,2176]{1,0:T(8,128)(2,1)S(1)}, bf16[224,2176]{1,0:T(8,128)(2,1)}, u32[]{:S(2)}, u32[]{:S(2)}) collective-permute-start(bf16[224,2176]{1,0:T(8,128)(2,1)S(1)} %copy-done.4), channel_id=1, source_target_pairs={{0,4},{4,0},{8,12},{12,8},{16,20},{20,16},{24,28},{28,24},{32,36},... | collective-permute-start | bytes 2924552 | tf_op jit(solution)/shard_map/ppermute | solution.py:40
  164.0 10.5 %collective-permute-start.12 = (bf16[224,640]{1,0:T(8,128)(2,1)S(1)}, bf16[224,640]{1,0:T(8,128)(2,1)S(1)}, u32[]{:S(2)}, u32[]{:S(2)}) collective-permute-start(bf16[224,640]{1,0:T(8,128)(2,1)S(1)} %get-tuple-element.44), channel_id=1, source_target_pairs={{0,1},{1,2},{2,3},{3,0},{4,5},{5,6},{6,7},{7,4},{8,9},{9,10},{10,1... | collective-permute-start | bytes 860168 | tf_op jit(solution)/shard_map/ppermute | solution.py:48
  165.7 9.0 %collective-permute-start.13 = (bf16[224,640]{1,0:T(8,128)(2,1)S(1)}, bf16[224,640]{1,0:T(8,128)(2,1)S(1)}, u32[]{:S(2)}, u32[]{:S(2)}) collective-permute-start(bf16[224,640]{1,0:T(8,128)(2,1)S(1)} %get-tuple-element.45), channel_id=1, source_target_pairs={{0,3},{1,0},{2,1},{3,2},{4,7},{5,4},{6,5},{7,6},{8,11},{9,8},{10,9... | collective-permute-start | bytes 860168 | tf_op jit(solution)/shard_map/ppermute | solution.py:48
  167.0 15.1 %collective-permute-start.14 = (bf16[224,640]{1,0:T(8,128)(2,1)S(1)}, bf16[224,640]{1,0:T(8,128)(2,1)S(1)}, u32[]{:S(2)}, u32[]{:S(2)}) collective-permute-start(bf16[224,640]{1,0:T(8,128)(2,1)S(1)} %get-tuple-element.46), channel_id=1, source_target_pairs={{0,2},{1,3},{2,0},{3,1},{4,6},{5,7},{6,4},{7,5},{8,10},{9,11},{10,... | collective-permute-start | bytes 860168 | tf_op jit(solution)/shard_map/ppermute | solution.py:48
  209.1 7.5 %collective-permute-start.19 = (bf16[2,32,512]{2,1,0:T(8,128)(2,1)S(1)}, bf16[2,32,512]{2,1,0:T(8,128)(2,1)S(1)}, u32[]{:S(2)}, u32[]{:S(2)}) collective-permute-start(bf16[2,32,512]{2,1,0:T(8,128)(2,1)S(1)} %get-tuple-element.39), channel_id=1, source_target_pairs={{0,64},{4,68},{8,72},{12,76},{16,80},{20,84},{24,88},{28,92},{32,9... | collective-permute-start | bytes 196616 | tf_op jit(solution)/shard_map/ppermute | solution.py:44
  212.7 4.3 %collective-permute-start.20 = (bf16[2,32,512]{2,1,0:T(8,128)(2,1)S(1)}, bf16[2,32,512]{2,1,0:T(8,128)(2,1)S(1)}, u32[]{:S(2)}, u32[]{:S(2)}) collective-permute-start(bf16[2,32,512]{2,1,0:T(8,128)(2,1)S(1)} %get-tuple-element.40), channel_id=1, source_target_pairs={{0,192},{4,196},{8,200},{12,204},{16,208},{20,212},{24,216},{28,22... | collective-permute-start | bytes 196616 | tf_op jit(solution)/shard_map/ppermute | solution.py:44
  212.7 5.8 %collective-permute-start.21 = (bf16[2,32,512]{2,1,0:T(8,128)(2,1)S(1)}, bf16[2,32,512]{2,1,0:T(8,128)(2,1)S(1)}, u32[]{:S(2)}, u32[]{:S(2)}) collective-permute-start(bf16[2,32,512]{2,1,0:T(8,128)(2,1)S(1)} %get-tuple-element.41), channel_id=1, source_target_pairs={{0,128},{4,132},{8,136},{12,140},{16,144},{20,148},{24,152},{28,15... | collective-permute-start | bytes 196616 | tf_op jit(solution)/shard_map/ppermute | solution.py:44
  (15 other events, 175.9 us)

commit v3 on v2

--- a/solution.py
+++ b/solution.py
@@ -66,29 +66,40 @@
 
 STEPS = (0, 1, 3, 2)
 CHUNK = 64
-MIB = 1 << 20
-
-
-def copies_of(pairs, sems):
+
+
+class Copies:
+    def __init__(self, sems):
+        self.sems, self.used = sems, 0
+
+    def start(self, pairs):
+        started = []
+        for source, target in pairs:
+            started.append(pltpu.make_async_copy(source, target, self.sems.at[self.used]))
+            self.used += 1
+            started[-1].start()
+        return started
+
+
+def wait(copies):
+    for item in copies:
+        item.wait()
+
+
+def weight_pairs(at_ref, parts, full_ref):
     return [
-        pltpu.make_async_copy(source, target, sems.at[n])
-        for n, (source, target) in enumerate(pairs)
+        (part, full_ref.at[lax.rem(at_ref[1] + NY - step, NY)])
+        for part, step in zip(parts, STEPS)
     ]
 
 
-def weight_copies(at_ref, parts, full_ref, sems):
-    return copies_of(
-        [
-            (part, full_ref.at[lax.rem(at_ref[1] + NY - step, NY)])
-            for part, step in zip(parts, STEPS)
-        ],
-        sems,
-    )
-
-
-def norm_kernel(at_ref, own_ref, other_ref, normed_ref, up_ref, rms_ref, pooled_ref, sems):
+def norm_kernel(
+    at_ref, own_ref, other_ref, normed_out, up_out, rms_out,
+    pooled_ref, normed_ref, up_ref, rms_ref, sems,
+):
+    move = Copies(sems)
     rows, quarter = own_ref.shape[2:]
-    pairs = []
+    places = []
     for half, part in enumerate((own_ref, other_ref)):
         for n, step in enumerate(STEPS):
             x = lax.rem(at_ref[0] + NX - step, NX)
@@ -96,13 +107,10 @@
                 pl.ds(half * rows, rows),
                 pl.ds(pl.multiple_of(x * quarter, quarter), quarter),
             )
-            pairs.append((part.at[n, 0], pooled_ref.at[where]))
-            pairs.append((part.at[n, 1], up_ref.at[where]))
-    copies = copies_of(pairs, sems)
-    for item in copies:
-        item.start()
-    for item in copies:
-        item.wait()
+            places.append((part.at[n], where))
+    pooled = move.start([(part.at[0], pooled_ref.at[where]) for part, where in places])
+    ups = move.start([(part.at[1], up_ref.at[where]) for part, where in places])
+    wait(pooled)
 
     def norm_rows(i, carry):
         at = pl.ds(pl.multiple_of(i * CHUNK, CHUNK), CHUNK)
@@ -113,20 +121,24 @@
         return carry
 
     lax.fori_loop(0, pooled_ref.shape[0] // CHUNK, norm_rows, 0)
+    gone = move.start([(normed_ref, normed_out), (rms_ref, rms_out)])
+    wait(ups)
+    wait(gone + move.start([(up_ref, up_out)]))
 
 
 def act_kernel(at_ref, *refs):
-    parts, (normed_ref, up_ref, w_in_ref, pre_ref, out_ref, act_ref, sems) = refs[:4], refs[4:]
-    copies = weight_copies(at_ref, parts, w_in_ref, sems)
-    for item in copies:
-        item.start()
-    for item in copies:
-        item.wait()
+    parts, (normed_in, up_in, pre_out, out_out), refs = refs[:4], refs[4:8], refs[8:]
+    normed_ref, up_ref, w_in_ref, pre_ref, act_ref, out_ref, sems = refs
+    move = Copies(sems)
+    first = move.start([(normed_in, normed_ref)] + weight_pairs(at_ref, parts, w_in_ref))
+    second = move.start([(up_in, up_ref)])
+    wait(first)
     rows, width = normed_ref.shape
     depth, hidden = w_in_ref.shape[1:]
     for n in range(0, hidden, 256):
         weight = w_in_ref[:, :, n : n + 256].reshape(width, 256)
         pre_ref[:, n : n + 256] = jnp.dot(normed_ref[...], weight, preferred_element_type=f32)
+    gone = move.start([(pre_ref, pre_out)])
 
     def act_rows(i, carry):
         at = pl.ds(pl.multiple_of(i * CHUNK, CHUNK), CHUNK)
@@ -134,6 +146,7 @@
         return carry
 
     lax.fori_loop(0, rows // CHUNK, act_rows, 0)
+    wait(second)
     for y in range(NY):
         part = lax.dot_general(
             up_ref[:, y * depth : (y + 1) * depth],
@@ -141,7 +154,9 @@
             (((0,), (0,)), ((), ())),
             preferred_element_type=f32,
         ).astype(bf16)
-        out_ref[:, y * 32 : (y + 1) * 32, :] = part.reshape(NZ * NC, 32, hidden)
+        out_ref[y] = part.reshape(NZ * NC, 32, hidden)
+        gone += move.start([(out_ref.at[y], out_out.at[:, pl.ds(y * 32, 32), :])])
+    wait(gone)
 
 
 GELU_K = math.sqrt(2.0 / math.pi)
@@ -155,21 +170,24 @@
 
 
 def grad_kernel(at_ref, *refs):
-    parts, refs = refs[:4], refs[4:]
-    normed_ref, up_ref, w_in_ref, pre_ref, rms_ref = refs[:5]
-    in_refs, (own_ref, sent_ref, stat_ref) = refs[5:9], refs[9:12]
-    w_out_ref, proj_ref, grad_ref, row_ref, sems = refs[12:]
-    copies = weight_copies(at_ref, parts, w_out_ref, sems)
-    for item in copies:
-        item.start()
-    for item in copies:
-        item.wait()
+    out_parts, in_parts, refs = refs[:4], refs[4:8], refs[8:]
+    normed_in, up_in, pre_in, rms_in = refs[:4]
+    in_outs, (own_out, sent_out, stat_ref), refs = refs[4:8], refs[8:11], refs[11:]
+    normed_ref, up_ref, pre_ref, rms_ref, w_out_ref, w_in_ref = refs[:6]
+    proj_ref, grad_ref, row_ref, in_ref, own_ref, sent_ref, sems = refs[6:]
+    move = Copies(sems)
+    first = move.start([(up_in, up_ref)] + weight_pairs(at_ref, out_parts, w_out_ref))
+    second = move.start([(pre_in, pre_ref), (rms_in, rms_ref)])
+    third = move.start([(normed_in, normed_ref)])
+    fourth = move.start(weight_pairs(at_ref, in_parts, w_in_ref))
+    wait(first)
     rows, width = normed_ref.shape
     depth, hidden = w_in_ref.shape[1:]
     half = rows // 2
     for n in range(0, hidden, 256):
         weight = w_out_ref[:, :, n : n + 256].reshape(width, 256)
         proj_ref[:, n : n + 256] = jnp.dot(up_ref[...], weight, preferred_element_type=f32)
+    wait(second)
 
     def grad_rows(i, carry):
         at = pl.ds(pl.multiple_of(i * CHUNK, CHUNK), CHUNK)
@@ -181,12 +199,16 @@
         return carry
 
     lax.fori_loop(0, rows // CHUNK, grad_rows, 0)
-    for step, in_ref in zip(STEPS, in_refs):
+    wait(third)
+    gone = []
+    for n, step in enumerate(STEPS):
         y = lax.rem(at_ref[1] + step, NY)
         block = normed_ref[:, pl.ds(pl.multiple_of(y * depth, depth), depth)]
-        in_ref[...] = lax.dot_general(
+        in_ref[n] = lax.dot_general(
             block, grad_ref[...], (((0,), (0,)), ((), ())), preferred_element_type=f32
         ).astype(bf16)
+        gone += move.start([(in_ref.at[n], in_outs[n])])
+    wait(fourth)
     for n in range(NY):
         part = lax.dot_general(
             grad_ref[...], w_in_ref[n], (((1,), (1,)), ((), ())), preferred_element_type=f32
@@ -199,23 +221,23 @@
     low = jnp.where(lane == 1, stat - high, 0.0)
     sent_ref[:, width:] = jnp.where(lane == 0, high, low).astype(bf16)
     stat_ref[...] = row_ref[:half, :]
-
-
-def call(kernel, at, far, near, outs, scratch, n_copies, limit, flops):
+    wait(gone + move.start([(own_ref, own_out), (sent_ref, sent_out)]))
+
+
+def call(kernel, at, far, outs, scratch, n_copies, flops, near=0):
     outs = [jax.ShapeDtypeStruct(shape, dtype) for shape, dtype in outs]
-    moved = sum(v.size * v.dtype.itemsize for v in [*far, *near, *outs])
+    moved = sum(v.size * v.dtype.itemsize for v in [*far, *outs])
     return pl.pallas_call(
         kernel,
         out_shape=tuple(outs),
         in_specs=[pl.BlockSpec(memory_space=pltpu.SMEM)]
-        + [pl.BlockSpec(memory_space=pl.ANY)] * len(far)
-        + [pl.BlockSpec(memory_space=pltpu.VMEM)] * len(near),
-        out_specs=(pl.BlockSpec(memory_space=pltpu.VMEM),) * len(outs),
+        + [pl.BlockSpec(memory_space=pl.ANY)] * len(far),
+        out_specs=(pl.BlockSpec(memory_space=pltpu.HBM),) * (len(outs) - near)
+        + (pl.BlockSpec(memory_space=pltpu.VMEM),) * near,
         scratch_shapes=[pltpu.VMEM(shape, dtype) for shape, dtype in scratch]
         + [pltpu.SemaphoreType.DMA((n_copies,))],
         cost_estimate=pl.CostEstimate(flops=flops, bytes_accessed=moved, transcendentals=0),
-        compiler_params=pltpu.CompilerParams(vmem_limit_bytes=limit * MIB),
-    )(at, *far, *near)
+    )(at, *far)
 
 
 def reduce_sent(own, pieces):
@@ -277,31 +299,25 @@
     other_parts = swap_cores(own_parts)
     at = jnp.stack([x_idx, y_idx]).astype(jnp.int32)
     rows_all, depth = 2 * CAP, width // NY
+    wide, thin = ((rows_all, width), bf16), ((rows_all, 128), f32)
+    square, weight = ((rows_all, hidden), f32), ((NY, depth, hidden), bf16)
     normed, wide_up, wide_rms = call(
         norm_kernel,
         at,
         [own_parts, other_parts],
-        [],
-        [((rows_all, width), bf16), ((rows_all, width), bf16), ((rows_all, 128), f32)],
-        [((rows_all, width), bf16)],
-        16,
-        16,
+        [wide, wide, thin],
+        [wide, wide, wide, thin],
+        19,
         0,
     )
     product = 2 * rows_all * width * hidden
-    full_w_in, pre_act, out_pieces = call(
+    pre_act, out_pieces = call(
         act_kernel,
         at,
-        in_parts,
-        [normed, wide_up],
-        [
-            ((NY, depth, hidden), bf16),
-            ((rows_all, hidden), f32),
-            ((NZ * NC, NY * 32, hidden), bf16),
-        ],
-        [((rows_all, hidden), bf16)],
-        4,
-        24,
+        [*in_parts, normed, wide_up],
+        [square, ((NZ * NC, NY * 32, hidden), bf16)],
+        [wide, wide, weight, square, ((rows_all, hidden), bf16), ((NY, NZ * NC, 32, hidden), bf16)],
+        11,
         2 * product,
     )
     out_rows = exchange(out_pieces, ZC_GROUPS)
@@ -310,19 +326,26 @@
     *in_pieces, own_part, sent, own_stat = call(
         grad_kernel,
         at,
-        out_parts,
-        [normed, wide_up, full_w_in, pre_act, wide_rms],
+        [*out_parts, *in_parts, normed, wide_up, pre_act, wide_rms],
         [((depth, hidden), bf16)] * NY
         + [((CAP, width), f32), ((CAP, width + 128), bf16), ((CAP, 128), f32)],
         [
-            ((NY, depth, hidden), bf16),
-            ((rows_all, hidden), f32),
+            wide,
+            wide,
+            square,
+            thin,
+            weight,
+            weight,
+            square,
             ((rows_all, hidden), bf16),
-            ((rows_all, 128), f32),
+            thin,
+            weight,
+            ((CAP, width), f32),
+            ((CAP, width + 128), bf16),
         ],
-        4,
-        32,
+        18,
         3 * product,
+        near=1,
     )
     in_rows = reduce_sent(in_pieces[0], in_pieces[1:])
     in_rows = exchange(in_rows.astype(bf16).reshape(NZ * NC, 32, hidden), ZC_GROUPS)

time: 223 us -> 230 us (1.031)
  waiting for transfers between devices: 98.9 us -> 92 us
  Pallas kernels: 16.2 us -> 21.7 us
  starting transfers between devices: 58.2 us -> 62.1 us
  other arithmetic: 11.5 us -> 15.2 us
    pallas_call x3, Pallas kernels: 16.2 us -> 21.7 us  [call(): pl.pallas_call(kernel, out_shape=tuple(outs), in_specs=[pl.BlockSpec(memo...]
    all_to_all x3, waiting for transfers between devices: 33.1 us -> 28.7 us  [exchange(): lax.all_to_all(value, 'seq', 0, 0, axis_index_groups=groups, tiled=True)]
    ppermute x12, starting transfers between devices: 23.9 us -> 26.9 us  [send_y(): return lax.ppermute(value, 'seq', y_pairs(step))]
  transfers between devices with their start and end apart: 25 -> 25, of which waited for: 20 -> 20; matrix products, arithmetic and copies ran while one was open for 5% -> 7% of each run, Pallas kernels for 4% -> 5%
where the time goes in v3:
time: 230 us; the launch traced here: 227 us
  waiting for transfers between devices  92 us (40%)
  starting transfers between devices  62.1 us (27%)
  blocking collectives  22.4 us (10%)
  Pallas kernels  21.7 us (9%)
  other arithmetic  15.2 us (7%)
  local copies, waits for them, and re-layouts  9.07 us (4%)
  between operations  2.89 us (1%)
    ppermute x12, waiting for transfers between devices, send_y(): return lax.ppermute(value, 'seq', y_pairs(step))  40.2 us
    all_to_all x3, waiting for transfers between devices, exchange(): lax.all_to_all(value, 'seq', 0, 0, axis_index_groups=groups, tiled=True)  28.7 us
    ppermute x12, starting transfers between devices, send_y(): return lax.ppermute(value, 'seq', y_pairs(step))  26.9 us
    all_to_all x1, blocking collectives, exchange(): lax.all_to_all(value, 'seq', 0, 0, axis_index_groups=groups, tiled=True)  22.4 us
    pallas_call x3, Pallas kernels, call(): pl.pallas_call(kernel, out_shape=tuple(outs), in_specs=[pl.BlockSpec(memo...  21.7 us
    ppermute x6, waiting for transfers between devices, send_x(): return lax.ppermute(value, 'mp', [(i, (i + step) % NX) for i in range(NX)])  21.4 us
    all_to_all x3, starting transfers between devices, exchange(): lax.all_to_all(value, 'seq', 0, 0, axis_index_groups=groups, tiled=True)  19.6 us
    ppermute x6, starting transfers between devices, send_x(): return lax.ppermute(value, 'mp', [(i, (i + step) % NX) for i in range(NX)])  9.84 us
  transfers between devices with their start and end apart: 25, of which 20 were waited for; matrix products, arithmetic and copies ran while one was open for 7% of the time, Pallas kernels for 5%

profile of v3, /device:TPU:2, one launch (start us, length us, event | category | flops | bytes accessed | tf_op | source)
XLA Modules:
  0.0 226.9 jit_solution(10136851047464490383)
XLA Ops:
  11.1 2.2 collective-permute-start.2
  16.8 9.9 %all-to-all-start.1 = ((bf16[16,32,512]{2,1,0:T(8,128)(2,1)}), bf16[16,32,512]{2,1,0:T(8,128)(2,1)}, u32[]{:S(2)}, u32[]{:S(2)}) async-start(bf16[16,32,512]{2,1,0:T(8,128)(2,1)} %bitcast.18), calls=%async_computation.1 | async-start | bytes 1048576 | tf_op jit(solution)/shard_map/all_to_all | solution.py:52
  26.8 7.4 %collective-permute-done.3 = bf16[2,224,512]{2,1,0:T(8,128)(2,1)S(1)} collective-permute-done((bf16[2,224,512]{2,1,0:T(8,128)(2,1)}, bf16[2,224,512]{2,1,0:T(8,128)(2,1)S(1)}, u32[]{:S(2)}, u32[]{:S(2)}) %collective-permute-start.3) | collective-permute-done | bytes 458784 | tf_op jit(solution)/shard_map/ppermute | solution.py:48
  39.4 3.4 %all-to-all-done.1 = bf16[16,32,512]{2,1,0:T(8,128)(2,1)} async-done(((bf16[16,32,512]{2,1,0:T(8,128)(2,1)}), bf16[16,32,512]{2,1,0:T(8,128)(2,1)}, u32[]{:S(2)}, u32[]{:S(2)}) %all-to-all-start.1) | async-done | bytes 524320 | tf_op jit(solution)/shard_map/all_to_all | solution.py:52
  43.6 5.4 %all-to-all-start = ((bf16[16,32,512]{2,1,0:T(8,128)(2,1)}), bf16[16,32,512]{2,1,0:T(8,128)(2,1)}, u32[]{:S(2)}, u32[]{:S(2)}) async-start(bf16[16,32,512]{2,1,0:T(8,128)(2,1)} %bitcast.71), calls=%async_computation | async-start | bytes 1048576 | tf_op jit(solution)/shard_map/all_to_all | solution.py:52
  49.0 3.3 %collective-permute-start.10 = (bf16[512,512]{1,0:T(8,128)(2,1)}, bf16[512,512]{1,0:T(8,128)(2,1)}, u32[]{:S(2)}, u32[]{:S(2)}) collective-permute-start(bf16[512,512]{1,0:T(8,128)(2,1)} %bitcast.19.refs_0_.refs_4_), channel_id=1, source_target_pairs={{0,128},{4,132},{8,136},{12,140},{16,144},{20,148},{24,152},{28,15... | collective-permute-start | bytes 1572872 | tf_op jit(solution)/shard_map/ppermute | solution.py:44
  53.0 2.6 %collective-permute-start.9 = (bf16[512,512]{1,0:T(8,128)(2,1)}, bf16[512,512]{1,0:T(8,128)(2,1)}, u32[]{:S(2)}, u32[]{:S(2)}) collective-permute-start(bf16[512,512]{1,0:T(8,128)(2,1)} %bitcast.19.refs_0_.refs_4_), channel_id=1, source_target_pairs={{0,192},{4,196},{8,200},{12,204},{16,208},{20,212},{24,216},{28,22... | collective-permute-start | bytes 1572872 | tf_op jit(solution)/shard_map/ppermute | solution.py:44
  55.6 9.5 %all-to-all-done = bf16[16,32,512]{2,1,0:T(8,128)(2,1)} async-done(((bf16[16,32,512]{2,1,0:T(8,128)(2,1)}), bf16[16,32,512]{2,1,0:T(8,128)(2,1)}, u32[]{:S(2)}, u32[]{:S(2)}) %all-to-all-start) | async-done | bytes 524320 | tf_op jit(solution)/shard_map/all_to_all | solution.py:52
  70.9 5.3 %shard_map.76 = (bf16[448,2048]{1,0:T(8,128)(2,1)}, bf16[448,2048]{1,0:T(8,128)(2,1)}, f32[448,128]{1,0:T(8,128)}) custom-call(s32[2]{0:T(128)} %pad_add_fusion.at_ref, bf16[4,2,224,512]{3,2,1,0:T(8,128)(2,1)} %copy-done.1, bf16[4,2,224,512]{3,2,1,0:T(8,128)(2,1)} %collective-permute-done.4.other_ref), custom_call_target="tpu_custom_call" | custom-call | bytes 7569408 | tf_op jit(solution)/shard_map/pallas_call | solution.py:230
  77.4 6.4 %shard_map.77 = (f32[448,512]{1,0:T(8,128)}, bf16[16,128,512]{2,1,0:T(8,128)(2,1)}) custom-call(s32[2]{0:T(128)} %pad_add_fusion.at_ref, bf16[512,512]{1,0:T(8,128)(2,1)} %bitcast.19.refs_0_.refs_4_, bf16[512,512]{1,0:T(8,128)(2,1)} %collective-permute-done.8.refs_1_.refs_5_, bf16[512,512]{1,0:T(8,128)(2,1)} %collective-permute-done.9.refs_2_.refs_6_, ...), custom_call_target="tpu_custom_call" | custom-call | flops 1879048192 | bytes 8781824 | tf_op jit(solution)/shard_map/pallas_call | solution.py:230
  83.8 4.4 %collective-permute-done.5.refs_1_ = bf16[512,512]{1,0:T(8,128)(2,1)} collective-permute-done((bf16[512,512]{1,0:T(8,128)(2,1)}, bf16[512,512]{1,0:T(8,128)(2,1)}, u32[]{:S(2)}, u32[]{:S(2)}) %collective-permute-start.5) | collective-permute-done | bytes 524320 | tf_op jit(solution)/shard_map/ppermute | solution.py:44
  88.6 10.3 %collective-permute-done.7.refs_3_ = bf16[512,512]{1,0:T(8,128)(2,1)} collective-permute-done((bf16[512,512]{1,0:T(8,128)(2,1)}, bf16[512,512]{1,0:T(8,128)(2,1)}, u32[]{:S(2)}, u32[]{:S(2)}) %collective-permute-start.7) | collective-permute-done | bytes 524320 | tf_op jit(solution)/shard_map/ppermute | solution.py:44
  98.9 9.9 %shard_map.78 = (bf16[512,512]{1,0:T(8,128)(2,1)}, bf16[512,512]{1,0:T(8,128)(2,1)}, bf16[512,512]{1,0:T(8,128)(2,1)}, bf16[512,512]{1,0:T(8,128)(2,1)}, f32[224...) custom-call(s32[2]{0:T(128)} %pad_add_fusion.at_ref, bf16[512,512]{1,0:T(8,128)(2,1)} %bitcast.15.refs_0_, ...), custom_call_target="tpu_custom_call" | custom-call | flops 2818572288 | bytes 14032896 | tf_op jit(solution)/shard_map/pallas_call | solution.py:230
  114.2 9.9 %collective-permute-done.16 = bf16[512,512]{1,0:T(8,128)(2,1)S(1)} collective-permute-done((bf16[512,512]{1,0:T(8,128)(2,1)}, bf16[512,512]{1,0:T(8,128)(2,1)S(1)}, u32[]{:S(2)}, u32[]{:S(2)}) %collective-permute-start.16) | collective-permute-done | bytes 524320 | tf_op jit(solution)/shard_map/ppermute | solution.py:44
  124.0 10.5 %collective-permute-done.17 = bf16[512,512]{1,0:T(8,128)(2,1)S(1)} collective-permute-done((bf16[512,512]{1,0:T(8,128)(2,1)}, bf16[512,512]{1,0:T(8,128)(2,1)S(1)}, u32[]{:S(2)}, u32[]{:S(2)}) %collective-permute-start.17) | collective-permute-done | bytes 524320 | tf_op jit(solution)/shard_map/ppermute | solution.py:44
  137.5 22.4 %all_to_all.20 = bf16[16,32,512]{2,1,0:T(8,128)(2,1)} all-to-all(bf16[16,32,512]{2,1,0:T(8,128)(2,1)S(1)} %bitcast.69), channel_id=1, replica_groups={{0,4,8,12,16,20,24,28,32,36,40,44,48,52,56,60},{64,68,72,76,80,84,88,92..., dimensions={0} | all-to-all | bytes 1048576 | tf_op jit(solution)/shard_map/all_to_all | solution.py:52
  159.9 4.2 %all-to-all-start.3 = ((bf16[16,128,512]{2,1,0:T(8,128)(2,1)}), bf16[16,128,512]{2,1,0:T(8,128)(2,1)S(1)}, u32[]{:S(2)}, u32[]{:S(2)}) async-start(bf16[16,128,512]{2,1,0:T(8,128)(2,1)} %get-tuple-element.26), calls=%async_computation.3 | async-start | bytes 4194304 | tf_op jit(solution)/shard_map/all_to_all | solution.py:52
  176.2 5.0 %collective-permute-done.12 = bf16[224,640]{1,0:T(8,128)(2,1)S(1)} collective-permute-done((bf16[224,640]{1,0:T(8,128)(2,1)S(1)}, bf16[224,640]{1,0:T(8,128)(2,1)S(1)}, u32[]{:S(2)}, u32[]{:S(2)}) %collective-permute-start.12) | collective-permute-done | bytes 286752 | tf_op jit(solution)/shard_map/ppermute | solution.py:48
  181.3 7.5 %collective-permute-done.14 = bf16[224,640]{1,0:T(8,128)(2,1)S(1)} collective-permute-done((bf16[224,640]{1,0:T(8,128)(2,1)S(1)}, bf16[224,640]{1,0:T(8,128)(2,1)S(1)}, u32[]{:S(2)}, u32[]{:S(2)}) %collective-permute-start.14) | collective-permute-done | bytes 286752 | tf_op jit(solution)/shard_map/ppermute | solution.py:48
  192.5 2.5 %gather_fusion = f32[512,512]{1,0:T(8,128)} fusion(f32[225,512]{1,0:T(8,128)S(1)} %pad_maximum_fusion.1, s32[1024]{0:T(1024)} %pad_clamp_fusion), kind=kCustom, calls=%fused_computation | custom fusion | bytes 2099200 | tf_op jit(solution)/shard_map/jit(_take)/gather | solution.py:386
  195.0 2.4 %add_convert_fusion.1 = bf16[512,512]{1,0:T(8,128)(2,1)} fusion(f32[512,512]{1,0:T(8,128)} %gather_fusion, bf16[512,512]{1,0:T(8,128)(2,1)} %param.6, pred[512]{0:T(512)(128)(4,1)S(1)} %copy-done.24), kind=kLoop, calls=%fused_computation.6 | loop fusion | flops 1048576 | bytes 2097664 | tf_op jit(solution)/shard_map/convert_element_type | solution.py:386
  197.5 15.8 %all-to-all-done.3 = bf16[16,128,512]{2,1,0:T(8,128)(2,1)S(1)} async-done(((bf16[16,128,512]{2,1,0:T(8,128)(2,1)}), bf16[16,128,512]{2,1,0:T(8,128)(2,1)S(1)}, u32[]{:S(2)}, u32[]{:S(2)}) %all-to-all-start.3) | async-done | bytes 2097184 | tf_op jit(solution)/shard_map/all_to_all | solution.py:52
  213.7 6.7 %collective-permute-start.19 = (bf16[2,32,512]{2,1,0:T(8,128)(2,1)S(1)}, bf16[2,32,512]{2,1,0:T(8,128)(2,1)S(1)}, u32[]{:S(2)}, u32[]{:S(2)}) collective-permute-start(bf16[2,32,512]{2,1,0:T(8,128)(2,1)S(1)} %get-tuple-element.37), channel_id=1, source_target_pairs={{0,64},{4,68},{8,72},{12,76},{16,80},{20,84},{24,88},{28,92},{32,9... | collective-permute-start | bytes 196616 | tf_op jit(solution)/shard_map/ppermute | solution.py:44
  220.4 3.2 %collective-permute-start.21 = (bf16[2,32,512]{2,1,0:T(8,128)(2,1)S(1)}, bf16[2,32,512]{2,1,0:T(8,128)(2,1)S(1)}, u32[]{:S(2)}, u32[]{:S(2)}) collective-permute-start(bf16[2,32,512]{2,1,0:T(8,128)(2,1)S(1)} %get-tuple-element.39), channel_id=1, source_target_pairs={{0,128},{4,132},{8,136},{12,140},{16,144},{20,148},{24,152},{28,15... | collective-permute-start | bytes 196616 | tf_op jit(solution)/shard_map/ppermute | solution.py:44
  (130 shorter events, 53.8 us)
Async XLA Ops:
  5.3 3.1 %collective-permute-start = (f32[3,512]{1,0:T(4,128)S(1)}, f32[3,512]{1,0:T(4,128)S(1)}, u32[]{:S(2)}, u32[]{:S(2)}) collective-permute-start(f32[3,512]{1,0:T(4,128)S(1)} %maximum_maximum_fusion), channel_id=1, source_target_pairs={{4,0},{8,4},{12,8},{16,12},{20,16},{24,20},{28,24},{32,28},{36,32}... | collective-permute-start | bytes 18440 | tf_op jit(solution)/shard_map/ppermute | solution.py:287
  11.1 15.7 %collective-permute-start.2 = (bf16[2,224,512]{2,1,0:T(8,128)(2,1)}, bf16[2,224,512]{2,1,0:T(8,128)(2,1)S(1)}, u32[]{:S(2)}, u32[]{:S(2)}) collective-permute-start(bf16[2,224,512]{2,1,0:T(8,128)(2,1)} %get-tuple-element.41), channel_id=1, source_target_pairs={{0,3},{1,0},{2,1},{3,2},{4,7},{5,4},{6,5},{7,6},{8,11},{9,8},{10,9... | collective-permute-start | bytes 1376264 | tf_op jit(solution)/shard_map/ppermute | solution.py:48
  13.3 20.9 %collective-permute-start.3 = (bf16[2,224,512]{2,1,0:T(8,128)(2,1)}, bf16[2,224,512]{2,1,0:T(8,128)(2,1)S(1)}, u32[]{:S(2)}, u32[]{:S(2)}) collective-permute-start(bf16[2,224,512]{2,1,0:T(8,128)(2,1)} %get-tuple-element.41), channel_id=1, source_target_pairs={{0,2},{1,3},{2,0},{3,1},{4,6},{5,7},{6,4},{7,5},{8,10},{9,11},{10,... | collective-permute-start | bytes 1376264 | tf_op jit(solution)/shard_map/ppermute | solution.py:48
  14.1 21.6 %collective-permute-start.1 = (bf16[2,224,512]{2,1,0:T(8,128)(2,1)}, bf16[2,224,512]{2,1,0:T(8,128)(2,1)S(1)}, u32[]{:S(2)}, u32[]{:S(2)}) collective-permute-start(bf16[2,224,512]{2,1,0:T(8,128)(2,1)} %get-tuple-element.41), channel_id=1, source_target_pairs={{0,1},{1,2},{2,3},{3,0},{4,5},{5,6},{6,7},{7,4},{8,9},{9,10},{10,1... | collective-permute-start | bytes 1376264 | tf_op jit(solution)/shard_map/ppermute | solution.py:48
  16.8 25.9 %all-to-all-start.1 = ((bf16[16,32,512]{2,1,0:T(8,128)(2,1)}), bf16[16,32,512]{2,1,0:T(8,128)(2,1)}, u32[]{:S(2)}, u32[]{:S(2)}) async-start(bf16[16,32,512]{2,1,0:T(8,128)(2,1)} %bitcast.18), calls=%async_computation.1 | async-start | bytes 1048576 | tf_op jit(solution)/shard_map/all_to_all | solution.py:52
  38.0 30.8 %collective-permute-start.4 = (bf16[4,2,224,512]{3,2,1,0:T(8,128)(2,1)S(1)}, bf16[4,2,224,512]{3,2,1,0:T(8,128)(2,1)}, u32[]{:S(2)}, u32[]{:S(2)}) collective-permute-start(bf16[4,2,224,512]{3,2,1,0:T(8,128)(2,1)S(1)} %pad_maximum_fusion.own_ref), channel_id=1, source_target_pairs={{0,4},{4,0},{8,12},{12,8},{16,20},{20,16},{24,28},{28,24},{32,36},... | collective-permute-start | bytes 5505032 | tf_op jit(solution)/shard_map/ppermute | solution.py:40
  43.6 21.4 %all-to-all-start = ((bf16[16,32,512]{2,1,0:T(8,128)(2,1)}), bf16[16,32,512]{2,1,0:T(8,128)(2,1)}, u32[]{:S(2)}, u32[]{:S(2)}) async-start(bf16[16,32,512]{2,1,0:T(8,128)(2,1)} %bitcast.71), calls=%async_computation | async-start | bytes 1048576 | tf_op jit(solution)/shard_map/all_to_all | solution.py:52
  49.0 17.6 %collective-permute-start.10 = (bf16[512,512]{1,0:T(8,128)(2,1)}, bf16[512,512]{1,0:T(8,128)(2,1)}, u32[]{:S(2)}, u32[]{:S(2)}) collective-permute-start(bf16[512,512]{1,0:T(8,128)(2,1)} %bitcast.19.refs_0_.refs_4_), channel_id=1, source_target_pairs={{0,128},{4,132},{8,136},{12,140},{16,144},{20,148},{24,152},{28,15... | collective-permute-start | bytes 1572872 | tf_op jit(solution)/shard_map/ppermute | solution.py:44
  52.3 24.1 %collective-permute-start.8 = (bf16[512,512]{1,0:T(8,128)(2,1)}, bf16[512,512]{1,0:T(8,128)(2,1)}, u32[]{:S(2)}, u32[]{:S(2)}) collective-permute-start(bf16[512,512]{1,0:T(8,128)(2,1)} %bitcast.19.refs_0_.refs_4_), channel_id=1, source_target_pairs={{0,64},{4,68},{8,72},{12,76},{16,80},{20,84},{24,88},{28,92},{32,9... | collective-permute-start | bytes 1572872 | tf_op jit(solution)/shard_map/ppermute | solution.py:44
  53.0 24.4 %collective-permute-start.9 = (bf16[512,512]{1,0:T(8,128)(2,1)}, bf16[512,512]{1,0:T(8,128)(2,1)}, u32[]{:S(2)}, u32[]{:S(2)}) collective-permute-start(bf16[512,512]{1,0:T(8,128)(2,1)} %bitcast.19.refs_0_.refs_4_), channel_id=1, source_target_pairs={{0,192},{4,196},{8,200},{12,204},{16,208},{20,212},{24,216},{28,22... | collective-permute-start | bytes 1572872 | tf_op jit(solution)/shard_map/ppermute | solution.py:44
  65.0 23.1 %collective-permute-start.5 = (bf16[512,512]{1,0:T(8,128)(2,1)}, bf16[512,512]{1,0:T(8,128)(2,1)}, u32[]{:S(2)}, u32[]{:S(2)}) collective-permute-start(bf16[512,512]{1,0:T(8,128)(2,1)} %bitcast.15.refs_0_), channel_id=1, source_target_pairs={{0,64},{4,68},{8,72},{12,76},{16,80},{20,84},{24,88},{28,92},{32,9... | collective-permute-start | bytes 1572872 | tf_op jit(solution)/shard_map/ppermute | solution.py:44
  66.6 22.0 %collective-permute-start.6 = (bf16[512,512]{1,0:T(8,128)(2,1)}, bf16[512,512]{1,0:T(8,128)(2,1)}, u32[]{:S(2)}, u32[]{:S(2)}) collective-permute-start(bf16[512,512]{1,0:T(8,128)(2,1)} %bitcast.15.refs_0_), channel_id=1, source_target_pairs={{0,192},{4,196},{8,200},{12,204},{16,208},{20,212},{24,216},{28,22... | collective-permute-start | bytes 1572872 | tf_op jit(solution)/shard_map/ppermute | solution.py:44
  68.8 30.1 %collective-permute-start.7 = (bf16[512,512]{1,0:T(8,128)(2,1)}, bf16[512,512]{1,0:T(8,128)(2,1)}, u32[]{:S(2)}, u32[]{:S(2)}) collective-permute-start(bf16[512,512]{1,0:T(8,128)(2,1)} %bitcast.15.refs_0_), channel_id=1, source_target_pairs={{0,128},{4,132},{8,136},{12,140},{16,144},{20,148},{24,152},{28,15... | collective-permute-start | bytes 1572872 | tf_op jit(solution)/shard_map/ppermute | solution.py:44
  108.9 15.2 %collective-permute-start.16 = (bf16[512,512]{1,0:T(8,128)(2,1)}, bf16[512,512]{1,0:T(8,128)(2,1)S(1)}, u32[]{:S(2)}, u32[]{:S(2)}) collective-permute-start(bf16[512,512]{1,0:T(8,128)(2,1)} %get-tuple-element.23), channel_id=1, source_target_pairs={{0,64},{4,68},{8,72},{12,76},{16,80},{20,84},{24,88},{28,92},{32,9... | collective-permute-start | bytes 1572872 | tf_op jit(solution)/shard_map/ppermute | solution.py:44
  110.5 24.0 %collective-permute-start.17 = (bf16[512,512]{1,0:T(8,128)(2,1)}, bf16[512,512]{1,0:T(8,128)(2,1)S(1)}, u32[]{:S(2)}, u32[]{:S(2)}) collective-permute-start(bf16[512,512]{1,0:T(8,128)(2,1)} %get-tuple-element.24), channel_id=1, source_target_pairs={{0,192},{4,196},{8,200},{12,204},{16,208},{20,212},{24,216},{28,22... | collective-permute-start | bytes 1572872 | tf_op jit(solution)/shard_map/ppermute | solution.py:44
  112.2 24.0 %collective-permute-start.18 = (bf16[512,512]{1,0:T(8,128)(2,1)}, bf16[512,512]{1,0:T(8,128)(2,1)S(1)}, u32[]{:S(2)}, u32[]{:S(2)}) collective-permute-start(bf16[512,512]{1,0:T(8,128)(2,1)} %get-tuple-element.25), channel_id=1, source_target_pairs={{0,128},{4,132},{8,136},{12,140},{16,144},{20,148},{24,152},{28,15... | collective-permute-start | bytes 1572872 | tf_op jit(solution)/shard_map/ppermute | solution.py:44
  159.9 53.4 %all-to-all-start.3 = ((bf16[16,128,512]{2,1,0:T(8,128)(2,1)}), bf16[16,128,512]{2,1,0:T(8,128)(2,1)S(1)}, u32[]{:S(2)}, u32[]{:S(2)}) async-start(bf16[16,128,512]{2,1,0:T(8,128)(2,1)} %get-tuple-element.26), calls=%async_computation.3 | async-start | bytes 4194304 | tf_op jit(solution)/shard_map/all_to_all | solution.py:52
  164.1 3.7 %collective-permute-start.11 = (bf16[224,2176]{1,0:T(8,128)(2,1)}, bf16[224,2176]{1,0:T(8,128)(2,1)}, u32[]{:S(2)}, u32[]{:S(2)}) collective-permute-start(bf16[224,2176]{1,0:T(8,128)(2,1)} %get-tuple-element.20), channel_id=1, source_target_pairs={{0,4},{4,0},{8,12},{12,8},{16,20},{20,16},{24,28},{28,24},{32,36},... | collective-permute-start | bytes 2924552 | tf_op jit(solution)/shard_map/ppermute | solution.py:40
  170.5 10.6 %collective-permute-start.12 = (bf16[224,640]{1,0:T(8,128)(2,1)S(1)}, bf16[224,640]{1,0:T(8,128)(2,1)S(1)}, u32[]{:S(2)}, u32[]{:S(2)}) collective-permute-start(bf16[224,640]{1,0:T(8,128)(2,1)S(1)} %get-tuple-element.42), channel_id=1, source_target_pairs={{0,1},{1,2},{2,3},{3,0},{4,5},{5,6},{6,7},{7,4},{8,9},{9,10},{10,1... | collective-permute-start | bytes 860168 | tf_op jit(solution)/shard_map/ppermute | solution.py:48
  172.2 9.0 %collective-permute-start.13 = (bf16[224,640]{1,0:T(8,128)(2,1)S(1)}, bf16[224,640]{1,0:T(8,128)(2,1)S(1)}, u32[]{:S(2)}, u32[]{:S(2)}) collective-permute-start(bf16[224,640]{1,0:T(8,128)(2,1)S(1)} %get-tuple-element.43), channel_id=1, source_target_pairs={{0,3},{1,0},{2,1},{3,2},{4,7},{5,4},{6,5},{7,6},{8,11},{9,8},{10,9... | collective-permute-start | bytes 860168 | tf_op jit(solution)/shard_map/ppermute | solution.py:48
  173.6 15.2 %collective-permute-start.14 = (bf16[224,640]{1,0:T(8,128)(2,1)S(1)}, bf16[224,640]{1,0:T(8,128)(2,1)S(1)}, u32[]{:S(2)}, u32[]{:S(2)}) collective-permute-start(bf16[224,640]{1,0:T(8,128)(2,1)S(1)} %get-tuple-element.44), channel_id=1, source_target_pairs={{0,2},{1,3},{2,0},{3,1},{4,6},{5,7},{6,4},{7,5},{8,10},{9,11},{10,... | collective-permute-start | bytes 860168 | tf_op jit(solution)/shard_map/ppermute | solution.py:48
  213.7 10.6 %collective-permute-start.19 = (bf16[2,32,512]{2,1,0:T(8,128)(2,1)S(1)}, bf16[2,32,512]{2,1,0:T(8,128)(2,1)S(1)}, u32[]{:S(2)}, u32[]{:S(2)}) collective-permute-start(bf16[2,32,512]{2,1,0:T(8,128)(2,1)S(1)} %get-tuple-element.37), channel_id=1, source_target_pairs={{0,64},{4,68},{8,72},{12,76},{16,80},{20,84},{24,88},{28,92},{32,9... | collective-permute-start | bytes 196616 | tf_op jit(solution)/shard_map/ppermute | solution.py:44
  220.4 4.3 %collective-permute-start.20 = (bf16[2,32,512]{2,1,0:T(8,128)(2,1)S(1)}, bf16[2,32,512]{2,1,0:T(8,128)(2,1)S(1)}, u32[]{:S(2)}, u32[]{:S(2)}) collective-permute-start(bf16[2,32,512]{2,1,0:T(8,128)(2,1)S(1)} %get-tuple-element.38), channel_id=1, source_target_pairs={{0,192},{4,196},{8,200},{12,204},{16,208},{20,212},{24,216},{28,22... | collective-permute-start | bytes 196616 | tf_op jit(solution)/shard_map/ppermute | solution.py:44
  220.4 5.8 %collective-permute-start.21 = (bf16[2,32,512]{2,1,0:T(8,128)(2,1)S(1)}, bf16[2,32,512]{2,1,0:T(8,128)(2,1)S(1)}, u32[]{:S(2)}, u32[]{:S(2)}) collective-permute-start(bf16[2,32,512]{2,1,0:T(8,128)(2,1)S(1)} %get-tuple-element.39), channel_id=1, source_target_pairs={{0,128},{4,132},{8,136},{12,140},{16,144},{20,148},{24,152},{28,15... | collective-permute-start | bytes 196616 | tf_op jit(solution)/shard_map/ppermute | solution.py:44
  (26 other events, 236.2 us)

commit v4 on v3

--- a/solution.py
+++ b/solution.py
@@ -170,20 +170,17 @@
 
 
 def grad_kernel(at_ref, *refs):
-    out_parts, in_parts, refs = refs[:4], refs[4:8], refs[8:]
-    normed_in, up_in, pre_in, rms_in = refs[:4]
-    in_outs, (own_out, sent_out, stat_ref), refs = refs[4:8], refs[8:11], refs[11:]
-    normed_ref, up_ref, pre_ref, rms_ref, w_out_ref, w_in_ref = refs[:6]
-    proj_ref, grad_ref, row_ref, in_ref, own_ref, sent_ref, sems = refs[6:]
+    parts, (normed_in, up_in, pre_in, rms_in), refs = refs[:4], refs[4:8], refs[8:]
+    in_outs, (grad_out, row_out), refs = refs[:4], refs[4:6], refs[6:]
+    normed_ref, up_ref, pre_ref, rms_ref, w_out_ref = refs[:5]
+    proj_ref, grad_ref, row_ref, in_ref, sems = refs[5:]
     move = Copies(sems)
-    first = move.start([(up_in, up_ref)] + weight_pairs(at_ref, out_parts, w_out_ref))
+    first = move.start([(up_in, up_ref)] + weight_pairs(at_ref, parts, w_out_ref))
     second = move.start([(pre_in, pre_ref), (rms_in, rms_ref)])
     third = move.start([(normed_in, normed_ref)])
-    fourth = move.start(weight_pairs(at_ref, in_parts, w_in_ref))
     wait(first)
     rows, width = normed_ref.shape
-    depth, hidden = w_in_ref.shape[1:]
-    half = rows // 2
+    depth, hidden = w_out_ref.shape[1:]
     for n in range(0, hidden, 256):
         weight = w_out_ref[:, :, n : n + 256].reshape(width, 256)
         proj_ref[:, n : n + 256] = jnp.dot(up_ref[...], weight, preferred_element_type=f32)
@@ -200,7 +197,7 @@
 
     lax.fori_loop(0, rows // CHUNK, grad_rows, 0)
     wait(third)
-    gone = []
+    gone = move.start([(grad_ref, grad_out), (row_ref, row_out)])
     for n, step in enumerate(STEPS):
         y = lax.rem(at_ref[1] + step, NY)
         block = normed_ref[:, pl.ds(pl.multiple_of(y * depth, depth), depth)]
@@ -208,7 +205,21 @@
             block, grad_ref[...], (((0,), (0,)), ((), ())), preferred_element_type=f32
         ).astype(bf16)
         gone += move.start([(in_ref.at[n], in_outs[n])])
-    wait(fourth)
+    wait(gone)
+
+
+def normed_kernel(at_ref, *refs):
+    parts, (grad_in, row_in, own_out, sent_out, stat_out), refs = refs[:4], refs[4:9], refs[9:]
+    grad_ref, row_ref, w_in_ref, own_ref, sent_ref, sems = refs
+    move = Copies(sems)
+    copies = move.start(
+        [(grad_in, grad_ref), (row_in, row_ref)] + weight_pairs(at_ref, parts, w_in_ref)
+    )
+    wait(copies)
+    half = grad_ref.shape[0] // 2
+    depth = w_in_ref.shape[1]
+    width = NY * depth
+    gone = move.start([(row_ref.at[pl.ds(0, half), :], stat_out)])
     for n in range(NY):
         part = lax.dot_general(
             grad_ref[...], w_in_ref[n], (((1,), (1,)), ((), ())), preferred_element_type=f32
@@ -220,11 +231,10 @@
     lane = lax.broadcasted_iota(jnp.int32, (half, 128), 1)
     low = jnp.where(lane == 1, stat - high, 0.0)
     sent_ref[:, width:] = jnp.where(lane == 0, high, low).astype(bf16)
-    stat_ref[...] = row_ref[:half, :]
     wait(gone + move.start([(own_ref, own_out), (sent_ref, sent_out)]))
 
 
-def call(kernel, at, far, outs, scratch, n_copies, flops, near=0):
+def call(kernel, at, far, outs, scratch, n_copies, flops):
     outs = [jax.ShapeDtypeStruct(shape, dtype) for shape, dtype in outs]
     moved = sum(v.size * v.dtype.itemsize for v in [*far, *outs])
     return pl.pallas_call(
@@ -232,8 +242,7 @@
         out_shape=tuple(outs),
         in_specs=[pl.BlockSpec(memory_space=pltpu.SMEM)]
         + [pl.BlockSpec(memory_space=pl.ANY)] * len(far),
-        out_specs=(pl.BlockSpec(memory_space=pltpu.HBM),) * (len(outs) - near)
-        + (pl.BlockSpec(memory_space=pltpu.VMEM),) * near,
+        out_specs=(pl.BlockSpec(memory_space=pltpu.HBM),) * len(outs),
         scratch_shapes=[pltpu.VMEM(shape, dtype) for shape, dtype in scratch]
         + [pltpu.SemaphoreType.DMA((n_copies,))],
         cost_estimate=pl.CostEstimate(flops=flops, bytes_accessed=moved, transcendentals=0),
@@ -280,10 +289,10 @@
     act_sums = jnp.dot(one_hot, byte_acts, preferred_element_type=f32)
     grad_sums = jnp.dot(one_hot, byte_grads, preferred_element_type=f32)
     byte_counts = jnp.sum(one_hot.astype(f32), axis=1)
-    own_count = jnp.max(jnp.where(leading, -1, local_row)) + 1
     frag = jnp.stack(
         [act_sums[CAP], grad_sums[CAP], jnp.broadcast_to(byte_counts[CAP], (quarter,))]
     )
+    own_count = jnp.max(jnp.where(leading, -1, local_row)) + 1
     frag = lax.ppermute(frag, "seq", [(s, s - 1) for s in range(1, SEQ)])
     last_mark = (jnp.arange(CAP, dtype=jnp.int32) == own_count - 1).astype(f32)
     act_total = act_sums[:CAP] + last_mark[:, None] * frag[0][None, :]
@@ -323,34 +332,30 @@
     out_rows = exchange(out_pieces, ZC_GROUPS)
     out_rows = jnp.sum(out_rows.astype(f32).reshape(NZ, NC, NY, 32, hidden), axis=0)
     grad_out = reduce_by_y(out_rows.swapaxes(0, 1), y_idx)
-    *in_pieces, own_part, sent, own_stat = call(
+    hidden_rows = ((rows_all, hidden), bf16)
+    *in_pieces, act_grad, row_stats = call(
         grad_kernel,
         at,
-        [*out_parts, *in_parts, normed, wide_up, pre_act, wide_rms],
-        [((depth, hidden), bf16)] * NY
-        + [((CAP, width), f32), ((CAP, width + 128), bf16), ((CAP, 128), f32)],
-        [
-            wide,
-            wide,
-            square,
-            thin,
-            weight,
-            weight,
-            square,
-            ((rows_all, hidden), bf16),
-            thin,
-            weight,
-            ((CAP, width), f32),
-            ((CAP, width + 128), bf16),
-        ],
-        18,
-        3 * product,
-        near=1,
+        [*out_parts, normed, wide_up, pre_act, wide_rms],
+        [((depth, hidden), bf16)] * NY + [hidden_rows, thin],
+        [wide, wide, square, thin, weight, square, hidden_rows, thin, weight],
+        14,
+        2 * product,
     )
     in_rows = reduce_sent(in_pieces[0], in_pieces[1:])
     in_rows = exchange(in_rows.astype(bf16).reshape(NZ * NC, 32, hidden), ZC_GROUPS)
     grad_in = jnp.sum(in_rows.astype(f32).reshape(NZ, NC, 32, hidden), axis=0)
 
+    own_shape, sent_shape = ((CAP, width), f32), ((CAP, width + 128), bf16)
+    own_part, sent, own_stat = call(
+        normed_kernel,
+        at,
+        [*in_parts, act_grad, row_stats],
+        [own_shape, sent_shape, ((CAP, 128), f32)],
+        [hidden_rows, thin, weight, own_shape, sent_shape],
+        9,
+        product,
+    )
     got = swap_cores(sent)
     got = got.astype(f32)
     chip_part = own_part + got[:, :width]

time: 230 us -> 228 us (level)
  waiting for transfers between devices: 92 us -> 86.7 us
  Pallas kernels: 21.7 us -> 24.3 us
    all_to_all x3, waiting for transfers between devices: 28.7 us -> 24.7 us  [exchange(): lax.all_to_all(value, 'seq', 0, 0, axis_index_groups=groups, tiled=True)]
    pallas_call x3 -> x4, Pallas kernels: 21.7 us -> 24.3 us  [call(): pl.pallas_call(kernel, out_shape=tuple(outs), in_specs=[pl.BlockSpec(memo...]
  transfers between devices with their start and end apart: 25 -> 25, of which waited for: 20 -> 15; matrix products, arithmetic and copies ran while one was open for 7% -> 7% of each run, Pallas kernels for 5% -> 8%
where the time goes in v4:
time: 228 us; the launch traced here: 225 us
  waiting for transfers between devices  86.7 us (38%)
  starting transfers between devices  62.3 us (27%)
  Pallas kernels  24.3 us (11%)
  blocking collectives  22.6 us (10%)
  other arithmetic  15.2 us (7%)
  local copies, waits for them, and re-layouts  9.08 us (4%)
  between operations  2.91 us (1%)
    ppermute x12, waiting for transfers between devices, send_y(): return lax.ppermute(value, 'seq', y_pairs(step))  38.9 us
    ppermute x12, starting transfers between devices, send_y(): return lax.ppermute(value, 'seq', y_pairs(step))  27.2 us
    all_to_all x3, waiting for transfers between devices, exchange(): lax.all_to_all(value, 'seq', 0, 0, axis_index_groups=groups, tiled=True)  24.7 us
    pallas_call x4, Pallas kernels, call(): pl.pallas_call(kernel, out_shape=tuple(outs), in_specs=[pl.BlockSpec(memo...  24.3 us
    all_to_all x1, blocking collectives, exchange(): lax.all_to_all(value, 'seq', 0, 0, axis_index_groups=groups, tiled=True)  22.6 us
    ppermute x6, waiting for transfers between devices, send_x(): return lax.ppermute(value, 'mp', [(i, (i + step) % NX) for i in range(NX)])  21.4 us
    all_to_all x3, starting transfers between devices, exchange(): lax.all_to_all(value, 'seq', 0, 0, axis_index_groups=groups, tiled=True)  19.6 us
    ppermute x6, starting transfers between devices, send_x(): return lax.ppermute(value, 'mp', [(i, (i + step) % NX) for i in range(NX)])  9.8 us
  transfers between devices with their start and end apart: 25, of which 15 were waited for; matrix products, arithmetic and copies ran while one was open for 7% of the time, Pallas kernels for 8%

profile of v4, /device:TPU:2, one launch (start us, length us, event | category | flops | bytes accessed | tf_op | source)
XLA Modules:
  0.0 224.7 jit_solution(10074514761407847100)
XLA Ops:
  16.9 9.9 %all-to-all-start = ((bf16[16,32,512]{2,1,0:T(8,128)(2,1)}), bf16[16,32,512]{2,1,0:T(8,128)(2,1)}, u32[]{:S(2)}, u32[]{:S(2)}) async-start(bf16[16,32,512]{2,1,0:T(8,128)(2,1)} %bitcast.14), calls=%async_computation | async-start | bytes 1048576 | tf_op jit(solution)/shard_map/all_to_all | solution.py:52
  26.8 7.4 %collective-permute-done.3 = bf16[2,224,512]{2,1,0:T(8,128)(2,1)S(1)} collective-permute-done((bf16[2,224,512]{2,1,0:T(8,128)(2,1)}, bf16[2,224,512]{2,1,0:T(8,128)(2,1)S(1)}, u32[]{:S(2)}, u32[]{:S(2)}) %collective-permute-start.3) | collective-permute-done | bytes 458784 | tf_op jit(solution)/shard_map/ppermute | solution.py:48
  39.4 3.4 %all-to-all-done = bf16[16,32,512]{2,1,0:T(8,128)(2,1)} async-done(((bf16[16,32,512]{2,1,0:T(8,128)(2,1)}), bf16[16,32,512]{2,1,0:T(8,128)(2,1)}, u32[]{:S(2)}, u32[]{:S(2)}) %all-to-all-start) | async-done | bytes 524320 | tf_op jit(solution)/shard_map/all_to_all | solution.py:52
  43.6 5.5 %all-to-all-start.1 = ((bf16[16,32,512]{2,1,0:T(8,128)(2,1)}), bf16[16,32,512]{2,1,0:T(8,128)(2,1)}, u32[]{:S(2)}, u32[]{:S(2)}) async-start(bf16[16,32,512]{2,1,0:T(8,128)(2,1)} %bitcast.71), calls=%async_computation.1 | async-start | bytes 1048576 | tf_op jit(solution)/shard_map/all_to_all | solution.py:52
  54.4 10.7 %all-to-all-done.1 = bf16[16,32,512]{2,1,0:T(8,128)(2,1)} async-done(((bf16[16,32,512]{2,1,0:T(8,128)(2,1)}), bf16[16,32,512]{2,1,0:T(8,128)(2,1)}, u32[]{:S(2)}, u32[]{:S(2)}) %all-to-all-start.1) | async-done | bytes 524320 | tf_op jit(solution)/shard_map/all_to_all | solution.py:52
  65.1 3.2 %collective-permute-start.10 = (bf16[512,512]{1,0:T(8,128)(2,1)}, bf16[512,512]{1,0:T(8,128)(2,1)}, u32[]{:S(2)}, u32[]{:S(2)}) collective-permute-start(bf16[512,512]{1,0:T(8,128)(2,1)} %bitcast.19.refs_0_), channel_id=1, source_target_pairs={{0,128},{4,132},{8,136},{12,140},{16,144},{20,148},{24,152},{28,15... | collective-permute-start | bytes 1572872 | tf_op jit(solution)/shard_map/ppermute | solution.py:44
  69.0 2.6 %collective-permute-start.9 = (bf16[512,512]{1,0:T(8,128)(2,1)}, bf16[512,512]{1,0:T(8,128)(2,1)}, u32[]{:S(2)}, u32[]{:S(2)}) collective-permute-start(bf16[512,512]{1,0:T(8,128)(2,1)} %bitcast.19.refs_0_), channel_id=1, source_target_pairs={{0,192},{4,196},{8,200},{12,204},{16,208},{20,212},{24,216},{28,22... | collective-permute-start | bytes 1572872 | tf_op jit(solution)/shard_map/ppermute | solution.py:44
  72.1 5.3 %shard_map.76 = (bf16[448,2048]{1,0:T(8,128)(2,1)}, bf16[448,2048]{1,0:T(8,128)(2,1)}, f32[448,128]{1,0:T(8,128)}) custom-call(s32[2]{0:T(128)} %pad_add_fusion.at_ref, bf16[4,2,224,512]{3,2,1,0:T(8,128)(2,1)} %copy-done.1, bf16[4,2,224,512]{3,2,1,0:T(8,128)(2,1)} %collective-permute-done.4.other_ref), custom_call_target="tpu_custom_call" | custom-call | bytes 7569408 | tf_op jit(solution)/shard_map/pallas_call | solution.py:240
  77.5 8.6 %collective-permute-done.6.refs_2_ = bf16[512,512]{1,0:T(8,128)(2,1)} collective-permute-done((bf16[512,512]{1,0:T(8,128)(2,1)}, bf16[512,512]{1,0:T(8,128)(2,1)}, u32[]{:S(2)}, u32[]{:S(2)}) %collective-permute-start.6) | collective-permute-done | bytes 524320 | tf_op jit(solution)/shard_map/ppermute | solution.py:44
  86.2 6.4 %shard_map.77 = (f32[448,512]{1,0:T(8,128)}, bf16[16,128,512]{2,1,0:T(8,128)(2,1)}) custom-call(s32[2]{0:T(128)} %pad_add_fusion.at_ref, bf16[512,512]{1,0:T(8,128)(2,1)} %bitcast.15.refs_0_, bf16[512,512]{1,0:T(8,128)(2,1)} %collective-permute-done.5.refs_1_, bf16[512,512]{1,0:T(8,128)(2,1)} %collective-permute-done.6.refs_2_, ...), custom_call_target="tpu_custom_call" | custom-call | flops 1879048192 | bytes 8781824 | tf_op jit(solution)/shard_map/pallas_call | solution.py:240
  92.6 7.2 %collective-permute-done.8.refs_1_ = bf16[512,512]{1,0:T(8,128)(2,1)} collective-permute-done((bf16[512,512]{1,0:T(8,128)(2,1)}, bf16[512,512]{1,0:T(8,128)(2,1)}, u32[]{:S(2)}, u32[]{:S(2)}) %collective-permute-start.8) | collective-permute-done | bytes 524320 | tf_op jit(solution)/shard_map/ppermute | solution.py:44
  99.8 7.3 %shard_map.78 = (bf16[512,512]{1,0:T(8,128)(2,1)}, bf16[512,512]{1,0:T(8,128)(2,1)}, bf16[512,512]{1,0:T(8,128)(2,1)}, bf16[512,512]{1,0:T(8,128)(2,1)}, bf16[448,512]{1,0:T(8,128)(2,1)}, /*index=5*/f32[448,128]{1,0:T(8,128)}) custom-call(s32[2]{0:T(128)} %pad_add_fusion.at_ref, bf16[512,512]{1,0:T(8,128)(2,1)} %bitcast.19.refs_0_, ...), custom_call_target="tpu_custom_call" | custom-call | flops 1879048192 | bytes 9699328 | tf_op jit(solution)/shard_map/pallas_call | solution.py:240
  110.4 2.3 %collective-permute-start.18 = (bf16[512,512]{1,0:T(8,128)(2,1)}, bf16[512,512]{1,0:T(8,128)(2,1)S(1)}, u32[]{:S(2)}, u32[]{:S(2)}) collective-permute-start(bf16[512,512]{1,0:T(8,128)(2,1)} %get-tuple-element.29), channel_id=1, source_target_pairs={{0,128},{4,132},{8,136},{12,140},{16,144},{20,148},{24,152},{28,15... | collective-permute-start | bytes 1572872 | tf_op jit(solution)/shard_map/ppermute | solution.py:44
  112.7 21.1 %collective-permute-done.16 = bf16[512,512]{1,0:T(8,128)(2,1)S(1)} collective-permute-done((bf16[512,512]{1,0:T(8,128)(2,1)}, bf16[512,512]{1,0:T(8,128)(2,1)S(1)}, u32[]{:S(2)}, u32[]{:S(2)}) %collective-permute-start.16) | collective-permute-done | bytes 524320 | tf_op jit(solution)/shard_map/ppermute | solution.py:44
  135.1 22.6 %all_to_all.20 = bf16[16,32,512]{2,1,0:T(8,128)(2,1)} all-to-all(bf16[16,32,512]{2,1,0:T(8,128)(2,1)S(1)} %bitcast.69), channel_id=1, replica_groups={{0,4,8,12,16,20,24,28,32,36,40,44,48,52,56,60},{64,68,72,76,80,84,88,92..., dimensions={0} | all-to-all | bytes 1048576 | tf_op jit(solution)/shard_map/all_to_all | solution.py:52
  157.7 4.2 %all-to-all-start.3 = ((bf16[16,128,512]{2,1,0:T(8,128)(2,1)}), bf16[16,128,512]{2,1,0:T(8,128)(2,1)S(1)}, u32[]{:S(2)}, u32[]{:S(2)}) async-start(bf16[16,128,512]{2,1,0:T(8,128)(2,1)} %get-tuple-element.30), calls=%async_computation.3 | async-start | bytes 4194304 | tf_op jit(solution)/shard_map/all_to_all | solution.py:52
  162.0 5.2 %shard_map.79 = (f32[224,2048]{1,0:T(8,128)}, bf16[224,2176]{1,0:T(8,128)(2,1)}, f32[224,128]{1,0:T(8,128)}) custom-call(s32[2]{0:T(128)} %pad_add_fusion.at_ref, bf16[512,512]{1,0:T(8,128)(2,1)} %bitcast.15.refs_0_, bf16[512,512]{1,0:T(8,128)(2,1)} %collective-permute-done.5.refs_1_, bf16[512,512]{1,0:T(8,128)(2,1)} %collective-permute-done.6.refs_2_, ...), custom_call_target="tpu_custom_call" | custom-call | flops 939524096 | bytes 5709824 | tf_op jit(solution)/shard_map/pallas_call | solution.py:240
  179.2 5.0 %collective-permute-done.12 = bf16[224,640]{1,0:T(8,128)(2,1)S(1)} collective-permute-done((bf16[224,640]{1,0:T(8,128)(2,1)S(1)}, bf16[224,640]{1,0:T(8,128)(2,1)S(1)}, u32[]{:S(2)}, u32[]{:S(2)}) %collective-permute-start.12) | collective-permute-done | bytes 286752 | tf_op jit(solution)/shard_map/ppermute | solution.py:48
  184.3 7.5 %collective-permute-done.14 = bf16[224,640]{1,0:T(8,128)(2,1)S(1)} collective-permute-done((bf16[224,640]{1,0:T(8,128)(2,1)S(1)}, bf16[224,640]{1,0:T(8,128)(2,1)S(1)}, u32[]{:S(2)}, u32[]{:S(2)}) %collective-permute-start.14) | collective-permute-done | bytes 286752 | tf_op jit(solution)/shard_map/ppermute | solution.py:48
  195.6 2.5 %gather_fusion = f32[512,512]{1,0:T(8,128)} fusion(f32[225,512]{1,0:T(8,128)S(1)} %pad_maximum_fusion.1, s32[1024]{0:T(1024)} %pad_clamp_fusion), kind=kCustom, calls=%fused_computation | custom fusion | bytes 2099200 | tf_op jit(solution)/shard_map/jit(_take)/gather | solution.py:391
  198.0 2.4 %add_convert_fusion.1 = bf16[512,512]{1,0:T(8,128)(2,1)} fusion(f32[512,512]{1,0:T(8,128)} %gather_fusion, bf16[512,512]{1,0:T(8,128)(2,1)} %param.6, pred[512]{0:T(512)(128)(4,1)S(1)} %copy-done.24), kind=kLoop, calls=%fused_computation.6 | loop fusion | flops 1048576 | bytes 2097664 | tf_op jit(solution)/shard_map/convert_element_type | solution.py:391
  200.5 10.6 %all-to-all-done.3 = bf16[16,128,512]{2,1,0:T(8,128)(2,1)S(1)} async-done(((bf16[16,128,512]{2,1,0:T(8,128)(2,1)}), bf16[16,128,512]{2,1,0:T(8,128)(2,1)S(1)}, u32[]{:S(2)}, u32[]{:S(2)}) %all-to-all-start.3) | async-done | bytes 2097184 | tf_op jit(solution)/shard_map/all_to_all | solution.py:52
  211.6 6.7 %collective-permute-start.19 = (bf16[2,32,512]{2,1,0:T(8,128)(2,1)S(1)}, bf16[2,32,512]{2,1,0:T(8,128)(2,1)S(1)}, u32[]{:S(2)}, u32[]{:S(2)}) collective-permute-start(bf16[2,32,512]{2,1,0:T(8,128)(2,1)S(1)} %get-tuple-element.41), channel_id=1, source_target_pairs={{0,64},{4,68},{8,72},{12,76},{16,80},{20,84},{24,88},{28,92},{32,9... | collective-permute-start | bytes 196616 | tf_op jit(solution)/shard_map/ppermute | solution.py:44
  218.2 3.1 %collective-permute-start.21 = (bf16[2,32,512]{2,1,0:T(8,128)(2,1)S(1)}, bf16[2,32,512]{2,1,0:T(8,128)(2,1)S(1)}, u32[]{:S(2)}, u32[]{:S(2)}) collective-permute-start(bf16[2,32,512]{2,1,0:T(8,128)(2,1)S(1)} %get-tuple-element.43), channel_id=1, source_target_pairs={{0,128},{4,132},{8,136},{12,140},{16,144},{20,148},{24,152},{28,15... | collective-permute-start | bytes 196616 | tf_op jit(solution)/shard_map/ppermute | solution.py:44
  (131 shorter events, 51.0 us)
Async XLA Ops:
  5.3 3.1 %collective-permute-start = (f32[3,512]{1,0:T(4,128)S(1)}, f32[3,512]{1,0:T(4,128)S(1)}, u32[]{:S(2)}, u32[]{:S(2)}) collective-permute-start(f32[3,512]{1,0:T(4,128)S(1)} %maximum_maximum_fusion), channel_id=1, source_target_pairs={{4,0},{8,4},{12,8},{16,12},{20,16},{24,20},{28,24},{32,28},{36,32}... | collective-permute-start | bytes 18440 | tf_op jit(solution)/shard_map/ppermute | solution.py:296
  11.1 15.7 %collective-permute-start.2 = (bf16[2,224,512]{2,1,0:T(8,128)(2,1)}, bf16[2,224,512]{2,1,0:T(8,128)(2,1)S(1)}, u32[]{:S(2)}, u32[]{:S(2)}) collective-permute-start(bf16[2,224,512]{2,1,0:T(8,128)(2,1)} %get-tuple-element.45), channel_id=1, source_target_pairs={{0,3},{1,0},{2,1},{3,2},{4,7},{5,4},{6,5},{7,6},{8,11},{9,8},{10,9... | collective-permute-start | bytes 1376264 | tf_op jit(solution)/shard_map/ppermute | solution.py:48
  13.4 20.9 %collective-permute-start.3 = (bf16[2,224,512]{2,1,0:T(8,128)(2,1)}, bf16[2,224,512]{2,1,0:T(8,128)(2,1)S(1)}, u32[]{:S(2)}, u32[]{:S(2)}) collective-permute-start(bf16[2,224,512]{2,1,0:T(8,128)(2,1)} %get-tuple-element.45), channel_id=1, source_target_pairs={{0,2},{1,3},{2,0},{3,1},{4,6},{5,7},{6,4},{7,5},{8,10},{9,11},{10,... | collective-permute-start | bytes 1376264 | tf_op jit(solution)/shard_map/ppermute | solution.py:48
  14.1 21.6 %collective-permute-start.1 = (bf16[2,224,512]{2,1,0:T(8,128)(2,1)}, bf16[2,224,512]{2,1,0:T(8,128)(2,1)S(1)}, u32[]{:S(2)}, u32[]{:S(2)}) collective-permute-start(bf16[2,224,512]{2,1,0:T(8,128)(2,1)} %get-tuple-element.45), channel_id=1, source_target_pairs={{0,1},{1,2},{2,3},{3,0},{4,5},{5,6},{6,7},{7,4},{8,9},{9,10},{10,1... | collective-permute-start | bytes 1376264 | tf_op jit(solution)/shard_map/ppermute | solution.py:48
  16.9 25.9 %all-to-all-start = ((bf16[16,32,512]{2,1,0:T(8,128)(2,1)}), bf16[16,32,512]{2,1,0:T(8,128)(2,1)}, u32[]{:S(2)}, u32[]{:S(2)}) async-start(bf16[16,32,512]{2,1,0:T(8,128)(2,1)} %bitcast.14), calls=%async_computation | async-start | bytes 1048576 | tf_op jit(solution)/shard_map/all_to_all | solution.py:52
  38.1 30.9 %collective-permute-start.4 = (bf16[4,2,224,512]{3,2,1,0:T(8,128)(2,1)S(1)}, bf16[4,2,224,512]{3,2,1,0:T(8,128)(2,1)}, u32[]{:S(2)}, u32[]{:S(2)}) collective-permute-start(bf16[4,2,224,512]{3,2,1,0:T(8,128)(2,1)S(1)} %pad_maximum_fusion.own_ref), channel_id=1, source_target_pairs={{0,4},{4,0},{8,12},{12,8},{16,20},{20,16},{24,28},{28,24},{32,36},... | collective-permute-start | bytes 5505032 | tf_op jit(solution)/shard_map/ppermute | solution.py:40
  43.6 21.5 %all-to-all-start.1 = ((bf16[16,32,512]{2,1,0:T(8,128)(2,1)}), bf16[16,32,512]{2,1,0:T(8,128)(2,1)}, u32[]{:S(2)}, u32[]{:S(2)}) async-start(bf16[16,32,512]{2,1,0:T(8,128)(2,1)} %bitcast.71), calls=%async_computation.1 | async-start | bytes 1048576 | tf_op jit(solution)/shard_map/all_to_all | solution.py:52
  49.1 19.2 %collective-permute-start.5 = (bf16[512,512]{1,0:T(8,128)(2,1)}, bf16[512,512]{1,0:T(8,128)(2,1)}, u32[]{:S(2)}, u32[]{:S(2)}) collective-permute-start(bf16[512,512]{1,0:T(8,128)(2,1)} %bitcast.15.refs_0_), channel_id=1, source_target_pairs={{0,64},{4,68},{8,72},{12,76},{16,80},{20,84},{24,88},{28,92},{32,9... | collective-permute-start | bytes 1572872 | tf_op jit(solution)/shard_map/ppermute | solution.py:44
  50.8 35.4 %collective-permute-start.6 = (bf16[512,512]{1,0:T(8,128)(2,1)}, bf16[512,512]{1,0:T(8,128)(2,1)}, u32[]{:S(2)}, u32[]{:S(2)}) collective-permute-start(bf16[512,512]{1,0:T(8,128)(2,1)} %bitcast.15.refs_0_), channel_id=1, source_target_pairs={{0,192},{4,196},{8,200},{12,204},{16,208},{20,212},{24,216},{28,22... | collective-permute-start | bytes 1572872 | tf_op jit(solution)/shard_map/ppermute | solution.py:44
  52.4 33.7 %collective-permute-start.7 = (bf16[512,512]{1,0:T(8,128)(2,1)}, bf16[512,512]{1,0:T(8,128)(2,1)}, u32[]{:S(2)}, u32[]{:S(2)}) collective-permute-start(bf16[512,512]{1,0:T(8,128)(2,1)} %bitcast.15.refs_0_), channel_id=1, source_target_pairs={{0,128},{4,132},{8,136},{12,140},{16,144},{20,148},{24,152},{28,15... | collective-permute-start | bytes 1572872 | tf_op jit(solution)/shard_map/ppermute | solution.py:44
  65.1 27.5 %collective-permute-start.10 = (bf16[512,512]{1,0:T(8,128)(2,1)}, bf16[512,512]{1,0:T(8,128)(2,1)}, u32[]{:S(2)}, u32[]{:S(2)}) collective-permute-start(bf16[512,512]{1,0:T(8,128)(2,1)} %bitcast.19.refs_0_), channel_id=1, source_target_pairs={{0,128},{4,132},{8,136},{12,140},{16,144},{20,148},{24,152},{28,15... | collective-permute-start | bytes 1572872 | tf_op jit(solution)/shard_map/ppermute | solution.py:44
  68.3 31.5 %collective-permute-start.8 = (bf16[512,512]{1,0:T(8,128)(2,1)}, bf16[512,512]{1,0:T(8,128)(2,1)}, u32[]{:S(2)}, u32[]{:S(2)}) collective-permute-start(bf16[512,512]{1,0:T(8,128)(2,1)} %bitcast.19.refs_0_), channel_id=1, source_target_pairs={{0,64},{4,68},{8,72},{12,76},{16,80},{20,84},{24,88},{28,92},{32,9... | collective-permute-start | bytes 1572872 | tf_op jit(solution)/shard_map/ppermute | solution.py:44
  69.0 30.8 %collective-permute-start.9 = (bf16[512,512]{1,0:T(8,128)(2,1)}, bf16[512,512]{1,0:T(8,128)(2,1)}, u32[]{:S(2)}, u32[]{:S(2)}) collective-permute-start(bf16[512,512]{1,0:T(8,128)(2,1)} %bitcast.19.refs_0_), channel_id=1, source_target_pairs={{0,192},{4,196},{8,200},{12,204},{16,208},{20,212},{24,216},{28,22... | collective-permute-start | bytes 1572872 | tf_op jit(solution)/shard_map/ppermute | solution.py:44
  107.1 26.7 %collective-permute-start.16 = (bf16[512,512]{1,0:T(8,128)(2,1)}, bf16[512,512]{1,0:T(8,128)(2,1)S(1)}, u32[]{:S(2)}, u32[]{:S(2)}) collective-permute-start(bf16[512,512]{1,0:T(8,128)(2,1)} %get-tuple-element.27), channel_id=1, source_target_pairs={{0,64},{4,68},{8,72},{12,76},{16,80},{20,84},{24,88},{28,92},{32,9... | collective-permute-start | bytes 1572872 | tf_op jit(solution)/shard_map/ppermute | solution.py:44
  108.6 25.2 %collective-permute-start.17 = (bf16[512,512]{1,0:T(8,128)(2,1)}, bf16[512,512]{1,0:T(8,128)(2,1)S(1)}, u32[]{:S(2)}, u32[]{:S(2)}) collective-permute-start(bf16[512,512]{1,0:T(8,128)(2,1)} %get-tuple-element.28), channel_id=1, source_target_pairs={{0,192},{4,196},{8,200},{12,204},{16,208},{20,212},{24,216},{28,22... | collective-permute-start | bytes 1572872 | tf_op jit(solution)/shard_map/ppermute | solution.py:44
  110.4 23.4 %collective-permute-start.18 = (bf16[512,512]{1,0:T(8,128)(2,1)}, bf16[512,512]{1,0:T(8,128)(2,1)S(1)}, u32[]{:S(2)}, u32[]{:S(2)}) collective-permute-start(bf16[512,512]{1,0:T(8,128)(2,1)} %get-tuple-element.29), channel_id=1, source_target_pairs={{0,128},{4,132},{8,136},{12,140},{16,144},{20,148},{24,152},{28,15... | collective-permute-start | bytes 1572872 | tf_op jit(solution)/shard_map/ppermute | solution.py:44
  157.7 53.4 %all-to-all-start.3 = ((bf16[16,128,512]{2,1,0:T(8,128)(2,1)}), bf16[16,128,512]{2,1,0:T(8,128)(2,1)S(1)}, u32[]{:S(2)}, u32[]{:S(2)}) async-start(bf16[16,128,512]{2,1,0:T(8,128)(2,1)} %get-tuple-element.30), calls=%async_computation.3 | async-start | bytes 4194304 | tf_op jit(solution)/shard_map/all_to_all | solution.py:52
  167.2 3.7 %collective-permute-start.11 = (bf16[224,2176]{1,0:T(8,128)(2,1)}, bf16[224,2176]{1,0:T(8,128)(2,1)}, u32[]{:S(2)}, u32[]{:S(2)}) collective-permute-start(bf16[224,2176]{1,0:T(8,128)(2,1)} %get-tuple-element.24), channel_id=1, source_target_pairs={{0,4},{4,0},{8,12},{12,8},{16,20},{20,16},{24,28},{28,24},{32,36},... | collective-permute-start | bytes 2924552 | tf_op jit(solution)/shard_map/ppermute | solution.py:40
  173.6 10.6 %collective-permute-start.12 = (bf16[224,640]{1,0:T(8,128)(2,1)S(1)}, bf16[224,640]{1,0:T(8,128)(2,1)S(1)}, u32[]{:S(2)}, u32[]{:S(2)}) collective-permute-start(bf16[224,640]{1,0:T(8,128)(2,1)S(1)} %get-tuple-element.46), channel_id=1, source_target_pairs={{0,1},{1,2},{2,3},{3,0},{4,5},{5,6},{6,7},{7,4},{8,9},{9,10},{10,1... | collective-permute-start | bytes 860168 | tf_op jit(solution)/shard_map/ppermute | solution.py:48
  175.3 9.0 %collective-permute-start.13 = (bf16[224,640]{1,0:T(8,128)(2,1)S(1)}, bf16[224,640]{1,0:T(8,128)(2,1)S(1)}, u32[]{:S(2)}, u32[]{:S(2)}) collective-permute-start(bf16[224,640]{1,0:T(8,128)(2,1)S(1)} %get-tuple-element.47), channel_id=1, source_target_pairs={{0,3},{1,0},{2,1},{3,2},{4,7},{5,4},{6,5},{7,6},{8,11},{9,8},{10,9... | collective-permute-start | bytes 860168 | tf_op jit(solution)/shard_map/ppermute | solution.py:48
  176.6 15.2 %collective-permute-start.14 = (bf16[224,640]{1,0:T(8,128)(2,1)S(1)}, bf16[224,640]{1,0:T(8,128)(2,1)S(1)}, u32[]{:S(2)}, u32[]{:S(2)}) collective-permute-start(bf16[224,640]{1,0:T(8,128)(2,1)S(1)} %get-tuple-element.48), channel_id=1, source_target_pairs={{0,2},{1,3},{2,0},{3,1},{4,6},{5,7},{6,4},{7,5},{8,10},{9,11},{10,... | collective-permute-start | bytes 860168 | tf_op jit(solution)/shard_map/ppermute | solution.py:48
  211.6 10.5 %collective-permute-start.19 = (bf16[2,32,512]{2,1,0:T(8,128)(2,1)S(1)}, bf16[2,32,512]{2,1,0:T(8,128)(2,1)S(1)}, u32[]{:S(2)}, u32[]{:S(2)}) collective-permute-start(bf16[2,32,512]{2,1,0:T(8,128)(2,1)S(1)} %get-tuple-element.41), channel_id=1, source_target_pairs={{0,64},{4,68},{8,72},{12,76},{16,80},{20,84},{24,88},{28,92},{32,9... | collective-permute-start | bytes 196616 | tf_op jit(solution)/shard_map/ppermute | solution.py:44
  218.2 4.3 %collective-permute-start.20 = (bf16[2,32,512]{2,1,0:T(8,128)(2,1)S(1)}, bf16[2,32,512]{2,1,0:T(8,128)(2,1)S(1)}, u32[]{:S(2)}, u32[]{:S(2)}) collective-permute-start(bf16[2,32,512]{2,1,0:T(8,128)(2,1)S(1)} %get-tuple-element.42), channel_id=1, source_target_pairs={{0,192},{4,196},{8,200},{12,204},{16,208},{20,212},{24,216},{28,22... | collective-permute-start | bytes 196616 | tf_op jit(solution)/shard_map/ppermute | solution.py:44
  218.2 5.8 %collective-permute-start.21 = (bf16[2,32,512]{2,1,0:T(8,128)(2,1)S(1)}, bf16[2,32,512]{2,1,0:T(8,128)(2,1)S(1)}, u32[]{:S(2)}, u32[]{:S(2)}) collective-permute-start(bf16[2,32,512]{2,1,0:T(8,128)(2,1)S(1)} %get-tuple-element.43), channel_id=1, source_target_pairs={{0,128},{4,132},{8,136},{12,140},{16,144},{20,148},{24,152},{28,15... | collective-permute-start | bytes 196616 | tf_op jit(solution)/shard_map/ppermute | solution.py:44
  (26 other events, 237.4 us)
